TPU v7x, 32 devices: a whole 2x2x4 slice. The times are simulated.
32 devices in a mesh: dp: 8 (over z, y), mp: 4 (over x, core).
Axes of the slice: x: 2, y: 2, z: 4, core: 2. Of those that a mesh axis runs over, the one named last changes fastest.
Arguments:
- tokens: bfloat16 [16384, 1024], P(('dp', 'mp')), may hold values from -6 to 6
- segment_ids: int32 [16384], P(('dp', 'mp')), may hold values from 0 to 63, never falling along the last dimension, each value on 1 to 512 neighbouring positions
- w_qkv: bfloat16 [3, 1024, 1024], P(None, None, 'mp'), may hold values from -0.1875 to 0.1875
- b_qv: bfloat16 [2, 1024], P(None, 'mp'), may hold values from -1.75 to 1.75
- w_out: bfloat16 [1024, 1024], P('mp'), may hold values from -2 to 2
- b_out: bfloat16 [1024], replicated, may hold values from -1.75 to 1.75
- w_up: bfloat16 [1024, 4096], P(None, 'mp'), may hold values from -0.1875 to 0.1875
- b_up: bfloat16 [4096], P('mp'), may hold values from -1.75 to 1.75
- w_down: bfloat16 [4096, 1024], P('mp'), may hold values from -0.125 to 0.125
- b_down: bfloat16 [1024], replicated, may hold values from -1.75 to 1.75
- ln_gain: float32 [2, 1024], replicated, may hold values from 0.5 to 1.5
- ln_bias: float32 [2, 1024], replicated, may hold values from -1.75 to 1.75
- out_grad: bfloat16 [16384, 1024], P(('dp', 'mp')), may hold values from -6 to 6
Outputs:
- block_out: bfloat16 [16384, 1024], P(('dp', 'mp'))
- grad_in: float32 [16384, 1024], P(('dp', 'mp'))
- grad_qkv: float32 [3, 1024, 1024], P(None, None, 'mp')
- grad_bqv: float32 [2, 1024], P(None, 'mp')
- grad_wout: float32 [1024, 1024], P('mp')
- grad_bout: float32 [1024], replicated
- grad_up: float32 [1024, 4096], P(None, 'mp')
- grad_bup: float32 [4096], P('mp')
- grad_down: float32 [4096, 1024], P('mp')
- grad_bdown: float32 [1024], replicated
- grad_gain: float32 [2, 1024], replicated
- grad_shift: float32 [2, 1024], replicated
Inputs may be any that keep to these rules, and one draw needn't show every extreme that they name: `segment_ids`: along all frames in order, segment numbers never fall; each segment covers 1 to 512 frames and one covers exactly 512; attention never crosses a row of 1024 frames.
All inputs are finite; a program needn't handle non-finite values.
Results may differ from a plain program's by a relative error of at most 0.02.
Values may be sent and summed in bfloat16 or wider, within the bound.
No kernel may reach another device: no remote copies, remote signals or barrier semaphores. Data moves between devices by JAX's collectives and lax.ppermute only.
A program may use at most 192 MiB of HBM per device.

v0:
```python
from functools import partial

import jax
import jax.numpy as jnp
from jax import lax
from jax.experimental import pallas as pl
from jax.experimental.pallas import tpu as pltpu
from jax.sharding import Mesh
from jax.sharding import PartitionSpec as P

HD = 64
LEN = 1024
QBLK = 512
EPS = 1e-05
BLK = 256

NEG = -1e30
GRANT = 10 << 20
EXTRA = 128
BRIEF = pl.CostEstimate(flops=1, bytes_accessed=1, transcendentals=0)
f32 = jnp.float32
bf16 = jnp.bfloat16


def nt(left, right):
    return lax.dot_general(left, right, (((1,), (1,)), ((), ())), preferred_element_type=f32)


def nn(left, right):
    return lax.dot_general(left, right, (((1,), (0,)), ((), ())), preferred_element_type=f32)


def tn(left, right):
    return lax.dot_general(left, right, (((0,), (0,)), ((), ())), preferred_element_type=f32)


def attn_bias(block, j, first):
    q_pos = block * BLK + lax.broadcasted_iota(jnp.int32, (1, BLK), 1)
    k_pos = j * BLK + lax.broadcasted_iota(jnp.int32, (BLK, BLK), 0)
    return jnp.where((k_pos >= first) & (k_pos <= q_pos), 0.0, NEG)


def head_rows(refs, scratch, heads):
    lane = lax.broadcasted_iota(jnp.int32, (LEN, 2 * HD), 1)
    for ref, out in zip(refs, scratch):
        for h in range(heads):
            pair = ref[:, (h // 2) * 2 * HD : (h // 2 + 1) * 2 * HD]
            out[h] = jnp.where((lane < HD) == (h % 2 == 0), pair, jnp.zeros_like(pair))


def attn_fwd_body(info, q_ref, k_ref, v_ref, st_ref, o_ref, lse_ref, k_heads, v_turned):
    block = pl.program_id(0)
    heads = q_ref.shape[1] // HD
    first = st_ref[...]

    @pl.when(block == 0)
    def _():
        head_rows([k_ref], [k_heads], heads)
        for pair in range(heads // 2):
            turned = v_ref[:, pair * 2 * HD : (pair + 1) * 2 * HD].T
            for h in (0, 1):
                v_turned[2 * pair + h, :HD] = turned[h * HD : (h + 1) * HD]
                v_turned[2 * pair + h, HD:] = jnp.ones((16, LEN), bf16)

    def step(at, carry):
        j = block - at
        row = pl.multiple_of((j ^ info[0]) * BLK, BLK)
        bias = attn_bias(block, j, first)
        out = []
        for h in range(heads):
            top, acc = carry[h]
            query = q_ref[:, (h // 2) * 2 * HD : (h // 2 + 1) * 2 * HD]
            s = nt(k_heads[h, pl.ds(row, BLK), :], query) + bias
            new = jnp.maximum(top, jnp.max(s, axis=0, keepdims=True))
            p = jnp.exp(s - new).astype(bf16)
            acc = acc * jnp.exp(top - new) + nn(v_turned[h, :, pl.ds(row, BLK)], p)
            out.append((new, acc))
        return tuple(out)

    init = tuple((jnp.full((1, BLK), NEG, f32), jnp.zeros((HD + 16, BLK), f32)) for _ in range(heads))
    done = lax.fori_loop(0, block + 1 - info[1 + block], step, init)
    for pair in range(heads // 2):
        both = [acc[:HD] / acc[HD : HD + 1] for _, acc in done[2 * pair : 2 * pair + 2]]
        o_ref[:, pair * 2 * HD : (pair + 1) * 2 * HD] = jnp.concatenate(both, axis=0).T.astype(bf16)
    for h in range(heads):
        top, acc = done[h]
        lse_ref[h : h + 1, :] = top + jnp.log(acc[HD : HD + 1])


def attn_bwd_body(base, info, q_ref, k_ref, v_ref, st_ref, o_ref, lse_ref, do_ref, d_ref, k_heads, v_heads, dk_acc, dv_acc):
    block = pl.program_id(0)
    heads = q_ref.shape[1] // HD
    first = st_ref[...]
    lane = lax.broadcasted_iota(jnp.int32, (BLK, 2 * HD), 1)

    @pl.when(block == 0)
    def _():
        head_rows([k_ref, v_ref], [k_heads, v_heads], heads)
        dk_acc[...] = jnp.zeros_like(dk_acc)
        dv_acc[...] = jnp.zeros_like(dv_acc)

    deltas = []
    for pair in range(heads // 2):
        cols = slice(pair * 2 * HD, (pair + 1) * 2 * HD)
        turned = (do_ref[:, cols].astype(f32) * o_ref[:, cols].astype(f32)).T
        for h in (0, 1):
            deltas.append(jnp.sum(turned[h * HD : (h + 1) * HD], axis=0, keepdims=True))

    def step(j, dqs):
        row = pl.multiple_of((j ^ info[0]) * BLK, BLK)
        bias = attn_bias(block, j, first)
        out = list(dqs)
        for pair in range(heads // 2):
            cols = slice(pair * 2 * HD, (pair + 1) * 2 * HD)
            query, cot = q_ref[:, cols], do_ref[:, cols]
            dk = dk_acc[pl.ds(row, BLK), cols]
            dv = dv_acc[pl.ds(row, BLK), cols]
            for h in (2 * pair, 2 * pair + 1):
                mask = (lane < HD) == (h % 2 == 0)
                keys = k_heads[h, pl.ds(row, BLK), :]
                p = jnp.exp(nt(keys, query) + (bias - lse_ref[base + h : base + h + 1, :]))
                dp = nt(v_heads[h, pl.ds(row, BLK), :], cot)
                ds = (p * (dp - deltas[h])).astype(bf16)
                dv = dv + nn(p.astype(bf16), jnp.where(mask, cot, jnp.zeros_like(cot)))
                dk = dk + nn(ds, jnp.where(mask, query, jnp.zeros_like(query)))
                out[pair] = out[pair] + tn(ds, keys)
            dk_acc[pl.ds(row, BLK), cols] = dk
            dv_acc[pl.ds(row, BLK), cols] = dv
        return tuple(out)

    init = tuple(jnp.zeros((BLK, 2 * HD), f32) for _ in range(heads // 2))
    dqs = lax.fori_loop(info[1 + block], block + 1, step, init)
    here = pl.multiple_of((block ^ info[0]) * BLK, BLK)
    for pair in range(heads // 2):
        cols = slice(pair * 2 * HD, (pair + 1) * 2 * HD)
        d_ref[0, pl.ds(here, BLK), cols] = (dqs[pair] * HD**-0.5).astype(bf16)

    @pl.when(block == pl.num_programs(0) - 1)
    def _():
        d_ref[1] = dk_acc[...].astype(bf16)
        d_ref[2] = dv_acc[...].astype(bf16)


def attn_specs(width):
    small = pl.BlockSpec((BLK, width), lambda i, info: (i ^ info[0], 0))
    whole = pl.BlockSpec((LEN, width), lambda i, info: (0, 0))
    start = pl.BlockSpec((1, BLK), lambda i, info: (0, i ^ info[0]))
    lse = pl.BlockSpec((width // HD, BLK), lambda i, info: (0, i ^ info[0]))
    return small, whole, start, lse


def attn_fwd(info, query, keys, values, start):
    width = query.shape[1]
    heads = width // HD
    small, whole, first, lse = attn_specs(width)
    return pl.pallas_call(
        attn_fwd_body,
        out_shape=(jax.ShapeDtypeStruct(query.shape, bf16), jax.ShapeDtypeStruct((heads, LEN), f32)),
        grid_spec=pltpu.PrefetchScalarGridSpec(
            num_scalar_prefetch=1,
            grid=(LEN // BLK,),
            in_specs=[small, whole, whole, first],
            out_specs=[small, lse],
            scratch_shapes=[pltpu.VMEM((heads, LEN, 2 * HD), bf16), pltpu.VMEM((heads, HD + 16, LEN), bf16)],
        ),
        cost_estimate=BRIEF,
        compiler_params=pltpu.CompilerParams(vmem_limit_bytes=GRANT),
        name="attn_fwd",
    )(info, query, keys, values, start)


def attn_bwd(info, query, keys, values, start, out, lse, cot, part=0, parts=1, prior=None):
    width = query.shape[1] // parts
    heads = width // HD
    small = pl.BlockSpec((BLK, width), lambda i, info: (i ^ info[0], part))
    whole = pl.BlockSpec((LEN, width), lambda i, info: (0, part))
    first = pl.BlockSpec((1, BLK), lambda i, info: (0, i ^ info[0]))
    lse_spec = pl.BlockSpec((heads * parts, BLK), lambda i, info: (0, i ^ info[0]))
    more = () if prior is None else (prior,)

    def body(*refs):
        attn_bwd_body(part * heads, *refs[:8], *refs[8 + len(more) :])

    return pl.pallas_call(
        body,
        out_shape=jax.ShapeDtypeStruct((3,) + query.shape, bf16),
        grid_spec=pltpu.PrefetchScalarGridSpec(
            num_scalar_prefetch=1,
            grid=(LEN // BLK,),
            in_specs=[small, whole, whole, first, small, lse_spec, small]
            + [pl.BlockSpec(memory_space=pl.ANY)] * len(more),
            out_specs=pl.BlockSpec((3, LEN, width), lambda i, info: (0, 0, part)),
            scratch_shapes=[
                pltpu.VMEM((heads, LEN, 2 * HD), bf16),
                pltpu.VMEM((heads, LEN, 2 * HD), bf16),
                pltpu.VMEM((LEN, width), f32),
                pltpu.VMEM((LEN, width), f32),
            ],
        ),
        input_output_aliases={8: 0} if more else {},
        cost_estimate=BRIEF,
        compiler_params=pltpu.CompilerParams(vmem_limit_bytes=GRANT),
        name="attn_bwd",
    )(info, query, keys, values, start, out, lse, cot, *more)


def up_body(a_ref, w_ref, b_ref, g_ref, s_ref):
    rows = a_ref[...]
    for part in range(w_ref.shape[1] // 256):
        cols = slice(part * 256, part * 256 + 256)
        u = nn(rows, w_ref[:, cols]) + b_ref[:, cols].astype(f32)
        size = jnp.abs(u)
        t = 1.0 / (1.0 + 0.3275911 * 0.7071067811865476 * size)
        poly = t * (0.5 * 0.254829592 + t * (0.5 * -0.284496736 + t * (0.5 * 1.421413741 + t * (0.5 * -1.453152027 + t * (0.5 * 1.061405429)))))
        bell = jnp.exp(-0.5 * u * u)
        tail = poly * bell
        cdf = jnp.where(u >= 0, 1.0 - tail, tail)
        g_ref[:, cols] = (u * cdf).astype(bf16)
        s_ref[:, cols] = (cdf + u * bell * 0.3989422804014327).astype(bf16)


def up_gelu(rows, weight, bias):
    m, k = rows.shape
    n = weight.shape[1]
    bm = 256
    shape = jax.ShapeDtypeStruct((m, n), bf16)
    tile = pl.BlockSpec((bm, n), lambda i: (i, 0))
    return pl.pallas_call(
        up_body,
        out_shape=(shape, shape),
        grid=(m // bm,),
        in_specs=[pl.BlockSpec((bm, k), lambda i: (i, 0)), pl.BlockSpec((k, n), lambda i: (0, 0)), pl.BlockSpec((1, n), lambda i: (0, 0))],
        out_specs=(tile, tile),
        cost_estimate=BRIEF,
        compiler_params=pltpu.CompilerParams(vmem_limit_bytes=GRANT),
        name="up_gelu",
    )(rows, weight, bias.reshape(1, n))


def const_spec(shape):
    return pl.BlockSpec(shape, lambda i: (0,) * len(shape))


def row_spec(rows, cols):
    return pl.BlockSpec((rows, cols), lambda i: (i, 0))


def project_body(a_ref, w_ref, b_ref, q_ref, k_ref, v_ref):
    rows = a_ref[...]
    q_ref[...] = (nn(rows, w_ref[0]) + b_ref[0:1].astype(f32)).astype(bf16) * jnp.bfloat16(HD**-0.5)
    k_ref[...] = nn(rows, w_ref[1]).astype(bf16)
    v_ref[...] = (nn(rows, w_ref[2]) + b_ref[1:2].astype(f32)).astype(bf16)


def project(rows, weight, bias):
    m, k = rows.shape
    n = weight.shape[2]
    tile = 256
    shape = jax.ShapeDtypeStruct((m, n), bf16)
    return pl.pallas_call(
        project_body,
        out_shape=(shape, shape, shape),
        grid=(m // tile,),
        in_specs=[row_spec(tile, k), const_spec(weight.shape), const_spec(bias.shape)],
        out_specs=[row_spec(tile, n)] * 3,
        cost_estimate=BRIEF,
        compiler_params=pltpu.CompilerParams(vmem_limit_bytes=GRANT),
        name="project",
    )(rows, weight, bias)


def sum_dots(product, lefts, rights):
    stacked = lefts[0].ndim == 3
    m, k = lefts[0].shape[-2:]
    n = rights[0].shape[-1] if product is nn else rights[0].shape[-2]
    terms = len(lefts)
    tile = 256
    steps = m // tile // 2

    def body(*refs):
        total = None
        for left, right in zip(refs[:terms], refs[terms : 2 * terms]):
            for at in range(left.shape[0] if stacked else 1):
                term = product(left[at], right[at]) if stacked else product(left[...], right[...])
                total = term if total is None else total + term
        here, there = refs[2 * terms :]

        @pl.when(pl.program_id(0) < steps)
        def _():
            there[...] = total.astype(bf16)

        @pl.when(pl.program_id(0) >= steps)
        def _():
            here[...] = total

    def turn(i):
        return jnp.where(i < steps, i + steps, i - steps)

    if stacked:
        left_spec = pl.BlockSpec((lefts[0].shape[0], tile, k), lambda i: (0, turn(i), 0))
    else:
        left_spec = pl.BlockSpec((tile, k), lambda i: (turn(i), 0))
    return pl.pallas_call(
        body,
        out_shape=(jax.ShapeDtypeStruct((m // 2, n), f32), jax.ShapeDtypeStruct((m // 2, n), bf16)),
        grid=(2 * steps,),
        in_specs=[left_spec] * terms + [const_spec(r.shape) for r in rights],
        out_specs=[
            pl.BlockSpec((tile, n), lambda i: (jnp.maximum(i - steps, 0), 0)),
            pl.BlockSpec((tile, n), lambda i: (jnp.minimum(i, steps - 1), 0)),
        ],
        cost_estimate=BRIEF,
        compiler_params=pltpu.CompilerParams(vmem_limit_bytes=GRANT),
        name="sum_dots",
    )(*lefts, *rights)


def center_rows(rows):
    center = rows - jnp.mean(rows, axis=-1, keepdims=True)
    scale = lax.rsqrt(jnp.mean(center * center, axis=-1, keepdims=True) + EPS)
    return center * scale, scale


def first_norm_body(x_ref, g_ref, gain_ref, shift_ref, a_ref, sum_ref):
    normal, _ = center_rows(x_ref[...].astype(f32))
    a_ref[...] = (normal * gain_ref[...] + shift_ref[...]).astype(bf16)

    @pl.when(pl.program_id(0) == 0)
    def _():
        sum_ref[...] = jnp.zeros_like(sum_ref)

    sum_ref[...] += jnp.sum(g_ref[...].astype(f32), axis=0, keepdims=True)


def first_norm(tokens, cotangent, gain, shift):
    m, d = tokens.shape
    tile = 128
    return pl.pallas_call(
        first_norm_body,
        out_shape=(jax.ShapeDtypeStruct((m, d), bf16), jax.ShapeDtypeStruct((1, d), f32)),
        grid=(m // tile,),
        in_specs=[row_spec(tile, d), row_spec(tile, d), const_spec((1, d)), const_spec((1, d))],
        out_specs=[row_spec(tile, d), const_spec((1, d))],
        cost_estimate=BRIEF,
        compiler_params=pltpu.CompilerParams(vmem_limit_bytes=GRANT),
        name="first_norm",
    )(tokens, cotangent, gain, shift)


def second_norm_body(x_ref, here_ref, came_ref, b_ref, gain_ref, shift_ref, h_ref, a_ref):
    mixed = x_ref[...].astype(f32) + (here_ref[...] + came_ref[...].astype(f32)) + b_ref[...].astype(f32)
    h_ref[...] = mixed
    normal, _ = center_rows(mixed)
    a_ref[...] = (normal * gain_ref[...] + shift_ref[...]).astype(bf16)


def second_norm(tokens, here, came, bias, gain, shift):
    m, d = tokens.shape
    tile = 128
    return pl.pallas_call(
        second_norm_body,
        out_shape=(jax.ShapeDtypeStruct((m, d), f32), jax.ShapeDtypeStruct((m, d), bf16)),
        grid=(m // tile,),
        in_specs=[row_spec(tile, d)] * 3 + [const_spec((1, d))] * 3,
        out_specs=[row_spec(tile, d)] * 2,
        cost_estimate=BRIEF,
        compiler_params=pltpu.CompilerParams(vmem_limit_bytes=GRANT),
        name="second_norm",
    )(tokens, here, came, bias, gain, shift)


def norm_back_body(v_ref, here_ref, low_came_ref, high_came_ref, gain_ref, res_ref, out_ref, low_ref, sums_ref):
    normal, scale = center_rows(v_ref[...].astype(f32))
    first = pl.program_id(0) < pl.num_programs(0) // 2
    came = jnp.where(first, low_came_ref[...], high_came_ref[...])
    grad = here_ref[...] + came.astype(f32)
    scaled = grad * gain_ref[...]
    inner = jnp.mean(scaled * normal, axis=-1, keepdims=True)
    back = scale * (scaled - jnp.mean(scaled, axis=-1, keepdims=True) - normal * inner)
    back = back + res_ref[...].astype(f32)
    low = back.astype(bf16)
    out_ref[...] = back
    low_ref[...] = low

    @pl.when(pl.program_id(0) == 0)
    def _():
        sums_ref[...] = jnp.zeros_like(sums_ref)

    sums_ref[0:1] += jnp.sum(grad * normal, axis=0, keepdims=True)
    sums_ref[1:2] += jnp.sum(grad, axis=0, keepdims=True)
    sums_ref[2:3] += jnp.sum(low.astype(f32), axis=0, keepdims=True)


def norm_back(values, here, came, gain, residual):
    m, d = values.shape
    tile = 128
    half = m // tile // 2
    low = pl.BlockSpec((tile, d), lambda i: (jnp.minimum(i, half - 1), 0))
    high = pl.BlockSpec((tile, d), lambda i: (jnp.maximum(i - half, 0), 0))
    return pl.pallas_call(
        norm_back_body,
        out_shape=(
            jax.ShapeDtypeStruct((m, d), f32),
            jax.ShapeDtypeStruct((m, d), bf16),
            jax.ShapeDtypeStruct((8, d), f32),
        ),
        grid=(m // tile,),
        in_specs=[row_spec(tile, d)] * 2 + [low, high, const_spec((1, d)), row_spec(tile, d)],
        out_specs=[row_spec(tile, d)] * 2 + [const_spec((8, d))],
        cost_estimate=BRIEF,
        compiler_params=pltpu.CompilerParams(vmem_limit_bytes=GRANT),
        name="norm_back",
    )(values, here, *came, gain, residual)


def back_act_body(z_ref, w_ref, s_ref, du_ref, sum_ref):
    du = (nt(z_ref[...], w_ref[...]) * s_ref[...].astype(f32)).astype(bf16)
    du_ref[...] = du

    @pl.when(pl.program_id(0) == 0)
    def _():
        sum_ref[...] = jnp.zeros_like(sum_ref)

    sum_ref[...] += jnp.sum(du.astype(f32), axis=0, keepdims=True)


def back_act(cotangent, weight, slope):
    m, d = cotangent.shape
    n = weight.shape[0]
    tile = 256
    return pl.pallas_call(
        back_act_body,
        out_shape=(jax.ShapeDtypeStruct((m, n), bf16), jax.ShapeDtypeStruct((1, n), f32)),
        grid=(m // tile,),
        in_specs=[row_spec(tile, d), const_spec((n, d)), row_spec(tile, n)],
        out_specs=[row_spec(tile, n), const_spec((1, n))],
        cost_estimate=BRIEF,
        compiler_params=pltpu.CompilerParams(vmem_limit_bytes=GRANT),
        name="back_act",
    )(cotangent, weight, slope)


def frame_sums_body(a_ref, d_ref, o_ref, g_ref, one_ref, two_ref, sums_ref, a_turned):
    rows, width = g_ref.shape[1], o_ref.shape[1]
    count = rows // width
    a_turned[...] = a_ref[...].T
    for at in range(4 * count):
        kind, part = divmod(at, count)
        out = one_ref if at < 2 * count else two_ref
        if kind < 3:
            block = nn(a_turned[part * width : (part + 1) * width, :], d_ref[kind])
        else:
            block = tn(o_ref[...], g_ref[:, part * width : (part + 1) * width])
        low = (at % (2 * count)) * width
        out[low : low + width, :] = block.astype(bf16)
    two_ref[2 * rows :, :] = jnp.zeros((EXTRA, width), bf16)
    for kind in range(3):
        sums_ref[kind] = jnp.sum(d_ref[kind].astype(f32), axis=0, keepdims=True)


def frame_sums(rows, trio, out, cotangent):
    t, d = rows.shape
    n = trio.shape[2]
    half = jax.ShapeDtypeStruct((2 * d, n), bf16)
    one, two, sums = pl.pallas_call(
        frame_sums_body,
        out_shape=(half, jax.ShapeDtypeStruct((2 * d + EXTRA, n), bf16), jax.ShapeDtypeStruct((3, 1, n), f32)),
        grid=(1,),
        in_specs=[const_spec((t, d)), const_spec((3, t, n)), const_spec((t, n)), const_spec((t, d))],
        out_specs=[const_spec((2 * d, n)), const_spec((2 * d + EXTRA, n)), const_spec((3, 1, n))],
        scratch_shapes=[pltpu.VMEM((d, t), bf16)],
        cost_estimate=BRIEF,
        compiler_params=pltpu.CompilerParams(vmem_limit_bytes=GRANT),
        name="frame_sums",
    )(rows, trio, out, cotangent)
    return (one, two), sums


def frames_body(a_ref, g_ref, out_ref, turned):
    tile = out_ref.shape[0]
    turned[...] = a_ref[...].T
    out_ref[...] = nn(turned[...], g_ref[...]).astype(bf16)


def across_frames(left, right):
    t, m = left.shape
    n = right.shape[1]
    tile = 256
    return pl.pallas_call(
        frames_body,
        out_shape=jax.ShapeDtypeStruct((m, n), bf16),
        grid=(m // tile,),
        in_specs=[pl.BlockSpec((t, tile), lambda i: (0, i)), const_spec((t, n))],
        out_specs=row_spec(tile, n),
        scratch_shapes=[pltpu.VMEM((tile, t), bf16)],
        cost_estimate=BRIEF,
        compiler_params=pltpu.CompilerParams(vmem_limit_bytes=GRANT),
        name="across_frames",
    )(left, right)


def turn_back_body(a_ref, w_ref, out_ref):
    out_ref[...] = nt(a_ref[...], w_ref[...]).astype(bf16)


def turn_back(rows, weight):
    m, k = rows.shape
    n = weight.shape[0]
    tile = 256
    return pl.pallas_call(
        turn_back_body,
        out_shape=jax.ShapeDtypeStruct((m, n), bf16),
        grid=(m // tile,),
        in_specs=[row_spec(tile, k), const_spec((n, k))],
        out_specs=row_spec(tile, n),
        cost_estimate=BRIEF,
        compiler_params=pltpu.CompilerParams(vmem_limit_bytes=GRANT),
        name="turn_back",
    )(rows, weight)


def side_sum_body(info, *refs):
    total = refs[0][0].astype(f32)
    for ref in refs[1:-1]:
        total = total + (ref[0] if len(ref.shape) == 3 else ref[...]).astype(f32)
    refs[-1][...] = total.astype(bf16)


def side_sum(side, own, got, near=None):
    _, rows, cols = own.shape
    tile = rows // 4
    pick_spec = pl.BlockSpec((1, tile, cols), lambda i, info: (info[0], i, 0))
    flat = pl.BlockSpec((tile, cols), lambda i, info: (i, 0))
    args = [own, got] + ([] if near is None else [near])
    return pl.pallas_call(
        side_sum_body,
        out_shape=jax.ShapeDtypeStruct((rows, cols), bf16),
        grid_spec=pltpu.PrefetchScalarGridSpec(
            num_scalar_prefetch=1,
            grid=(4,),
            in_specs=[pick_spec, pick_spec] + [flat] * (len(args) - 2),
            out_specs=flat,
        ),
        cost_estimate=BRIEF,
        compiler_params=pltpu.CompilerParams(vmem_limit_bytes=GRANT),
        name="side_sum",
    )(side[None], *args)


def add_low_body(a_ref, b_ref, out_ref):
    out_ref[...] = (a_ref[...].astype(f32) + b_ref[...].astype(f32)).astype(bf16)


def add_low(left, right):
    rows, cols = left.shape
    tile = rows // 2
    return pl.pallas_call(
        add_low_body,
        out_shape=jax.ShapeDtypeStruct((rows, cols), bf16),
        grid=(2,),
        in_specs=[row_spec(tile, cols)] * 2,
        out_specs=row_spec(tile, cols),
        cost_estimate=BRIEF,
        compiler_params=pltpu.CompilerParams(vmem_limit_bytes=GRANT),
        name="add_low",
    )(left, right)


def quarter_sums_body(info, own_ref, got_ref, near_ref, send_ref, keep_ref):
    total = own_ref[0, 0].astype(f32) + got_ref[0, 0].astype(f32) + near_ref[0].astype(f32)

    @pl.when(pl.program_id(0) == 0)
    def _():
        send_ref[...] = total.astype(bf16)

    @pl.when(pl.program_id(0) == 1)
    def _():
        keep_ref[...] = total.astype(bf16)


def quarter_sums(place, own, got, near):
    _, rows, cols = own.shape
    rows = rows // 2
    tile = rows // 2
    deep = pl.BlockSpec((1, 1, tile, cols), lambda f, i, info: (info[0], info[1] ^ 1 ^ f, i, 0))
    flat = pl.BlockSpec((1, tile, cols), lambda f, i, info: (info[1] ^ 1 ^ f, i, 0))
    shape = jax.ShapeDtypeStruct((rows, cols), bf16)
    return pl.pallas_call(
        quarter_sums_body,
        out_shape=(shape, shape),
        grid_spec=pltpu.PrefetchScalarGridSpec(
            num_scalar_prefetch=1,
            grid=(2, 2),
            in_specs=[deep, deep, flat],
            out_specs=[
                pl.BlockSpec((tile, cols), lambda f, i, info: (jnp.where(f == 0, i, 1), 0)),
                pl.BlockSpec((tile, cols), lambda f, i, info: (jnp.where(f == 0, 0, i), 0)),
            ],
        ),
        cost_estimate=BRIEF,
        compiler_params=pltpu.CompilerParams(vmem_limit_bytes=GRANT),
        name="quarter_sums",
    )(place, own.reshape(2, 2, rows, cols), got.reshape(2, 2, rows, cols), near.reshape(2, rows, cols))


def settle_body(info, mine_ref, other_ref, *rest):
    for at, ref in enumerate((mine_ref, other_ref)):

        @pl.when(pl.program_id(0) == at)
        def _(ref=ref):
            rest[-1][0] = ref[...].astype(f32)


def settle(place, mine, other, flip=0, prior=None, extra=0):
    rows, cols = mine.shape
    tile = rows // 2
    first = pl.BlockSpec((tile, cols), lambda f, i, info: (jnp.where(f == 0, i, 1), 0))
    second = pl.BlockSpec((tile, cols), lambda f, i, info: (jnp.where(f == 0, 0, i), 0))
    more = () if prior is None else (prior.reshape(-1, rows, cols),)
    out = pl.pallas_call(
        settle_body,
        out_shape=jax.ShapeDtypeStruct((4 + extra // rows, rows, cols), f32),
        grid_spec=pltpu.PrefetchScalarGridSpec(
            num_scalar_prefetch=1,
            grid=(2, 2),
            in_specs=[first, second] + [pl.BlockSpec(memory_space=pl.ANY)] * len(more),
            out_specs=pl.BlockSpec(
                (1, tile, cols), lambda f, i, info: (2 * (info[0] ^ f) + (info[1] ^ flip), i, 0)
            ),
        ),
        input_output_aliases={3: 0} if more else {},
        cost_estimate=BRIEF,
        compiler_params=pltpu.CompilerParams(vmem_limit_bytes=GRANT),
        name="settle",
    )(place, mine, other, *more)
    return out.reshape(-1, cols)


def finish_body(h_ref, here_ref, came_ref, b_ref, out_ref):
    out_ref[...] = (h_ref[...] + here_ref[...] + came_ref[...].astype(f32) + b_ref[...].astype(f32)).astype(bf16)


def finish(mixed, here, came, bias):
    m, d = mixed.shape
    tile = 128
    return pl.pallas_call(
        finish_body,
        out_shape=jax.ShapeDtypeStruct((m, d), bf16),
        grid=(m // tile,),
        in_specs=[row_spec(tile, d)] * 3 + [const_spec((1, d))],
        out_specs=row_spec(tile, d),
        cost_estimate=BRIEF,
        compiler_params=pltpu.CompilerParams(vmem_limit_bytes=GRANT),
        name="finish",
    )(mixed, here, came, bias)


def ride_body(vector_ref, whole_ref, out_ref):
    count, cols = vector_ref.shape
    rest = jnp.zeros((out_ref.shape[0] - count, cols), f32)
    out_ref[...] = jnp.concatenate([vector_ref[...], rest], axis=0).astype(bf16)


def ride(whole, vector):
    rows, cols = whole.shape
    vector = jnp.pad(vector.reshape(-1, cols), ((0, -(vector.size // cols) % 8), (0, 0)))
    return pl.pallas_call(
        ride_body,
        out_shape=jax.ShapeDtypeStruct((rows, cols), bf16),
        grid=(1,),
        in_specs=[const_spec(vector.shape), pl.BlockSpec(memory_space=pl.ANY)],
        out_specs=pl.BlockSpec((EXTRA, cols), lambda i: (rows // EXTRA - 1, 0)),
        input_output_aliases={1: 0},
        cost_estimate=BRIEF,
        compiler_params=pltpu.CompilerParams(vmem_limit_bytes=GRANT),
        name="ride",
    )(vector, whole)


def norm_rows(values, gain, shift):
    center = values - jnp.mean(values, axis=-1, keepdims=True)
    spread = jnp.mean(center * center, axis=-1, keepdims=True)
    return center * lax.rsqrt(spread + EPS) * gain + shift


def split_heads(flat, rows):
    return flat.reshape(rows, LEN, flat.shape[1] // HD, HD)


def block_scores(query, keys, seg_q, seg_k, offset):
    scores = jnp.einsum(
        "rqhd,rkhd->rhqk", query, keys, preferred_element_type=jnp.float32
    ) * HD ** (-0.5)
    q_pos = offset + jnp.arange(query.shape[1], dtype=jnp.int32)
    k_pos = jnp.arange(keys.shape[1], dtype=jnp.int32)
    allowed = (seg_q[:, :, None] == seg_k[:, None, :]) & (
        k_pos[None, None, :] <= q_pos[None, :, None]
    )
    return jnp.where(allowed[:, None], scores, -1e30)


def attention_forward(query, keys, values, seg_all):
    rows = query.shape[0] // LEN
    q4 = split_heads(query, rows)
    k4 = split_heads(keys, rows)
    v4 = split_heads(values, rows)
    seg2 = seg_all.reshape(rows, LEN)
    outputs = []
    totals = []
    for block in range(LEN // QBLK):
        first = block * QBLK
        end = first + QBLK
        scores = block_scores(
            q4[:, first:end], k4[:, :end], seg2[:, first:end], seg2[:, :end], first
        )
        top = jnp.max(scores, axis=-1, keepdims=True)
        expd = jnp.exp(scores - top)
        summed = jnp.sum(expd, axis=-1, keepdims=True)
        weights = (expd / summed).astype(jnp.bfloat16)
        outputs.append(
            jnp.einsum("rhqk,rkhd->rqhd", weights, v4[:, :end], preferred_element_type=jnp.float32)
        )
        totals.append(top + jnp.log(summed))
    attended = jnp.concatenate(outputs, axis=1).reshape(query.shape).astype(jnp.bfloat16)
    return (attended, totals)


def attention_backward(query, keys, values, seg_all, totals, grad_att):
    rows = query.shape[0] // LEN
    q4 = split_heads(query, rows)
    k4 = split_heads(keys, rows)
    v4 = split_heads(values, rows)
    g4 = split_heads(grad_att, rows)
    seg2 = seg_all.reshape(rows, LEN)
    scale = HD ** (-0.5)
    grad_k = jnp.zeros(k4.shape, jnp.float32)
    grad_v = jnp.zeros(v4.shape, jnp.float32)
    grad_q_parts = []
    for block in range(LEN // QBLK):
        first = block * QBLK
        end = first + QBLK
        scores = block_scores(
            q4[:, first:end], k4[:, :end], seg2[:, first:end], seg2[:, :end], first
        )
        probs = jnp.exp(scores - totals[block])
        weights = probs.astype(jnp.bfloat16)
        grad_w = jnp.einsum(
            "rqhd,rkhd->rhqk", g4[:, first:end], v4[:, :end], preferred_element_type=jnp.float32
        )
        delta = jnp.sum(probs * grad_w, axis=-1, keepdims=True)
        grad_s = (probs * (grad_w - delta)).astype(jnp.bfloat16)
        grad_q_parts.append(
            jnp.einsum("rhqk,rkhd->rqhd", grad_s, k4[:, :end], preferred_element_type=jnp.float32)
            * scale
        )
        padding = ((0, 0), (0, LEN - end), (0, 0), (0, 0))
        grad_k = grad_k + jnp.pad(
            jnp.einsum(
                "rhqk,rqhd->rkhd", grad_s, q4[:, first:end], preferred_element_type=jnp.float32
            )
            * scale,
            padding,
        )
        grad_v = grad_v + jnp.pad(
            jnp.einsum(
                "rhqk,rqhd->rkhd", weights, g4[:, first:end], preferred_element_type=jnp.float32
            ),
            padding,
        )
    shape = query.shape
    grad_q = jnp.concatenate(grad_q_parts, axis=1).reshape(shape).astype(jnp.bfloat16)
    return (
        grad_q,
        grad_k.reshape(shape).astype(jnp.bfloat16),
        grad_v.reshape(shape).astype(jnp.bfloat16),
    )


def tensor_parallel_shards(
    tokens,
    segment_ids,
    w_qkv,
    b_qv,
    w_out,
    b_out,
    w_up,
    b_up,
    w_down,
    b_down,
    ln_gain,
    ln_bias,
    out_grad,
):
    resid = tokens.astype(jnp.float32)
    qv_bias = b_qv.astype(jnp.float32)
    up_bias = b_up.astype(jnp.float32)
    local_rows = tokens.shape[0]
    normed, first_back = jax.vjp(norm_rows, resid, ln_gain[0], ln_bias[0])
    lowered = normed.astype(jnp.bfloat16)
    joined, seg_all = (
        lax.all_gather(lowered, "mp", axis=0, tiled=True),
        lax.all_gather(segment_ids, "mp", axis=0, tiled=True),
    )
    query = (jnp.dot(joined, w_qkv[0], preferred_element_type=jnp.float32) + qv_bias[0]).astype(
        jnp.bfloat16
    )
    keys = jnp.dot(joined, w_qkv[1], preferred_element_type=jnp.float32).astype(jnp.bfloat16)
    values = (jnp.dot(joined, w_qkv[2], preferred_element_type=jnp.float32) + qv_bias[1]).astype(
        jnp.bfloat16
    )
    query, keys, values = (query, keys, values)
    attended, totals = attention_forward(query, keys, values, seg_all)
    attn_sum = lax.psum_scatter(
        jnp.dot(attended, w_out, preferred_element_type=jnp.float32).astype(jnp.bfloat16),
        "mp",
        scatter_dimension=0,
        tiled=True,
    ).astype(jnp.float32)
    mixed = resid + attn_sum + b_out.astype(jnp.float32)
    normed2, second_back = jax.vjp(norm_rows, mixed, ln_gain[1], ln_bias[1])
    lowered2 = normed2.astype(jnp.bfloat16)
    joined2 = lax.all_gather(lowered2, "mp", axis=0, tiled=True)
    pre_act = jnp.dot(joined2, w_up, preferred_element_type=jnp.float32) + up_bias
    pre_act, activ = (pre_act, jax.nn.gelu(pre_act, approximate=False).astype(jnp.bfloat16))
    block_out = (
        mixed
        + lax.psum_scatter(
            jnp.dot(activ, w_down, preferred_element_type=jnp.float32).astype(jnp.bfloat16),
            "mp",
            scatter_dimension=0,
            tiled=True,
        ).astype(jnp.float32)
        + b_down.astype(jnp.float32)
    ).astype(jnp.bfloat16)
    grad_y = out_grad.astype(jnp.float32)
    grad_z = lax.all_gather(out_grad, "mp", axis=0, tiled=True)
    grad_down = jnp.einsum("tf,td->fd", activ, grad_z, preferred_element_type=jnp.float32)
    grad_bdown = jnp.sum(grad_z, axis=0, dtype=jnp.float32)
    grad_act = jnp.einsum("td,fd->tf", grad_z, w_down, preferred_element_type=jnp.float32)
    gelu_back = jax.vjp(lambda value: jax.nn.gelu(value, approximate=False), pre_act)[1]
    grad_pre = gelu_back(grad_act)[0].astype(jnp.bfloat16)
    grad_up = jnp.einsum("td,tf->df", joined2, grad_pre, preferred_element_type=jnp.float32)
    grad_bup = jnp.sum(grad_pre, axis=0, dtype=jnp.float32)
    grad_n2 = lax.psum_scatter(
        jnp.einsum("tf,df->td", grad_pre, w_up, preferred_element_type=jnp.float32).astype(
            jnp.bfloat16
        ),
        "mp",
        scatter_dimension=0,
        tiled=True,
    ).astype(jnp.float32)
    grad_h, grad_g2, grad_s2 = second_back(grad_n2)
    grad_h = grad_h + grad_y
    grad_branch = lax.all_gather(grad_h.astype(jnp.bfloat16), "mp", axis=0, tiled=True)
    grad_wout = jnp.einsum("tc,td->cd", attended, grad_branch, preferred_element_type=jnp.float32)
    grad_bout = jnp.sum(grad_branch, axis=0, dtype=jnp.float32)
    grad_att = jnp.einsum(
        "td,cd->tc", grad_branch, w_out, preferred_element_type=jnp.float32
    ).astype(jnp.bfloat16)
    grad_q, grad_k, grad_v = attention_backward(query, keys, values, seg_all, totals, grad_att)
    grad_qkv = jnp.stack(
        [
            jnp.einsum("td,tc->dc", joined, piece, preferred_element_type=jnp.float32)
            for piece in (grad_q, grad_k, grad_v)
        ]
    )
    grad_bqv = jnp.stack(
        [jnp.sum(grad_q, axis=0, dtype=jnp.float32), jnp.sum(grad_v, axis=0, dtype=jnp.float32)]
    )
    summed = jnp.zeros((local_rows * lax.axis_size("mp"), w_qkv.shape[1]), jnp.float32)
    for index, piece in enumerate((grad_q, grad_k, grad_v)):
        summed = summed + jnp.einsum(
            "tc,dc->td", piece, w_qkv[index], preferred_element_type=jnp.float32
        )
    grad_n1 = lax.psum_scatter(
        summed.astype(jnp.bfloat16), "mp", scatter_dimension=0, tiled=True
    ).astype(jnp.float32)
    grad_x, grad_g1, grad_s1 = first_back(grad_n1)
    grad_in = grad_x + grad_h
    weight_totals = (
        lax.psum(grad_qkv.astype(jnp.bfloat16), "dp").astype(jnp.float32),
        lax.psum(grad_bqv.astype(jnp.bfloat16), "dp").astype(jnp.float32),
        lax.psum(grad_wout.astype(jnp.bfloat16), "dp").astype(jnp.float32),
        lax.psum(grad_bout.astype(jnp.bfloat16), "dp").astype(jnp.float32),
        lax.psum(grad_up.astype(jnp.bfloat16), "dp").astype(jnp.float32),
        lax.psum(grad_bup.astype(jnp.bfloat16), "dp").astype(jnp.float32),
        lax.psum(grad_down.astype(jnp.bfloat16), "dp").astype(jnp.float32),
        lax.psum(grad_bdown.astype(jnp.bfloat16), "dp").astype(jnp.float32),
    )
    norm_totals = lax.psum(
        (jnp.stack([grad_g1, grad_g2]), jnp.stack([grad_s1, grad_s2])), ("dp", "mp")
    )
    return (block_out, grad_in) + tuple(weight_totals) + tuple(norm_totals)


def row_per_chip(mesh):
    return mesh.shape["mp"] == 4 and mesh.shape["dp"] == 8


def swap(value, axis):
    return lax.ppermute(value, axis, [(0, 1), (1, 0)])


def core(value):
    return swap(value, "core")


def cross(value):
    return swap(value, "x")


def after(value, *others):
    return lax.optimization_barrier((value,) + others)[0]


def take(value, at):
    return lax.dynamic_index_in_dim(value, at, 0, keepdims=False)


def place(whole, piece, at):
    return lax.dynamic_update_index_in_dim(whole, piece, at, 0)


def quarter_of(weight):
    me = lax.axis_index("y") + 2 * (lax.axis_index("z") & 1)
    return take(weight.reshape(4, -1, weight.shape[-1]), me)


def share(mine):
    out = [swap(mine, "y")]
    for bits in (2, 3):
        out.append(lax.ppermute(mine, ("z", "y"), [(i, i ^ bits) for i in range(8)]))
    return out


def assemble(mine, others):
    me = lax.axis_index("y") + 2 * (lax.axis_index("z") & 1)
    whole = place(jnp.zeros((4,) + mine.shape, mine.dtype), mine, me)
    for bits, piece in zip((1, 2, 3), others):
        whole = place(whole, piece, me ^ bits)
    return whole.reshape(-1, mine.shape[-1])


def swap_z(value, bits):
    return lax.ppermute(value, "z", [(i, i ^ bits) for i in range(4)])


def by_side(value):
    return value.reshape(2, value.shape[0] // 2, value.shape[1])


class Line:
    def __init__(self):
        self.last = None

    def __call__(self, function, *args):
        if self.last is not None:
            args, _ = lax.optimization_barrier((args, self.last))
        out = function(*args)
        self.last = jax.tree.leaves(out)[0]
        return out


def row_per_chip_shards(
    tokens,
    segment_ids,
    w_qkv,
    b_qv,
    w_out,
    b_out,
    w_up,
    b_up,
    w_down,
    b_down,
    ln_gain,
    ln_bias,
    out_grad,
):
    side, here_y = lax.axis_index("core"), lax.axis_index("y")
    place = jnp.stack([here_y, lax.axis_index("z") & 1]).astype(jnp.int32)
    width, wide = b_qv.shape[1], tokens.shape[1]
    gains, shifts = ln_gain[:, None], ln_bias[:, None]
    line = Line()

    def pair(*parts):
        return line(lambda *all: jnp.concatenate(all), *parts)

    qkv_mine = cross(line(quarter_of, w_qkv.reshape(-1, width)))
    a1_own, sum_dz = line(first_norm, tokens, out_grad, gains[0], shifts[0])
    a1_came = core(a1_own)
    seg_other = core(segment_ids)
    small = cross(jnp.concatenate([b_qv.reshape(-1), b_up]))
    up_quarter = line(quarter_of, w_up)
    down_quarter = line(quarter_of, w_down)

    def ranges(mine, other):
        seg = jnp.concatenate([mine, other])
        start = jnp.sum((seg[None, :] < seg[:, None]).astype(jnp.int32), axis=1)[None]
        ordered = jnp.where(side == 0, seg, jnp.concatenate([other, mine]))
        blocks = ordered.reshape(LEN // BLK, BLK)
        low = jnp.sum((blocks[None, :, -1] < blocks[:, None, 0]).astype(jnp.int32), axis=1)
        return start, jnp.concatenate([(side * (LEN // BLK // 2))[None].astype(jnp.int32), low])

    start, info = line(ranges, segment_ids, seg_other)
    a1 = pair(a1_own, a1_came)
    own = tuple(line(project, a1, w_qkv, b_qv))
    qkv_mine, w_out_now, up_quarter, _ = lax.optimization_barrier((qkv_mine, w_out, up_quarter, own[0]))
    qkv_parts = share(qkv_mine)
    out_other = cross(w_out_now)
    up_mine = cross(up_quarter)
    own = own + tuple(line(partial(attn_fwd, info), *own, start))
    up_mine, down_quarter, _ = lax.optimization_barrier((up_mine, down_quarter, own[3]))
    up_parts = share(up_mine)
    down_mine = cross(down_quarter)
    qkv_other = line(assemble, qkv_mine, qkv_parts).reshape(w_qkv.shape)
    other = tuple(line(project, a1, qkv_other, small[: 2 * width].reshape(2, width)))
    other = other + tuple(line(partial(attn_fwd, info), *other, start))
    down_mine, dz_own, _ = lax.optimization_barrier((down_mine, out_grad, other[3]))
    down_parts = share(down_mine)
    dz_came = core(dz_own)

    here, there = line(partial(sum_dots, nn), [own[3], other[3]], [w_out, out_other])
    came = core(there)
    up_other = line(assemble, up_mine, up_parts)
    mixed, a2_own = line(second_norm, tokens, here, came, b_out[None], gains[1], shifts[1])
    a2_came = core(a2_own)
    dz = pair(dz_own, dz_came)
    a2 = pair(a2_own, a2_came)

    def core_halves(value):
        half = value.shape[0] // 2
        return core(value[:half]), core(value[half:])

    act_other, slope_other = line(up_gelu, a2, up_other, small[2 * width :])
    down_got = cross(line(across_frames, act_other, dz))
    act_own, slope_own = line(up_gelu, a2, w_up, b_up)
    down_own = line(across_frames, act_own, dz)
    du_own, sum_up_own = line(back_act, dz, w_down, slope_own)
    down_other = line(assemble, down_mine, down_parts)
    du_other, sum_up_other = line(back_act, dz, down_other, slope_other)
    here, there = line(partial(sum_dots, nt), [du_own, du_other], [w_up, up_other])
    came = core_halves(there)
    up_got = cross(line(across_frames, a2, du_other))
    grad_h, dattn_own, sums_h = line(norm_back, mixed, here, came, gains[1], out_grad)
    dattn_came = core_halves(dattn_own)
    up_own = line(across_frames, a2, du_own)

    def spread_y(own, got):
        return swap(line(side_sum, 1 - here_y, own, got), "y")

    def near_z(own, got, near):
        send, keep = line(quarter_sums, place, own, got, near)
        return keep, swap_z(send, 1)

    def far_z(keep, came):
        low = line(add_low, keep, came)
        return low, swap_z(low, 2)

    def back_z(low, came):
        mine = line(add_low, low, came)
        near = swap_z(mine, 1)
        return (mine, swap(mine, "y")), (near, swap(near, "y"))

    def put(pair, prior=None, extra=0):
        fill = partial(settle, flip=0 if prior is None else 1, extra=extra)
        return line(lambda mine, other, prior: fill(place, mine, other, prior=prior), *pair, prior)

    down_own, down_got = by_side(down_own), by_side(down_got)
    down_near = spread_y(down_own, down_got)
    dattn = pair(dattn_own, *dattn_came)

    def back(entry, weight):
        query, keys, values, out, lse = entry
        cot = line(turn_back, dattn, weight)
        trio = line(partial(attn_bwd, info), query, keys, values, start, out, lse, cot)
        return (trio,) + tuple(line(frame_sums, a1, trio, out, dattn))

    trio_other, attn_other, sum_trio_other = back(other, out_other)
    first_got = cross(attn_other[0])
    down_sum = near_z(down_own, down_got, down_near)
    y_here, y_there = line(partial(sum_dots, nn), [act_own, act_other], [w_down, down_other])
    y_came = core(y_there)
    query, keys, values, out, lse = own
    cot = line(turn_back, dattn, w_out)
    down_sum = far_z(*down_sum)
    up_own, up_got = by_side(up_own), by_side(up_got)
    up_near = spread_y(up_own, up_got)
    trio_own = line(partial(attn_bwd, info), query, keys, values, start, out, lse, cot)
    attn_own, sum_trio_own = line(frame_sums, a1, trio_own, out, dattn)
    first_own, first_got = by_side(attn_own[0]), by_side(first_got)
    down_sum = back_z(*down_sum)
    block_out = line(finish, mixed, y_here, y_came, b_down[None])
    first_near = spread_y(first_own, first_got)
    here, there = line(partial(sum_dots, nt), [trio_own, trio_other], [w_qkv, qkv_other])
    came = core_halves(there)
    up_sum = near_z(up_own, up_got, up_near)
    down_sum = down_sum[0], (line(lambda value: value, down_sum[1][0]), down_sum[1][1])
    grad_in, _, sums_x = line(norm_back, tokens, here, came, gains[0], grad_h)
    common = line(
        lambda h, z, x: jnp.concatenate([h[2], z[0], x[0], h[0], x[1], h[1]]), sums_h, sum_dz, sums_x
    )
    common_came = core(common)

    first_sum = near_z(first_own, first_got, first_near)
    up_sum = far_z(*up_sum)
    vectors = line(
        lambda mine, came, *parts: [
            jnp.concatenate([trio[0, 0], trio[2, 0], up[0], mine + came]) for trio, up in parts
        ],
        common, common_came, (sum_trio_own, sum_up_own), (sum_trio_other, sum_up_other),
    )
    second_other = line(ride, attn_other[1], vectors[1])
    second_got = cross(second_other)
    second_own = line(ride, attn_own[1], vectors[0])
    first_sum = far_z(*first_sum)
    grad_down = put(down_sum[0])
    grad_down = put(down_sum[1], grad_down)
    up_sum = back_z(*up_sum)
    second_own, second_got = by_side(second_own), by_side(second_got)
    second_near = spread_y(second_own, second_got)
    first_sum = back_z(*first_sum)
    second_sum = near_z(second_own, second_got, second_near)
    grad_up = put(up_sum[0])
    second_sum = far_z(*second_sum)
    first = put(first_sum[0], extra=wide)
    second_sum = back_z(*second_sum)
    grad_up = put(up_sum[1], grad_up)
    first = put(first_sum[1], first, extra=wide)
    second = put(second_sum[0])
    second = put(second_sum[1], second)
    grad_qkv = lax.dynamic_update_slice(first, second[:wide], (2 * wide, 0)).reshape(w_qkv.shape)
    grad_wout = jnp.swapaxes(second[wide : 2 * wide].reshape(-1, w_out.shape[0], width), 0, 1)
    grad_wout = grad_wout.reshape(w_out.shape)
    vector = second[2 * wide :].reshape(-1)
    units = b_up.shape[0]
    ends = [2 * width, units, wide, wide, 2 * wide, 2 * wide]
    cuts = [sum(ends[:i]) for i in range(len(ends) + 1)]
    grad_bqv, grad_bup, grad_bout, grad_bdown, grad_gain, grad_shift = [
        vector[low:high] for low, high in zip(cuts[:-1], cuts[1:])
    ]
    return (
        block_out,
        grad_in,
        grad_qkv,
        grad_bqv.reshape(b_qv.shape),
        grad_wout,
        grad_bout,
        grad_up,
        grad_bup,
        grad_down,
        grad_bdown,
        grad_gain.reshape(ln_gain.shape),
        grad_shift.reshape(ln_bias.shape),
    )


def solution(mesh):
    rows, frames = ("dp", "mp"), "mp"
    body = tensor_parallel_shards
    if row_per_chip(mesh):
        shape = (mesh.shape["dp"] // 2, 2, mesh.shape["mp"] // 2, 2)
        mesh = Mesh(mesh.devices.reshape(shape), ("z", "y", "x", "core"))
        rows, frames = ("z", "y", "x", "core"), ("x", "core")
        body = row_per_chip_shards
    in_specs = (
        P(rows, None),
        P(rows),
        P(None, None, frames),
        P(None, frames),
        P(frames, None),
        P(),
        P(None, frames),
        P(frames),
        P(frames, None),
        P(),
        P(),
        P(),
        P(rows, None),
    )
    out_specs = (
        P(rows, None),
        P(rows, None),
        P(None, None, frames),
        P(None, frames),
        P(frames, None),
        P(),
        P(None, frames),
        P(frames),
        P(frames, None),
        P(),
        P(),
        P(),
    )
    return jax.shard_map(body, mesh=mesh, in_specs=in_specs, out_specs=out_specs, check_vma=False)
```

profile of v0, /device:TPU:0, one launch (start us, length us, event | category | flops | bytes accessed | tf_op | source)
XLA Modules:
  0.0 342.3 jit_solution(12001321068515073293)
XLA Ops:
  28.0 10.5 %attn_fwd.2 = (bf16[1024,256]{1,0:T(8,128)(2,1)S(1)}, f32[4,1024]{1,0:T(4,128)S(1)}) custom-call(s32[5]{0:T(128)S(1)} %pad_add_fusion.info.refs_0_, bf16[1024,256]{1,0:T(8,128)(2,1)S(1)} %get-tuple-element.424.q_ref.refs_1_, bf16[1024,256]{1,0:T(8,128)(2,1)S(1)} %get-tuple-element.425.k_ref.refs_2_, bf16[1024,256]{1,0:T(8,128)(2,1)S(1)} %copy-done.36, ...), custom_call_target="tpu_custom_call" | custom-call | flops 1 | bytes 1 | tf_op jit(solution)/shard_map/attn_fwd/pallas_call | solution.py:156
  38.6 3.4 %collective-permute-done.5 = bf16[768,256]{1,0:T(8,128)(2,1)} collective-permute-done((bf16[768,256]{1,0:T(8,128)(2,1)}, bf16[768,256]{1,0:T(8,128)(2,1)}, u32[]{:S(2)}, u32[]{:S(2)}) %collective-permute-start.5) | collective-permute-done | bytes 393248 | tf_op jit(solution)/shard_map/ppermute | solution.py:932
  53.9 10.5 %attn_fwd.3 = (bf16[1024,256]{1,0:T(8,128)(2,1)S(1)}, f32[4,1024]{1,0:T(4,128)S(1)}) custom-call(s32[5]{0:T(128)S(1)} %pad_add_fusion.info.refs_0_, bf16[1024,256]{1,0:T(8,128)(2,1)S(1)} %get-tuple-element.392.q_ref.refs_1_, bf16[1024,256]{1,0:T(8,128)(2,1)S(1)} %get-tuple-element.393.k_ref.refs_2_, bf16[1024,256]{1,0:T(8,128)(2,1)S(1)} %get-tuple-element.394.v_ref.refs_3_, ...), custom_call_target="tpu_custom_call" | custom-call | flops 1 | bytes 1 | tf_op jit(solution)/shard_map/attn_fwd/pallas_call | solution.py:156
  77.9 6.2 %up_gelu.2 = (bf16[1024,1024]{1,0:T(8,128)(2,1)S(1)}, bf16[1024,1024]{1,0:T(8,128)(2,1)S(1)}) custom-call(bf16[1024,1024]{1,0:T(8,128)(2,1)S(1)} %constant_dynamic-update-slice_fusion.5.a_ref, bf16[1024,1024]{1,0:T(8,128)(2,1)S(1)} %bitcast.114, bf16[1,1024]{1,0:T(2,128)(2,1)S(1)} %reshape.203.b_ref), custom_call_target="tpu_custom_call" | custom-call | flops 1 | bytes 1 | tf_op jit(solution)/shard_map/up_gelu/pallas_call | solution.py:228
  84.1 4.1 %across_frames.4 = bf16[1024,1024]{1,0:T(8,128)(2,1)} custom-call(bf16[1024,1024]{1,0:T(8,128)(2,1)S(1)} %get-tuple-element.410.a_ref.refs_1_, bf16[1024,1024]{1,0:T(8,128)(2,1)S(1)} %constant_dynamic-update-slice_fusion.3.g_ref.z_ref), custom_call_target="tpu_custom_call" | custom-call | flops 1 | bytes 1 | tf_op jit(solution)/shard_map/across_frames/pallas_call | solution.py:489
  89.8 6.2 %up_gelu.3 = (bf16[1024,1024]{1,0:T(8,128)(2,1)S(1)}, bf16[1024,1024]{1,0:T(8,128)(2,1)S(1)}) custom-call(bf16[1024,1024]{1,0:T(8,128)(2,1)S(1)} %constant_dynamic-update-slice_fusion.5.a_ref, bf16[1024,1024]{1,0:T(8,128)(2,1)S(1)} %copy-done.10, bf16[1,1024]{1,0:T(2,128)(2,1)S(1)} %reshape.204.b_ref), custom_call_target="tpu_custom_call" | custom-call | flops 1 | bytes 1 | tf_op jit(solution)/shard_map/up_gelu/pallas_call | solution.py:228
  96.0 3.3 across_frames.5
  100.6 3.3 back_act.2
  104.5 3.3 back_act.3
  107.9 5.4 %sum_dots.5 = (f32[512,1024]{1,0:T(8,128)S(1)}, bf16[512,1024]{1,0:T(8,128)(2,1)S(1)}) custom-call(bf16[1024,1024]{1,0:T(8,128)(2,1)S(1)} %get-tuple-element.381.refs_0_.g_ref, bf16[1024,1024]{1,0:T(8,128)(2,1)S(1)} %get-tuple-element.372.refs_1_.g_ref, bf16[1024,1024]{1,0:T(8,128)(2,1)S(1)} %copy-done.10, bf16[1024,1024]{1,0:T(8,128)(2,1)S(1)} %bitcast.115), custom_call_target="tpu_custom_call" | custom-call | flops 1 | bytes 1 | tf_op jit(solution)/shard_map/sum_dots/pallas_call | solution.py:303
  114.9 4.1 %across_frames.6 = bf16[1024,1024]{1,0:T(8,128)(2,1)} custom-call(bf16[1024,1024]{1,0:T(8,128)(2,1)S(1)} %constant_dynamic-update-slice_fusion.5.a_ref, bf16[1024,1024]{1,0:T(8,128)(2,1)S(1)} %get-tuple-element.372.refs_1_.g_ref), custom_call_target="tpu_custom_call" | custom-call | flops 1 | bytes 1 | tf_op jit(solution)/shard_map/across_frames/pallas_call | solution.py:489
  123.0 3.9 %norm_back.2 = (f32[512,1024]{1,0:T(8,128)S(1)}, bf16[512,1024]{1,0:T(8,128)(2,1)S(1)}, f32[8,1024]{1,0:T(8,128)S(1)}) custom-call(f32[512,1024]{1,0:T(8,128)S(1)} %copy-done.23, f32[512,1024]{1,0:T(8,128)S(1)} %copy-done.45, bf16[256,1024]{1,0:T(8,128)(2,1)} %collective-permute-done.20.low_came_ref, ...), custom_call_target="tpu_custom_call" | custom-call | flops 1 | bytes 1 | tf_op jit(solution)/shard_map/norm_back/pallas_call | solution.py:400
  127.0 3.3 across_frames.7
  130.2 6.8 %collective-permute-done.19 = bf16[1024,1024]{1,0:T(8,128)(2,1)} collective-permute-done((bf16[1024,1024]{1,0:T(8,128)(2,1)}, bf16[1024,1024]{1,0:T(8,128)(2,1)}, u32[]{:S(2)}, u32[]{:S(2)}) %collective-permute-start.19) | collective-permute-done | bytes 2097184 | tf_op jit(solution)/shard_map/ppermute | solution.py:901
  145.3 11.7 %attn_bwd.2.d_ref.refs_1_ = bf16[3,1024,256]{2,1,0:T(8,128)(2,1)S(1)} custom-call(s32[5]{0:T(128)S(1)} %pad_add_fusion.info.refs_0_, bf16[1024,256]{1,0:T(8,128)(2,1)S(1)} %copy-done.39, bf16[1024,256]{1,0:T(8,128)(2,1)S(1)} %copy-done.41, bf16[1024,256]{1,0:T(8,128)(2,1)S(1)} %copy-done.43, s32[1,1024]{1,0:T(1,128)S(1)} %bitcast.135, ...), custom_call_target="tpu_custom_call" | custom-call | flops 1 | bytes 1 | tf_op jit(solution)/shard_map/attn_bwd/pallas_call | solution.py:184
  161.8 3.3 quarter_sums.4
  167.0 5.3 %sum_dots.6 = (f32[512,1024]{1,0:T(8,128)S(1)}, bf16[512,1024]{1,0:T(8,128)(2,1)S(1)}) custom-call(bf16[1024,1024]{1,0:T(8,128)(2,1)S(1)} %copy-done.19, bf16[1024,1024]{1,0:T(8,128)(2,1)S(1)} %copy-done.17, bf16[1024,1024]{1,0:T(8,128)(2,1)S(1)} %copy-done.9, bf16[1024,1024]{1,0:T(8,128)(2,1)S(1)} %bitcast.113), custom_call_target="tpu_custom_call" | custom-call | flops 1 | bytes 1 | tf_op jit(solution)/shard_map/sum_dots/pallas_call | solution.py:303
  175.3 3.9 %collective-permute-done.26.b_ref = bf16[256,1024]{1,0:T(8,128)(2,1)S(1)} collective-permute-done((bf16[256,1024]{1,0:T(8,128)(2,1)S(1)}, bf16[256,1024]{1,0:T(8,128)(2,1)S(1)}, u32[]{:S(2)}, u32[]{:S(2)}) %collective-permute-start.26) | collective-permute-done | bytes 524320 | tf_op jit(solution)/shard_map/ppermute | solution.py:945
  186.2 11.7 %attn_bwd.3.d_ref.refs_0_ = bf16[3,1024,256]{2,1,0:T(8,128)(2,1)S(1)} custom-call(s32[5]{0:T(128)S(1)} %pad_add_fusion.info.refs_0_, bf16[1024,256]{1,0:T(8,128)(2,1)S(1)} %copy-done.32, bf16[1024,256]{1,0:T(8,128)(2,1)S(1)} %copy-done.34, bf16[1024,256]{1,0:T(8,128)(2,1)S(1)} %copy-done.37, s32[1,1024]{1,0:T(1,128)S(1)} %bitcast.136, ...), custom_call_target="tpu_custom_call" | custom-call | flops 1 | bytes 1 | tf_op jit(solution)/shard_map/attn_bwd/pallas_call | solution.py:184
  200.4 4.4 %collective-permute-done.27.b_ref = bf16[256,1024]{1,0:T(8,128)(2,1)S(1)} collective-permute-done((bf16[256,1024]{1,0:T(8,128)(2,1)S(1)}, bf16[256,1024]{1,0:T(8,128)(2,1)S(1)}, u32[]{:S(2)}, u32[]{:S(2)}) %collective-permute-start.27) | collective-permute-done | bytes 524320 | tf_op jit(solution)/shard_map/ppermute | solution.py:945
  208.9 4.6 %sum_dots.7 = (f32[512,1024]{1,0:T(8,128)S(1)}, bf16[512,1024]{1,0:T(8,128)(2,1)S(1)}) custom-call(bf16[3,1024,256]{2,1,0:T(8,128)(2,1)S(1)} %attn_bwd.3.d_ref.refs_0_, bf16[3,1024,256]{2,1,0:T(8,128)(2,1)S(1)} %attn_bwd.2.d_ref.refs_1_, bf16[3,1024,256]{2,1,0:T(8,128)(2,1)S(1)} %copy-done.26, bf16[3,1024,256]{2,1,0:T(8,128)(2,1)S(1)} %bitcast.117), custom_call_target="tpu_custom_call" | custom-call | flops 1 | bytes 1 | tf_op jit(solution)/shard_map/sum_dots/pallas_call | solution.py:303
  218.7 3.3 norm_back.3
  222.2 5.8 %collective-permute-done.34 = bf16[1024,256]{1,0:T(8,128)(2,1)S(1)} collective-permute-done((bf16[1024,256]{1,0:T(8,128)(2,1)S(1)}, bf16[1024,256]{1,0:T(8,128)(2,1)S(1)}, u32[]{:S(2)}, u32[]{:S(2)}) %collective-permute-start.34) | collective-permute-done | bytes 524320 | tf_op jit(solution)/shard_map/ppermute | solution.py:901
  239.4 15.4 %collective-permute-done.35.b_ref = bf16[512,256]{1,0:T(8,128)(2,1)S(1)} collective-permute-done((bf16[512,256]{1,0:T(8,128)(2,1)}, bf16[512,256]{1,0:T(8,128)(2,1)S(1)}, u32[]{:S(2)}, u32[]{:S(2)}) %collective-permute-start.35) | collective-permute-done | bytes 262176 | tf_op jit(solution)/shard_map/ppermute | solution.py:945
  256.0 4.2 %settle.8 = f32[4,256,1024]{2,1,0:T(8,128)} custom-call(s32[2]{0:T(128)S(1)} %pad_add_fusion.1.info, bf16[256,1024]{1,0:T(8,128)(2,1)S(1)} %copy-done.51, bf16[256,1024]{1,0:T(8,128)(2,1)} %collective-permute-done.42.other_ref), custom_call_target="tpu_custom_call" | custom-call | flops 1 | bytes 1 | tf_op jit(solution)/shard_map/settle/pallas_call | solution.py:620
  260.2 4.2 %settle.9 = f32[4,256,1024]{2,1,0:T(8,128)} custom-call(s32[2]{0:T(128)S(1)} %pad_add_fusion.1.info, bf16[256,1024]{1,0:T(8,128)(2,1)S(1)} %copy-done.56, bf16[256,1024]{1,0:T(8,128)(2,1)} %collective-permute-done.41.other_ref, f32[4,256,1024]{2,1,0:T(8,128)} %settle.8), custom_call_target="tpu_custom_call", output_to_operand_aliasing={{}: (3, {})} | custom-call | flops 1 | bytes 1 | tf_op jit(solution)/shard_map/settle/pallas_call | solution.py:620
  270.4 8.9 %collective-permute-done.38.b_ref = bf16[512,256]{1,0:T(8,128)(2,1)S(1)} collective-permute-done((bf16[512,256]{1,0:T(8,128)(2,1)S(1)}, bf16[512,256]{1,0:T(8,128)(2,1)S(1)}, u32[]{:S(2)}, u32[]{:S(2)}) %collective-permute-start.38) | collective-permute-done | bytes 262176 | tf_op jit(solution)/shard_map/ppermute | solution.py:945
  284.7 4.7 %collective-permute-done.48.other_ref = bf16[256,1024]{1,0:T(8,128)(2,1)S(1)} collective-permute-done((bf16[256,1024]{1,0:T(8,128)(2,1)S(1)}, bf16[256,1024]{1,0:T(8,128)(2,1)S(1)}, u32[]{:S(2)}, u32[]{:S(2)}) %collective-permute-start.48) | collective-permute-done | bytes 524320 | tf_op jit(solution)/shard_map/ppermute | solution.py:901
  295.8 5.1 %collective-permute-done.45.other_ref = bf16[512,256]{1,0:T(8,128)(2,1)S(1)} collective-permute-done((bf16[512,256]{1,0:T(8,128)(2,1)S(1)}, bf16[512,256]{1,0:T(8,128)(2,1)S(1)}, u32[]{:S(2)}, u32[]{:S(2)}) %collective-permute-start.45) | collective-permute-done | bytes 262176 | tf_op jit(solution)/shard_map/ppermute | solution.py:901
  303.2 5.2 %collective-permute-start.52 = (bf16[544,256]{1,0:T(8,128)(2,1)S(1)}, bf16[544,256]{1,0:T(8,128)(2,1)S(1)}, u32[]{:S(2)}, u32[]{:S(2)}) collective-permute-start(bf16[544,256]{1,0:T(8,128)(2,1)S(1)} %add_low.15.mine_ref), channel_id=1, source_target_pairs={{0,8},{8,0},{16,24},{24,16},{1,9},{9,1},{17,25},{25,17},{2,10},{10... | collective-permute-start | bytes 835592 | tf_op jit(solution)/shard_map/ppermute | solution.py:945
  316.8 6.4 %collective-permute-done.50.other_ref = bf16[256,1024]{1,0:T(8,128)(2,1)S(1)} collective-permute-done((bf16[256,1024]{1,0:T(8,128)(2,1)S(1)}, bf16[256,1024]{1,0:T(8,128)(2,1)S(1)}, u32[]{:S(2)}, u32[]{:S(2)}) %collective-permute-start.50) | collective-permute-done | bytes 524320 | tf_op jit(solution)/shard_map/ppermute | solution.py:901
  325.6 6.5 %collective-permute-done.44.other_ref = bf16[512,256]{1,0:T(8,128)(2,1)S(1)} collective-permute-done((bf16[512,256]{1,0:T(8,128)(2,1)S(1)}, bf16[512,256]{1,0:T(8,128)(2,1)S(1)}, u32[]{:S(2)}, u32[]{:S(2)}) %collective-permute-start.44) | collective-permute-done | bytes 262176 | tf_op jit(solution)/shard_map/ppermute | solution.py:901
  (337 shorter events, 151.1 us)
Async XLA Ops:
  10.3 16.3 %collective-permute-start.6 = (bf16[1536]{0:T(1024)(128)(2,1)S(1)}, bf16[1536]{0:T(1024)(128)(2,1)S(1)}, u32[]{:S(2)}, u32[]{:S(2)}) collective-permute-start(bf16[1536]{0:T(1024)(128)(2,1)S(1)} %pad_maximum_fusion.2), channel_id=1, source_target_pairs={{0,2},{2,0},{1,3},{3,1},{4,6},{6,4},{5,7},{7,5},{8,10},{10,8},{9,1... | collective-permute-start | bytes 9224 | tf_op jit(solution)/shard_map/ppermute | solution.py:901
  20.9 17.7 %collective-permute-start.3 = (bf16[768,256]{1,0:T(8,128)(2,1)}, bf16[768,256]{1,0:T(8,128)(2,1)}, u32[]{:S(2)}, u32[]{:S(2)}) collective-permute-start(bf16[768,256]{1,0:T(8,128)(2,1)} %collective-permute-done.2), channel_id=1, source_target_pairs={{0,4},{4,0},{1,5},{5,1},{2,6},{6,2},{3,7},{7,3},{8,12},{12,8},{9,1... | collective-permute-start | bytes 1179656 | tf_op jit(solution)/shard_map/ppermute | solution.py:901
  22.6 15.9 %collective-permute-start.4 = (bf16[768,256]{1,0:T(8,128)(2,1)}, bf16[768,256]{1,0:T(8,128)(2,1)}, u32[]{:S(2)}, u32[]{:S(2)}) collective-permute-start(bf16[768,256]{1,0:T(8,128)(2,1)} %collective-permute-done.2), channel_id=1, source_target_pairs={{0,8},{4,12},{8,0},{12,4},{16,24},{20,28},{24,16},{28,20},{1,9},{5... | collective-permute-start | bytes 1179656 | tf_op jit(solution)/shard_map/ppermute | solution.py:932
  24.2 17.8 %collective-permute-start.5 = (bf16[768,256]{1,0:T(8,128)(2,1)}, bf16[768,256]{1,0:T(8,128)(2,1)}, u32[]{:S(2)}, u32[]{:S(2)}) collective-permute-start(bf16[768,256]{1,0:T(8,128)(2,1)} %collective-permute-done.2), channel_id=1, source_target_pairs={{0,12},{4,8},{8,4},{12,0},{16,28},{20,24},{24,20},{28,16},{1,13},{... | collective-permute-start | bytes 1179656 | tf_op jit(solution)/shard_map/ppermute | solution.py:932
  24.7 19.5 %collective-permute-start.9 = (bf16[256,1024]{1,0:T(8,128)(2,1)}, bf16[256,1024]{1,0:T(8,128)(2,1)}, u32[]{:S(2)}, u32[]{:S(2)}) collective-permute-start(bf16[256,1024]{1,0:T(8,128)(2,1)} %dynamic-slice_bitcast_fusion.1), channel_id=1, source_target_pairs={{0,2},{2,0},{1,3},{3,1},{4,6},{6,4},{5,7},{7,5},{8,10},{10,8},{9,1... | collective-permute-start | bytes 1572872 | tf_op jit(solution)/shard_map/ppermute | solution.py:901
  26.6 37.8 %collective-permute-start.7 = (bf16[256,1024]{1,0:T(8,128)(2,1)}, bf16[256,1024]{1,0:T(8,128)(2,1)S(1)}, u32[]{:S(2)}, u32[]{:S(2)}) collective-permute-start(bf16[256,1024]{1,0:T(8,128)(2,1)} %w_ref.3), channel_id=1, source_target_pairs={{0,2},{2,0},{1,3},{3,1},{4,6},{6,4},{5,7},{7,5},{8,10},{10,8},{9,1... | collective-permute-start | bytes 1572872 | tf_op jit(solution)/shard_map/ppermute | solution.py:901
  44.2 23.0 %collective-permute-start.10 = (bf16[256,1024]{1,0:T(8,128)(2,1)}, bf16[256,1024]{1,0:T(8,128)(2,1)S(1)}, u32[]{:S(2)}, u32[]{:S(2)}) collective-permute-start(bf16[256,1024]{1,0:T(8,128)(2,1)} %collective-permute-done.9), channel_id=1, source_target_pairs={{0,4},{4,0},{1,5},{5,1},{2,6},{6,2},{3,7},{7,3},{8,12},{12,8},{9,1... | collective-permute-start | bytes 1572872 | tf_op jit(solution)/shard_map/ppermute | solution.py:901
  45.9 21.3 %collective-permute-start.11 = (bf16[256,1024]{1,0:T(8,128)(2,1)}, bf16[256,1024]{1,0:T(8,128)(2,1)S(1)}, u32[]{:S(2)}, u32[]{:S(2)}) collective-permute-start(bf16[256,1024]{1,0:T(8,128)(2,1)} %collective-permute-done.9), channel_id=1, source_target_pairs={{0,8},{4,12},{8,0},{12,4},{16,24},{20,28},{24,16},{28,20},{1,9},{5... | collective-permute-start | bytes 1572872 | tf_op jit(solution)/shard_map/ppermute | solution.py:932
  47.5 22.3 %collective-permute-start.12 = (bf16[256,1024]{1,0:T(8,128)(2,1)}, bf16[256,1024]{1,0:T(8,128)(2,1)S(1)}, u32[]{:S(2)}, u32[]{:S(2)}) collective-permute-start(bf16[256,1024]{1,0:T(8,128)(2,1)} %collective-permute-done.9), channel_id=1, source_target_pairs={{0,12},{4,8},{8,4},{12,0},{16,28},{20,24},{24,20},{28,16},{1,13},{... | collective-permute-start | bytes 1572872 | tf_op jit(solution)/shard_map/ppermute | solution.py:932
  47.8 18.9 %collective-permute-start.14 = (bf16[256,1024]{1,0:T(8,128)(2,1)S(1)}, bf16[256,1024]{1,0:T(8,128)(2,1)S(1)}, u32[]{:S(2)}, u32[]{:S(2)}) collective-permute-start(bf16[256,1024]{1,0:T(8,128)(2,1)S(1)} %copy-done.59), channel_id=1, source_target_pairs={{0,2},{2,0},{1,3},{3,1},{4,6},{6,4},{5,7},{7,5},{8,10},{10,8},{9,1... | collective-permute-start | bytes 1572872 | tf_op jit(solution)/shard_map/ppermute | solution.py:901
  74.0 30.0 %collective-permute-start.16 = (bf16[256,1024]{1,0:T(8,128)(2,1)S(1)}, bf16[256,1024]{1,0:T(8,128)(2,1)S(1)}, u32[]{:S(2)}, u32[]{:S(2)}) collective-permute-start(bf16[256,1024]{1,0:T(8,128)(2,1)S(1)} %collective-permute-done.14), channel_id=1, source_target_pairs={{0,4},{4,0},{1,5},{5,1},{2,6},{6,2},{3,7},{7,3},{8,12},{12,8},{9,1... | collective-permute-start | bytes 1572872 | tf_op jit(solution)/shard_map/ppermute | solution.py:901
  75.6 28.4 %collective-permute-start.17 = (bf16[256,1024]{1,0:T(8,128)(2,1)S(1)}, bf16[256,1024]{1,0:T(8,128)(2,1)S(1)}, u32[]{:S(2)}, u32[]{:S(2)}) collective-permute-start(bf16[256,1024]{1,0:T(8,128)(2,1)S(1)} %collective-permute-done.14), channel_id=1, source_target_pairs={{0,8},{4,12},{8,0},{12,4},{16,24},{20,28},{24,16},{28,20},{1,9},{5... | collective-permute-start | bytes 1572872 | tf_op jit(solution)/shard_map/ppermute | solution.py:932
  77.2 26.8 %collective-permute-start.18 = (bf16[256,1024]{1,0:T(8,128)(2,1)S(1)}, bf16[256,1024]{1,0:T(8,128)(2,1)S(1)}, u32[]{:S(2)}, u32[]{:S(2)}) collective-permute-start(bf16[256,1024]{1,0:T(8,128)(2,1)S(1)} %collective-permute-done.14), channel_id=1, source_target_pairs={{0,12},{4,8},{8,4},{12,0},{16,28},{20,24},{24,20},{28,16},{1,13},{... | collective-permute-start | bytes 1572872 | tf_op jit(solution)/shard_map/ppermute | solution.py:932
  88.2 48.8 %collective-permute-start.19 = (bf16[1024,1024]{1,0:T(8,128)(2,1)}, bf16[1024,1024]{1,0:T(8,128)(2,1)}, u32[]{:S(2)}, u32[]{:S(2)}) collective-permute-start(bf16[1024,1024]{1,0:T(8,128)(2,1)} %across_frames.4), channel_id=1, source_target_pairs={{0,2},{2,0},{1,3},{3,1},{4,6},{6,4},{5,7},{7,5},{8,10},{10,8},{9,1... | collective-permute-start | bytes 6291464 | tf_op jit(solution)/shard_map/ppermute | solution.py:901
  119.0 63.0 %collective-permute-start.28 = (bf16[1024,1024]{1,0:T(8,128)(2,1)}, bf16[1024,1024]{1,0:T(8,128)(2,1)}, u32[]{:S(2)}, u32[]{:S(2)}) collective-permute-start(bf16[1024,1024]{1,0:T(8,128)(2,1)} %across_frames.6), channel_id=1, source_target_pairs={{0,2},{2,0},{1,3},{3,1},{4,6},{6,4},{5,7},{7,5},{8,10},{10,8},{9,1... | collective-permute-start | bytes 6291464 | tf_op jit(solution)/shard_map/ppermute | solution.py:901
  139.2 22.5 %collective-permute-start.22 = (bf16[512,1024]{1,0:T(8,128)(2,1)S(1)}, bf16[512,1024]{1,0:T(8,128)(2,1)S(1)}, u32[]{:S(2)}, u32[]{:S(2)}) collective-permute-start(bf16[512,1024]{1,0:T(8,128)(2,1)S(1)} %side_sum.4), channel_id=1, source_target_pairs={{0,4},{4,0},{1,5},{5,1},{2,6},{6,2},{3,7},{7,3},{8,12},{12,8},{9,1... | collective-permute-start | bytes 3145736 | tf_op jit(solution)/shard_map/ppermute | solution.py:901
  172.3 33.4 %collective-permute-start.25 = (bf16[512,1024]{1,0:T(8,128)(2,1)S(1)}, bf16[512,1024]{1,0:T(8,128)(2,1)S(1)}, u32[]{:S(2)}, u32[]{:S(2)}) collective-permute-start(bf16[512,1024]{1,0:T(8,128)(2,1)S(1)} %get-tuple-element.414), channel_id=1, source_target_pairs={{0,1},{1,0},{2,3},{3,2},{4,5},{5,4},{6,7},{7,6},{8,9},{9,8},{10,11... | collective-permute-start | bytes 3145736 | tf_op jit(solution)/shard_map/ppermute | solution.py:901
  172.4 35.1 %collective-permute-start.29 = (bf16[2048,256]{1,0:T(8,128)(2,1)S(1)}, bf16[2048,256]{1,0:T(8,128)(2,1)S(1)}, u32[]{:S(2)}, u32[]{:S(2)}) collective-permute-start(bf16[2048,256]{1,0:T(8,128)(2,1)S(1)} %get-tuple-element.403), channel_id=1, source_target_pairs={{0,2},{2,0},{1,3},{3,1},{4,6},{6,4},{5,7},{7,5},{8,10},{10,8},{9,1... | collective-permute-start | bytes 3145736 | tf_op jit(solution)/shard_map/ppermute | solution.py:901
  179.4 25.5 %collective-permute-start.27 = (bf16[256,1024]{1,0:T(8,128)(2,1)S(1)}, bf16[256,1024]{1,0:T(8,128)(2,1)S(1)}, u32[]{:S(2)}, u32[]{:S(2)}) collective-permute-start(bf16[256,1024]{1,0:T(8,128)(2,1)S(1)} %add_low.8.a_ref), channel_id=1, source_target_pairs={{0,16},{8,24},{16,0},{24,8},{1,17},{9,25},{17,1},{25,9},{2,18},{10... | collective-permute-start | bytes 1572872 | tf_op jit(solution)/shard_map/ppermute | solution.py:945
  184.6 29.6 %collective-permute-start.33 = (bf16[512,1024]{1,0:T(8,128)(2,1)S(1)}, bf16[512,1024]{1,0:T(8,128)(2,1)S(1)}, u32[]{:S(2)}, u32[]{:S(2)}) collective-permute-start(bf16[512,1024]{1,0:T(8,128)(2,1)S(1)} %side_sum.5), channel_id=1, source_target_pairs={{0,4},{4,0},{1,5},{5,1},{2,6},{6,2},{3,7},{7,3},{8,12},{12,8},{9,1... | collective-permute-start | bytes 3145736 | tf_op jit(solution)/shard_map/ppermute | solution.py:901
  233.7 31.8 %collective-permute-start.39 = (bf16[2176,256]{1,0:T(8,128)(2,1)}, bf16[2176,256]{1,0:T(8,128)(2,1)S(1)}, u32[]{:S(2)}, u32[]{:S(2)}) collective-permute-start(bf16[2176,256]{1,0:T(8,128)(2,1)} %copy-done.54), channel_id=1, source_target_pairs={{0,2},{2,0},{1,3},{3,1},{4,6},{6,4},{5,7},{7,5},{8,10},{10,8},{9,1... | collective-permute-start | bytes 3342344 | tf_op jit(solution)/shard_map/ppermute | solution.py:901
  234.9 20.1 %collective-permute-start.42 = (bf16[256,1024]{1,0:T(8,128)(2,1)}, bf16[256,1024]{1,0:T(8,128)(2,1)}, u32[]{:S(2)}, u32[]{:S(2)}) collective-permute-start(bf16[256,1024]{1,0:T(8,128)(2,1)} %copy-done.50), channel_id=1, source_target_pairs={{0,4},{4,0},{1,5},{5,1},{2,6},{6,2},{3,7},{7,3},{8,12},{12,8},{9,1... | collective-permute-start | bytes 1572872 | tf_op jit(solution)/shard_map/ppermute | solution.py:901
  236.6 23.5 %collective-permute-start.41 = (bf16[256,1024]{1,0:T(8,128)(2,1)}, bf16[256,1024]{1,0:T(8,128)(2,1)}, u32[]{:S(2)}, u32[]{:S(2)}) collective-permute-start(bf16[256,1024]{1,0:T(8,128)(2,1)} %copy-done.55), channel_id=1, source_target_pairs={{0,4},{4,0},{1,5},{5,1},{2,6},{6,2},{3,7},{7,3},{8,12},{12,8},{9,1... | collective-permute-start | bytes 1572872 | tf_op jit(solution)/shard_map/ppermute | solution.py:901
  236.9 27.4 %collective-permute-start.40 = (bf16[256,1024]{1,0:T(8,128)(2,1)S(1)}, bf16[256,1024]{1,0:T(8,128)(2,1)}, u32[]{:S(2)}, u32[]{:S(2)}) collective-permute-start(bf16[256,1024]{1,0:T(8,128)(2,1)S(1)} %add_low.10.a_ref), channel_id=1, source_target_pairs={{0,16},{8,24},{16,0},{24,8},{1,17},{9,25},{17,1},{25,9},{2,18},{10... | collective-permute-start | bytes 1572872 | tf_op jit(solution)/shard_map/ppermute | solution.py:945
  239.1 15.8 %collective-permute-start.35 = (bf16[512,256]{1,0:T(8,128)(2,1)}, bf16[512,256]{1,0:T(8,128)(2,1)S(1)}, u32[]{:S(2)}, u32[]{:S(2)}) collective-permute-start(bf16[512,256]{1,0:T(8,128)(2,1)} %get-tuple-element.475), channel_id=1, source_target_pairs={{0,8},{8,0},{16,24},{24,16},{1,9},{9,1},{17,25},{25,17},{2,10},{10... | collective-permute-start | bytes 786440 | tf_op jit(solution)/shard_map/ppermute | solution.py:945
  265.7 15.6 %collective-permute-start.46 = (bf16[1088,256]{1,0:T(8,128)(2,1)S(1)}, bf16[1088,256]{1,0:T(8,128)(2,1)S(1)}, u32[]{:S(2)}, u32[]{:S(2)}) collective-permute-start(bf16[1088,256]{1,0:T(8,128)(2,1)S(1)} %side_sum.7), channel_id=1, source_target_pairs={{0,4},{4,0},{1,5},{5,1},{2,6},{6,2},{3,7},{7,3},{8,12},{12,8},{9,1... | collective-permute-start | bytes 1671176 | tf_op jit(solution)/shard_map/ppermute | solution.py:901
  269.8 19.6 %collective-permute-start.48 = (bf16[256,1024]{1,0:T(8,128)(2,1)S(1)}, bf16[256,1024]{1,0:T(8,128)(2,1)S(1)}, u32[]{:S(2)}, u32[]{:S(2)}) collective-permute-start(bf16[256,1024]{1,0:T(8,128)(2,1)S(1)} %add_low.12.mine_ref), channel_id=1, source_target_pairs={{0,4},{4,0},{1,5},{5,1},{2,6},{6,2},{3,7},{7,3},{8,12},{12,8},{9,1... | collective-permute-start | bytes 1572872 | tf_op jit(solution)/shard_map/ppermute | solution.py:901
  284.7 23.7 %collective-permute-start.49 = (bf16[256,1024]{1,0:T(8,128)(2,1)S(1)}, bf16[256,1024]{1,0:T(8,128)(2,1)S(1)}, u32[]{:S(2)}, u32[]{:S(2)}) collective-permute-start(bf16[256,1024]{1,0:T(8,128)(2,1)S(1)} %add_low.12.mine_ref), channel_id=1, source_target_pairs={{0,8},{8,0},{16,24},{24,16},{1,9},{9,1},{17,25},{25,17},{2,10},{10... | collective-permute-start | bytes 1572872 | tf_op jit(solution)/shard_map/ppermute | solution.py:945
  308.4 14.8 %collective-permute-start.50 = (bf16[256,1024]{1,0:T(8,128)(2,1)S(1)}, bf16[256,1024]{1,0:T(8,128)(2,1)S(1)}, u32[]{:S(2)}, u32[]{:S(2)}) collective-permute-start(bf16[256,1024]{1,0:T(8,128)(2,1)S(1)} %collective-permute-done.49.mine_ref), channel_id=1, source_target_pairs={{0,4},{4,0},{1,5},{5,1},{2,6},{6,2},{3,7},{7,3},{8,12},{12,8},{9,1... | collective-permute-start | bytes 1572872 | tf_op jit(solution)/shard_map/ppermute | solution.py:901
  309.5 24.7 %collective-permute-start.54 = (bf16[544,256]{1,0:T(8,128)(2,1)S(1)}, bf16[544,256]{1,0:T(8,128)(2,1)S(1)}, u32[]{:S(2)}, u32[]{:S(2)}) collective-permute-start(bf16[544,256]{1,0:T(8,128)(2,1)S(1)} %add_low.15.mine_ref), channel_id=1, source_target_pairs={{0,4},{4,0},{1,5},{5,1},{2,6},{6,2},{3,7},{7,3},{8,12},{12,8},{9,1... | collective-permute-start | bytes 835592 | tf_op jit(solution)/shard_map/ppermute | solution.py:901
  313.0 22.0 %collective-permute-start.53 = (bf16[544,256]{1,0:T(8,128)(2,1)S(1)}, bf16[544,256]{1,0:T(8,128)(2,1)S(1)}, u32[]{:S(2)}, u32[]{:S(2)}) collective-permute-start(bf16[544,256]{1,0:T(8,128)(2,1)S(1)} %collective-permute-done.52.mine_ref), channel_id=1, source_target_pairs={{0,4},{4,0},{1,5},{5,1},{2,6},{6,2},{3,7},{7,3},{8,12},{12,8},{9,1... | collective-permute-start | bytes 835592 | tf_op jit(solution)/shard_map/ppermute | solution.py:901
  315.8 16.3 %collective-permute-start.44 = (bf16[512,256]{1,0:T(8,128)(2,1)S(1)}, bf16[512,256]{1,0:T(8,128)(2,1)S(1)}, u32[]{:S(2)}, u32[]{:S(2)}) collective-permute-start(bf16[512,256]{1,0:T(8,128)(2,1)S(1)} %collective-permute-done.43.mine_ref), channel_id=1, source_target_pairs={{0,4},{4,0},{1,5},{5,1},{2,6},{6,2},{3,7},{7,3},{8,12},{12,8},{9,1... | collective-permute-start | bytes 786440 | tf_op jit(solution)/shard_map/ppermute | solution.py:901
  (87 other events, 613.4 us)
where the time goes:
time: 345 us; the launch traced here: 342 us
  Pallas kernels  155 us (45%)
  waiting for transfers between devices  85 us (25%)
  starting transfers between devices  59.5 us (17%)
  local copies, waits for them, and re-layouts  39.9 us (12%)
    ppermute x37, waiting for transfers between devices, swap(): return lax.ppermute(value, axis, [(0, 1), (1, 0)])  40.5 us
    ppermute x12, waiting for transfers between devices, swap_z(): return lax.ppermute(value, 'z', [(i, i ^ bits) for i in range(4)])  38.4 us
    ppermute x37, starting transfers between devices, swap(): return lax.ppermute(value, axis, [(0, 1), (1, 0)])  32.1 us
    pallas_call x2, Pallas kernels, attn_bwd(): pl.pallas_call(body, out_shape=jax.ShapeDtypeStruct((3,) + query.shape, b...  23.4 us
    ppermute x12, starting transfers between devices, swap_z(): return lax.ppermute(value, 'z', [(i, i ^ bits) for i in range(4)])  21.8 us
    pallas_call x2, Pallas kernels, attn_fwd(): pl.pallas_call(attn_fwd_body, out_shape=(jax.ShapeDtypeStruct(query.shape...  21 us
    unnamed x145, local copies, waits for them, and re-layouts  20.6 us
    pallas_call x8, Pallas kernels, settle(): pl.pallas_call(settle_body, out_shape=jax.ShapeDtypeStruct((4 + extra //...  18.9 us
  transfers between devices with their start and end apart: 55, of which 20 were waited for; matrix products, arithmetic and copies ran while one was open for 4% of the time, Pallas kernels for 45%

commit v1 on v0

--- a/solution.py
+++ b/solution.py
@@ -655,26 +655,55 @@
     )(mixed, here, came, bias)
 
 
-def ride_body(vector_ref, whole_ref, out_ref):
-    count, cols = vector_ref.shape
-    rest = jnp.zeros((out_ref.shape[0] - count, cols), f32)
-    out_ref[...] = jnp.concatenate([vector_ref[...], rest], axis=0).astype(bf16)
-
-
-def ride(whole, vector):
+def common_body(h_ref, z_ref, x_ref, out_ref):
+    out_ref[...] = jnp.zeros_like(out_ref)
+    rows = [h_ref[2:3], z_ref[0:1], x_ref[0:1], h_ref[0:1], x_ref[1:2], h_ref[1:2]]
+    for at, row in enumerate(rows):
+        out_ref[at : at + 1] = row
+
+
+def common_rows(sums_h, sum_dz, sums_x):
+    return pl.pallas_call(
+        common_body,
+        out_shape=jax.ShapeDtypeStruct(sums_h.shape, f32),
+        cost_estimate=BRIEF,
+        compiler_params=pltpu.CompilerParams(vmem_limit_bytes=GRANT),
+        name="common_rows",
+    )(sums_h, sum_dz, sums_x)
+
+
+def ride_body(trio_ref, up_ref, mine_ref, came_ref, whole_ref, out_ref, lines):
+    cols = out_ref.shape[1]
+    lines[...] = jnp.zeros_like(lines)
+    lines[0:1] = trio_ref[0]
+    lines[1:2] = trio_ref[2]
+    at = 2
+    for part in range(up_ref.shape[1] // cols):
+        lines[at : at + 1] = up_ref[:, part * cols : (part + 1) * cols]
+        at += 1
+    both = mine_ref[...] + came_ref[...]
+    for row in range(6):
+        for part in range(both.shape[1] // cols):
+            lines[at : at + 1] = both[row : row + 1, part * cols : (part + 1) * cols]
+            at += 1
+    out_ref[...] = lines[...].astype(bf16)
+
+
+def ride(whole, trio, up, mine, came):
     rows, cols = whole.shape
-    vector = jnp.pad(vector.reshape(-1, cols), ((0, -(vector.size // cols) % 8), (0, 0)))
     return pl.pallas_call(
         ride_body,
         out_shape=jax.ShapeDtypeStruct((rows, cols), bf16),
         grid=(1,),
-        in_specs=[const_spec(vector.shape), pl.BlockSpec(memory_space=pl.ANY)],
+        in_specs=[const_spec(value.shape) for value in (trio, up, mine, came)]
+        + [pl.BlockSpec(memory_space=pl.ANY)],
         out_specs=pl.BlockSpec((EXTRA, cols), lambda i: (rows // EXTRA - 1, 0)),
-        input_output_aliases={1: 0},
+        scratch_shapes=[pltpu.VMEM((EXTRA, cols), f32)],
+        input_output_aliases={4: 0},
         cost_estimate=BRIEF,
         compiler_params=pltpu.CompilerParams(vmem_limit_bytes=GRANT),
         name="ride",
-    )(vector, whole)
+    )(trio, up, mine, came, whole)
 
 
 def norm_rows(values, gain, shift):
@@ -1061,6 +1090,10 @@
         near = swap_z(mine, 1)
         return (mine, swap(mine, "y")), (near, swap(near, "y"))
 
+    def wait_near(total):
+        near, other = total[1]
+        return total[0], (line(lambda value: value, near), other)
+
     def put(pair, prior=None, extra=0):
         fill = partial(settle, flip=0 if prior is None else 1, extra=extra)
         return line(lambda mine, other, prior: fill(place, mine, other, prior=prior), *pair, prior)
@@ -1094,24 +1127,16 @@
     here, there = line(partial(sum_dots, nt), [trio_own, trio_other], [w_qkv, qkv_other])
     came = core_halves(there)
     up_sum = near_z(up_own, up_got, up_near)
-    down_sum = down_sum[0], (line(lambda value: value, down_sum[1][0]), down_sum[1][1])
+    down_sum = wait_near(down_sum)
     grad_in, _, sums_x = line(norm_back, tokens, here, came, gains[0], grad_h)
-    common = line(
-        lambda h, z, x: jnp.concatenate([h[2], z[0], x[0], h[0], x[1], h[1]]), sums_h, sum_dz, sums_x
-    )
+    common = line(common_rows, sums_h, sum_dz, sums_x)
     common_came = core(common)
 
     first_sum = near_z(first_own, first_got, first_near)
     up_sum = far_z(*up_sum)
-    vectors = line(
-        lambda mine, came, *parts: [
-            jnp.concatenate([trio[0, 0], trio[2, 0], up[0], mine + came]) for trio, up in parts
-        ],
-        common, common_came, (sum_trio_own, sum_up_own), (sum_trio_other, sum_up_other),
-    )
-    second_other = line(ride, attn_other[1], vectors[1])
+    second_other = line(ride, attn_other[1], sum_trio_other, sum_up_other, common, common_came)
     second_got = cross(second_other)
-    second_own = line(ride, attn_own[1], vectors[0])
+    second_own = line(ride, attn_own[1], sum_trio_own, sum_up_own, common, common_came)
     first_sum = far_z(*first_sum)
     grad_down = put(down_sum[0])
     grad_down = put(down_sum[1], grad_down)
@@ -1120,12 +1145,14 @@
     second_near = spread_y(second_own, second_got)
     first_sum = back_z(*first_sum)
     second_sum = near_z(second_own, second_got, second_near)
+    up_sum = wait_near(up_sum)
     grad_up = put(up_sum[0])
+    first_sum = wait_near(first_sum)
     second_sum = far_z(*second_sum)
     first = put(first_sum[0], extra=wide)
-    second_sum = back_z(*second_sum)
     grad_up = put(up_sum[1], grad_up)
     first = put(first_sum[1], first, extra=wide)
+    second_sum = back_z(*second_sum)
     second = put(second_sum[0])
     second = put(second_sum[1], second)
     grad_qkv = lax.dynamic_update_slice(first, second[:wide], (2 * wide, 0)).reshape(w_qkv.shape)

time: 345 us -> 337 us (0.977)
  local copies, waits for them, and re-layouts: 39.9 us -> 35.6 us
    ppermute x12, waiting for transfers between devices: 38.4 us -> 48 us  [swap_z(): return lax.ppermute(value, 'z', [(i, i ^ bits) for i in range(4)])]
    ppermute x37, waiting for transfers between devices: 40.5 us -> 33.9 us  [swap(): return lax.ppermute(value, axis, [(0, 1), (1, 0)])]
    unnamed x145 -> x124, local copies, waits for them, and re-layouts: 20.6 us -> 16.4 us
    pallas_call x8, Pallas kernels: 18.9 us -> 15.4 us  [settle(): pl.pallas_call(settle_body, out_shape=jax.ShapeDtypeStruct((4 + extra //...]
  transfers between devices with their start and end apart: 55 -> 55, of which waited for: 20 -> 22; matrix products, arithmetic and copies ran while one was open for 4% -> 4% of each run, Pallas kernels for 45% -> 45%
where the time goes in v1:
time: 337 us; the launch traced here: 336 us
  Pallas kernels  155 us (46%)
  waiting for transfers between devices  84.7 us (25%)
  starting transfers between devices  58.2 us (17%)
  local copies, waits for them, and re-layouts  35.6 us (11%)
    ppermute x12, waiting for transfers between devices, swap_z(): return lax.ppermute(value, 'z', [(i, i ^ bits) for i in range(4)])  48 us
    ppermute x37, waiting for transfers between devices, swap(): return lax.ppermute(value, axis, [(0, 1), (1, 0)])  33.9 us
    ppermute x37, starting transfers between devices, swap(): return lax.ppermute(value, axis, [(0, 1), (1, 0)])  32.2 us
    pallas_call x2, Pallas kernels, attn_bwd(): pl.pallas_call(body, out_shape=jax.ShapeDtypeStruct((3,) + query.shape, b...  26.3 us
    pallas_call x2, Pallas kernels, attn_fwd(): pl.pallas_call(attn_fwd_body, out_shape=(jax.ShapeDtypeStruct(query.shape...  23.6 us
    ppermute x12, starting transfers between devices, swap_z(): return lax.ppermute(value, 'z', [(i, i ^ bits) for i in range(4)])  20.5 us
    pallas_call x4, Pallas kernels, sum_dots(): pl.pallas_call(body, out_shape=(jax.ShapeDtypeStruct((m // 2, n), f32), j...  17.3 us
    unnamed x124, local copies, waits for them, and re-layouts  16.4 us
  transfers between devices with their start and end apart: 55, of which 22 were waited for; matrix products, arithmetic and copies ran while one was open for 4% of the time, Pallas kernels for 45%

profile of v1, /device:TPU:0, one launch (start us, length us, event | category | flops | bytes accessed | tf_op | source)
XLA Modules:
  0.0 336.2 jit_solution(11138305077003733698)
XLA Ops:
  27.4 11.8 %attn_fwd.2 = (bf16[1024,256]{1,0:T(8,128)(2,1)S(1)}, f32[4,1024]{1,0:T(4,128)S(1)}) custom-call(s32[5]{0:T(128)S(1)} %pad_add_fusion.info.refs_0_, bf16[1024,256]{1,0:T(8,128)(2,1)S(1)} %get-tuple-element.426.q_ref.refs_1_, bf16[1024,256]{1,0:T(8,128)(2,1)S(1)} %get-tuple-element.427.k_ref.refs_2_, bf16[1024,256]{1,0:T(8,128)(2,1)S(1)} %copy-done.36, ...), custom_call_target="tpu_custom_call" | custom-call | flops 1 | bytes 1 | tf_op jit(solution)/shard_map/attn_fwd/pallas_call | solution.py:156
  52.9 11.8 %attn_fwd.3 = (bf16[1024,256]{1,0:T(8,128)(2,1)S(1)}, f32[4,1024]{1,0:T(4,128)S(1)}) custom-call(s32[5]{0:T(128)S(1)} %pad_add_fusion.info.refs_0_, bf16[1024,256]{1,0:T(8,128)(2,1)S(1)} %get-tuple-element.394.q_ref.refs_1_, bf16[1024,256]{1,0:T(8,128)(2,1)S(1)} %get-tuple-element.395.k_ref.refs_2_, bf16[1024,256]{1,0:T(8,128)(2,1)S(1)} %get-tuple-element.396.v_ref.refs_3_, ...), custom_call_target="tpu_custom_call" | custom-call | flops 1 | bytes 1 | tf_op jit(solution)/shard_map/attn_fwd/pallas_call | solution.py:156
  76.6 6.2 %up_gelu.2 = (bf16[1024,1024]{1,0:T(8,128)(2,1)S(1)}, bf16[1024,1024]{1,0:T(8,128)(2,1)S(1)}) custom-call(bf16[1024,1024]{1,0:T(8,128)(2,1)S(1)} %constant_dynamic-update-slice_fusion.5.a_ref, bf16[1024,1024]{1,0:T(8,128)(2,1)S(1)} %bitcast.102, bf16[1,1024]{1,0:T(2,128)(2,1)S(1)} %reshape.197.b_ref), custom_call_target="tpu_custom_call" | custom-call | flops 1 | bytes 1 | tf_op jit(solution)/shard_map/up_gelu/pallas_call | solution.py:228
  82.8 4.1 %across_frames.4 = bf16[1024,1024]{1,0:T(8,128)(2,1)} custom-call(bf16[1024,1024]{1,0:T(8,128)(2,1)S(1)} %get-tuple-element.412.a_ref.refs_1_, bf16[1024,1024]{1,0:T(8,128)(2,1)S(1)} %constant_dynamic-update-slice_fusion.3.g_ref.z_ref), custom_call_target="tpu_custom_call" | custom-call | flops 1 | bytes 1 | tf_op jit(solution)/shard_map/across_frames/pallas_call | solution.py:489
  88.5 6.2 %up_gelu.3 = (bf16[1024,1024]{1,0:T(8,128)(2,1)S(1)}, bf16[1024,1024]{1,0:T(8,128)(2,1)S(1)}) custom-call(bf16[1024,1024]{1,0:T(8,128)(2,1)S(1)} %constant_dynamic-update-slice_fusion.5.a_ref, bf16[1024,1024]{1,0:T(8,128)(2,1)S(1)} %copy-done.10, bf16[1,1024]{1,0:T(2,128)(2,1)S(1)} %reshape.198.b_ref), custom_call_target="tpu_custom_call" | custom-call | flops 1 | bytes 1 | tf_op jit(solution)/shard_map/up_gelu/pallas_call | solution.py:228
  94.7 3.3 across_frames.5
  99.4 3.3 back_act.2
  103.2 3.3 back_act.3
  106.6 5.4 %sum_dots.5 = (f32[512,1024]{1,0:T(8,128)S(1)}, bf16[512,1024]{1,0:T(8,128)(2,1)S(1)}) custom-call(bf16[1024,1024]{1,0:T(8,128)(2,1)S(1)} %get-tuple-element.383.refs_0_.g_ref, bf16[1024,1024]{1,0:T(8,128)(2,1)S(1)} %get-tuple-element.374.refs_1_.g_ref, bf16[1024,1024]{1,0:T(8,128)(2,1)S(1)} %copy-done.10, bf16[1024,1024]{1,0:T(8,128)(2,1)S(1)} %bitcast.103), custom_call_target="tpu_custom_call" | custom-call | flops 1 | bytes 1 | tf_op jit(solution)/shard_map/sum_dots/pallas_call | solution.py:303
  113.7 4.1 %across_frames.6 = bf16[1024,1024]{1,0:T(8,128)(2,1)} custom-call(bf16[1024,1024]{1,0:T(8,128)(2,1)S(1)} %constant_dynamic-update-slice_fusion.5.a_ref, bf16[1024,1024]{1,0:T(8,128)(2,1)S(1)} %get-tuple-element.374.refs_1_.g_ref), custom_call_target="tpu_custom_call" | custom-call | flops 1 | bytes 1 | tf_op jit(solution)/shard_map/across_frames/pallas_call | solution.py:489
  122.8 4.0 %norm_back.2 = (f32[512,1024]{1,0:T(8,128)S(1)}, bf16[512,1024]{1,0:T(8,128)(2,1)S(1)}, f32[8,1024]{1,0:T(8,128)S(1)}) custom-call(f32[512,1024]{1,0:T(8,128)S(1)} %copy-done.23, f32[512,1024]{1,0:T(8,128)S(1)} %copy-done.45, bf16[256,1024]{1,0:T(8,128)(2,1)} %collective-permute-done.20.low_came_ref, ...), custom_call_target="tpu_custom_call" | custom-call | flops 1 | bytes 1 | tf_op jit(solution)/shard_map/norm_back/pallas_call | solution.py:400
  126.9 3.3 across_frames.7
  130.2 5.6 %collective-permute-done.19 = bf16[1024,1024]{1,0:T(8,128)(2,1)} collective-permute-done((bf16[1024,1024]{1,0:T(8,128)(2,1)}, bf16[1024,1024]{1,0:T(8,128)(2,1)}, u32[]{:S(2)}, u32[]{:S(2)}) %collective-permute-start.19) | collective-permute-done | bytes 2097184 | tf_op jit(solution)/shard_map/ppermute | solution.py:930
  144.0 13.2 %attn_bwd.2.d_ref.refs_1_ = bf16[3,1024,256]{2,1,0:T(8,128)(2,1)S(1)} custom-call(s32[5]{0:T(128)S(1)} %pad_add_fusion.info.refs_0_, bf16[1024,256]{1,0:T(8,128)(2,1)S(1)} %copy-done.39, bf16[1024,256]{1,0:T(8,128)(2,1)S(1)} %copy-done.41, bf16[1024,256]{1,0:T(8,128)(2,1)S(1)} %copy-done.43, s32[1,1024]{1,0:T(1,128)S(1)} %bitcast.123, ...), custom_call_target="tpu_custom_call" | custom-call | flops 1 | bytes 1 | tf_op jit(solution)/shard_map/attn_bwd/pallas_call | solution.py:184
  160.5 3.3 quarter_sums.4
  165.5 5.3 %sum_dots.6 = (f32[512,1024]{1,0:T(8,128)S(1)}, bf16[512,1024]{1,0:T(8,128)(2,1)S(1)}) custom-call(bf16[1024,1024]{1,0:T(8,128)(2,1)S(1)} %copy-done.19, bf16[1024,1024]{1,0:T(8,128)(2,1)S(1)} %copy-done.17, bf16[1024,1024]{1,0:T(8,128)(2,1)S(1)} %copy-done.9, bf16[1024,1024]{1,0:T(8,128)(2,1)S(1)} %bitcast.101), custom_call_target="tpu_custom_call" | custom-call | flops 1 | bytes 1 | tf_op jit(solution)/shard_map/sum_dots/pallas_call | solution.py:303
  173.8 3.4 %collective-permute-done.26.b_ref = bf16[256,1024]{1,0:T(8,128)(2,1)S(1)} collective-permute-done((bf16[256,1024]{1,0:T(8,128)(2,1)S(1)}, bf16[256,1024]{1,0:T(8,128)(2,1)S(1)}, u32[]{:S(2)}, u32[]{:S(2)}) %collective-permute-start.26) | collective-permute-done | bytes 524320 | tf_op jit(solution)/shard_map/ppermute | solution.py:974
  177.4 3.4 collective-permute-done.28
  187.5 13.1 %attn_bwd.3.d_ref.refs_0_ = bf16[3,1024,256]{2,1,0:T(8,128)(2,1)S(1)} custom-call(s32[5]{0:T(128)S(1)} %pad_add_fusion.info.refs_0_, bf16[1024,256]{1,0:T(8,128)(2,1)S(1)} %copy-done.32, bf16[1024,256]{1,0:T(8,128)(2,1)S(1)} %copy-done.34, bf16[1024,256]{1,0:T(8,128)(2,1)S(1)} %copy-done.37, s32[1,1024]{1,0:T(1,128)S(1)} %bitcast.124, ...), custom_call_target="tpu_custom_call" | custom-call | flops 1 | bytes 1 | tf_op jit(solution)/shard_map/attn_bwd/pallas_call | solution.py:184
  203.2 4.8 %collective-permute-done.27.b_ref = bf16[256,1024]{1,0:T(8,128)(2,1)S(1)} collective-permute-done((bf16[256,1024]{1,0:T(8,128)(2,1)S(1)}, bf16[256,1024]{1,0:T(8,128)(2,1)S(1)}, u32[]{:S(2)}, u32[]{:S(2)}) %collective-permute-start.27) | collective-permute-done | bytes 524320 | tf_op jit(solution)/shard_map/ppermute | solution.py:974
  212.1 4.6 %sum_dots.7 = (f32[512,1024]{1,0:T(8,128)S(1)}, bf16[512,1024]{1,0:T(8,128)(2,1)S(1)}) custom-call(bf16[3,1024,256]{2,1,0:T(8,128)(2,1)S(1)} %attn_bwd.3.d_ref.refs_0_, bf16[3,1024,256]{2,1,0:T(8,128)(2,1)S(1)} %attn_bwd.2.d_ref.refs_1_, bf16[3,1024,256]{2,1,0:T(8,128)(2,1)S(1)} %copy-done.26, bf16[3,1024,256]{2,1,0:T(8,128)(2,1)S(1)} %bitcast.105), custom_call_target="tpu_custom_call" | custom-call | flops 1 | bytes 1 | tf_op jit(solution)/shard_map/sum_dots/pallas_call | solution.py:303
  222.3 3.3 norm_back.3
  225.6 5.6 %collective-permute-done.34 = bf16[1024,256]{1,0:T(8,128)(2,1)S(1)} collective-permute-done((bf16[1024,256]{1,0:T(8,128)(2,1)S(1)}, bf16[1024,256]{1,0:T(8,128)(2,1)S(1)}, u32[]{:S(2)}, u32[]{:S(2)}) %collective-permute-start.34) | collective-permute-done | bytes 524320 | tf_op jit(solution)/shard_map/ppermute | solution.py:930
  238.3 3.4 %collective-permute-start.40 = (bf16[256,1024]{1,0:T(8,128)(2,1)S(1)}, bf16[256,1024]{1,0:T(8,128)(2,1)S(1)}, u32[]{:S(2)}, u32[]{:S(2)}) collective-permute-start(bf16[256,1024]{1,0:T(8,128)(2,1)S(1)} %add_low.10.a_ref), channel_id=1, source_target_pairs={{0,16},{8,24},{16,0},{24,8},{1,17},{9,25},{17,1},{25,9},{2,18},{10... | collective-permute-start | bytes 1572872 | tf_op jit(solution)/shard_map/ppermute | solution.py:974
  242.0 14.8 %collective-permute-done.35.b_ref = bf16[512,256]{1,0:T(8,128)(2,1)S(1)} collective-permute-done((bf16[512,256]{1,0:T(8,128)(2,1)S(1)}, bf16[512,256]{1,0:T(8,128)(2,1)S(1)}, u32[]{:S(2)}, u32[]{:S(2)}) %collective-permute-start.35) | collective-permute-done | bytes 262176 | tf_op jit(solution)/shard_map/ppermute | solution.py:974
  268.8 13.2 %collective-permute-done.38.b_ref = bf16[512,256]{1,0:T(8,128)(2,1)S(1)} collective-permute-done((bf16[512,256]{1,0:T(8,128)(2,1)S(1)}, bf16[512,256]{1,0:T(8,128)(2,1)S(1)}, u32[]{:S(2)}, u32[]{:S(2)}) %collective-permute-start.38) | collective-permute-done | bytes 262176 | tf_op jit(solution)/shard_map/ppermute | solution.py:974
  286.5 3.8 %collective-permute-done.44.other_ref = bf16[256,1024]{1,0:T(8,128)(2,1)S(1)} collective-permute-done((bf16[256,1024]{1,0:T(8,128)(2,1)S(1)}, bf16[256,1024]{1,0:T(8,128)(2,1)S(1)}, u32[]{:S(2)}, u32[]{:S(2)}) %collective-permute-start.44) | collective-permute-done | bytes 524320 | tf_op jit(solution)/shard_map/ppermute | solution.py:930
  292.7 3.1 collective-permute-done.43.mine_ref
  295.9 4.2 %collective-permute-start.51 = (bf16[544,256]{1,0:T(8,128)(2,1)S(1)}, bf16[544,256]{1,0:T(8,128)(2,1)S(1)}, u32[]{:S(2)}, u32[]{:S(2)}) collective-permute-start(bf16[544,256]{1,0:T(8,128)(2,1)S(1)} %add_low.14.a_ref), channel_id=1, source_target_pairs={{0,16},{8,24},{16,0},{24,8},{1,17},{9,25},{17,1},{25,9},{2,18},{10... | collective-permute-start | bytes 835592 | tf_op jit(solution)/shard_map/ppermute | solution.py:974
  302.2 6.8 %collective-permute-done.48.other_ref = bf16[512,256]{1,0:T(8,128)(2,1)S(1)} collective-permute-done((bf16[512,256]{1,0:T(8,128)(2,1)S(1)}, bf16[512,256]{1,0:T(8,128)(2,1)S(1)}, u32[]{:S(2)}, u32[]{:S(2)}) %collective-permute-start.48) | collective-permute-done | bytes 262176 | tf_op jit(solution)/shard_map/ppermute | solution.py:930
  316.8 5.6 %collective-permute-done.52.mine_ref = bf16[544,256]{1,0:T(8,128)(2,1)S(1)} collective-permute-done((bf16[544,256]{1,0:T(8,128)(2,1)S(1)}, bf16[544,256]{1,0:T(8,128)(2,1)S(1)}, u32[]{:S(2)}, u32[]{:S(2)}) %collective-permute-start.52) | collective-permute-done | bytes 278560 | tf_op jit(solution)/shard_map/ppermute | solution.py:974
  325.8 3.1 collective-permute-done.53.other_ref
  (306 shorter events, 144.0 us)
Async XLA Ops:
  10.3 15.6 %collective-permute-start.6 = (bf16[1536]{0:T(1024)(128)(2,1)S(1)}, bf16[1536]{0:T(1024)(128)(2,1)S(1)}, u32[]{:S(2)}, u32[]{:S(2)}) collective-permute-start(bf16[1536]{0:T(1024)(128)(2,1)S(1)} %pad_maximum_fusion), channel_id=1, source_target_pairs={{0,2},{2,0},{1,3},{3,1},{4,6},{6,4},{5,7},{7,5},{8,10},{10,8},{9,1... | collective-permute-start | bytes 9224 | tf_op jit(solution)/shard_map/ppermute | solution.py:930
  20.2 19.0 %collective-permute-start.3 = (bf16[768,256]{1,0:T(8,128)(2,1)}, bf16[768,256]{1,0:T(8,128)(2,1)}, u32[]{:S(2)}, u32[]{:S(2)}) collective-permute-start(bf16[768,256]{1,0:T(8,128)(2,1)} %collective-permute-done.2), channel_id=1, source_target_pairs={{0,4},{4,0},{1,5},{5,1},{2,6},{6,2},{3,7},{7,3},{8,12},{12,8},{9,1... | collective-permute-start | bytes 1179656 | tf_op jit(solution)/shard_map/ppermute | solution.py:930
  22.0 17.2 %collective-permute-start.4 = (bf16[768,256]{1,0:T(8,128)(2,1)}, bf16[768,256]{1,0:T(8,128)(2,1)}, u32[]{:S(2)}, u32[]{:S(2)}) collective-permute-start(bf16[768,256]{1,0:T(8,128)(2,1)} %collective-permute-done.2), channel_id=1, source_target_pairs={{0,8},{4,12},{8,0},{12,4},{16,24},{20,28},{24,16},{28,20},{1,9},{5... | collective-permute-start | bytes 1179656 | tf_op jit(solution)/shard_map/ppermute | solution.py:961
  23.6 17.5 %collective-permute-start.5 = (bf16[768,256]{1,0:T(8,128)(2,1)}, bf16[768,256]{1,0:T(8,128)(2,1)}, u32[]{:S(2)}, u32[]{:S(2)}) collective-permute-start(bf16[768,256]{1,0:T(8,128)(2,1)} %collective-permute-done.2), channel_id=1, source_target_pairs={{0,12},{4,8},{8,4},{12,0},{16,28},{20,24},{24,20},{28,16},{1,13},{... | collective-permute-start | bytes 1179656 | tf_op jit(solution)/shard_map/ppermute | solution.py:961
  24.1 19.2 %collective-permute-start.9 = (bf16[256,1024]{1,0:T(8,128)(2,1)}, bf16[256,1024]{1,0:T(8,128)(2,1)}, u32[]{:S(2)}, u32[]{:S(2)}) collective-permute-start(bf16[256,1024]{1,0:T(8,128)(2,1)} %dynamic-slice_bitcast_fusion.1), channel_id=1, source_target_pairs={{0,2},{2,0},{1,3},{3,1},{4,6},{6,4},{5,7},{7,5},{8,10},{10,8},{9,1... | collective-permute-start | bytes 1572872 | tf_op jit(solution)/shard_map/ppermute | solution.py:930
  26.0 38.7 %collective-permute-start.7 = (bf16[256,1024]{1,0:T(8,128)(2,1)}, bf16[256,1024]{1,0:T(8,128)(2,1)S(1)}, u32[]{:S(2)}, u32[]{:S(2)}) collective-permute-start(bf16[256,1024]{1,0:T(8,128)(2,1)} %w_ref.3), channel_id=1, source_target_pairs={{0,2},{2,0},{1,3},{3,1},{4,6},{6,4},{5,7},{7,5},{8,10},{10,8},{9,1... | collective-permute-start | bytes 1572872 | tf_op jit(solution)/shard_map/ppermute | solution.py:930
  43.2 24.3 %collective-permute-start.10 = (bf16[256,1024]{1,0:T(8,128)(2,1)}, bf16[256,1024]{1,0:T(8,128)(2,1)S(1)}, u32[]{:S(2)}, u32[]{:S(2)}) collective-permute-start(bf16[256,1024]{1,0:T(8,128)(2,1)} %collective-permute-done.9), channel_id=1, source_target_pairs={{0,4},{4,0},{1,5},{5,1},{2,6},{6,2},{3,7},{7,3},{8,12},{12,8},{9,1... | collective-permute-start | bytes 1572872 | tf_op jit(solution)/shard_map/ppermute | solution.py:930
  45.0 22.6 %collective-permute-start.11 = (bf16[256,1024]{1,0:T(8,128)(2,1)}, bf16[256,1024]{1,0:T(8,128)(2,1)S(1)}, u32[]{:S(2)}, u32[]{:S(2)}) collective-permute-start(bf16[256,1024]{1,0:T(8,128)(2,1)} %collective-permute-done.9), channel_id=1, source_target_pairs={{0,8},{4,12},{8,0},{12,4},{16,24},{20,28},{24,16},{28,20},{1,9},{5... | collective-permute-start | bytes 1572872 | tf_op jit(solution)/shard_map/ppermute | solution.py:961
  46.5 22.0 %collective-permute-start.12 = (bf16[256,1024]{1,0:T(8,128)(2,1)}, bf16[256,1024]{1,0:T(8,128)(2,1)S(1)}, u32[]{:S(2)}, u32[]{:S(2)}) collective-permute-start(bf16[256,1024]{1,0:T(8,128)(2,1)} %collective-permute-done.9), channel_id=1, source_target_pairs={{0,12},{4,8},{8,4},{12,0},{16,28},{20,24},{24,20},{28,16},{1,13},{... | collective-permute-start | bytes 1572872 | tf_op jit(solution)/shard_map/ppermute | solution.py:961
  46.8 20.2 %collective-permute-start.14 = (bf16[256,1024]{1,0:T(8,128)(2,1)S(1)}, bf16[256,1024]{1,0:T(8,128)(2,1)S(1)}, u32[]{:S(2)}, u32[]{:S(2)}) collective-permute-start(bf16[256,1024]{1,0:T(8,128)(2,1)S(1)} %copy-done.51), channel_id=1, source_target_pairs={{0,2},{2,0},{1,3},{3,1},{4,6},{6,4},{5,7},{7,5},{8,10},{10,8},{9,1... | collective-permute-start | bytes 1572872 | tf_op jit(solution)/shard_map/ppermute | solution.py:930
  72.7 30.0 %collective-permute-start.16 = (bf16[256,1024]{1,0:T(8,128)(2,1)S(1)}, bf16[256,1024]{1,0:T(8,128)(2,1)S(1)}, u32[]{:S(2)}, u32[]{:S(2)}) collective-permute-start(bf16[256,1024]{1,0:T(8,128)(2,1)S(1)} %collective-permute-done.14), channel_id=1, source_target_pairs={{0,4},{4,0},{1,5},{5,1},{2,6},{6,2},{3,7},{7,3},{8,12},{12,8},{9,1... | collective-permute-start | bytes 1572872 | tf_op jit(solution)/shard_map/ppermute | solution.py:930
  74.3 28.4 %collective-permute-start.17 = (bf16[256,1024]{1,0:T(8,128)(2,1)S(1)}, bf16[256,1024]{1,0:T(8,128)(2,1)S(1)}, u32[]{:S(2)}, u32[]{:S(2)}) collective-permute-start(bf16[256,1024]{1,0:T(8,128)(2,1)S(1)} %collective-permute-done.14), channel_id=1, source_target_pairs={{0,8},{4,12},{8,0},{12,4},{16,24},{20,28},{24,16},{28,20},{1,9},{5... | collective-permute-start | bytes 1572872 | tf_op jit(solution)/shard_map/ppermute | solution.py:961
  75.9 26.9 %collective-permute-start.18 = (bf16[256,1024]{1,0:T(8,128)(2,1)S(1)}, bf16[256,1024]{1,0:T(8,128)(2,1)S(1)}, u32[]{:S(2)}, u32[]{:S(2)}) collective-permute-start(bf16[256,1024]{1,0:T(8,128)(2,1)S(1)} %collective-permute-done.14), channel_id=1, source_target_pairs={{0,12},{4,8},{8,4},{12,0},{16,28},{20,24},{24,20},{28,16},{1,13},{... | collective-permute-start | bytes 1572872 | tf_op jit(solution)/shard_map/ppermute | solution.py:961
  87.0 48.8 %collective-permute-start.19 = (bf16[1024,1024]{1,0:T(8,128)(2,1)}, bf16[1024,1024]{1,0:T(8,128)(2,1)}, u32[]{:S(2)}, u32[]{:S(2)}) collective-permute-start(bf16[1024,1024]{1,0:T(8,128)(2,1)} %across_frames.4), channel_id=1, source_target_pairs={{0,2},{2,0},{1,3},{3,1},{4,6},{6,4},{5,7},{7,5},{8,10},{10,8},{9,1... | collective-permute-start | bytes 6291464 | tf_op jit(solution)/shard_map/ppermute | solution.py:930
  117.8 63.0 %collective-permute-start.28 = (bf16[1024,1024]{1,0:T(8,128)(2,1)}, bf16[1024,1024]{1,0:T(8,128)(2,1)}, u32[]{:S(2)}, u32[]{:S(2)}) collective-permute-start(bf16[1024,1024]{1,0:T(8,128)(2,1)} %across_frames.6), channel_id=1, source_target_pairs={{0,2},{2,0},{1,3},{3,1},{4,6},{6,4},{5,7},{7,5},{8,10},{10,8},{9,1... | collective-permute-start | bytes 6291464 | tf_op jit(solution)/shard_map/ppermute | solution.py:930
  137.9 22.5 %collective-permute-start.22 = (bf16[512,1024]{1,0:T(8,128)(2,1)S(1)}, bf16[512,1024]{1,0:T(8,128)(2,1)S(1)}, u32[]{:S(2)}, u32[]{:S(2)}) collective-permute-start(bf16[512,1024]{1,0:T(8,128)(2,1)S(1)} %side_sum.4), channel_id=1, source_target_pairs={{0,4},{4,0},{1,5},{5,1},{2,6},{6,2},{3,7},{7,3},{8,12},{12,8},{9,1... | collective-permute-start | bytes 3145736 | tf_op jit(solution)/shard_map/ppermute | solution.py:930
  170.8 38.1 %collective-permute-start.25 = (bf16[512,1024]{1,0:T(8,128)(2,1)S(1)}, bf16[512,1024]{1,0:T(8,128)(2,1)S(1)}, u32[]{:S(2)}, u32[]{:S(2)}) collective-permute-start(bf16[512,1024]{1,0:T(8,128)(2,1)S(1)} %get-tuple-element.416), channel_id=1, source_target_pairs={{0,1},{1,0},{2,3},{3,2},{4,5},{5,4},{6,7},{7,6},{8,9},{9,8},{10,11... | collective-permute-start | bytes 3145736 | tf_op jit(solution)/shard_map/ppermute | solution.py:930
  170.9 39.8 %collective-permute-start.29 = (bf16[2048,256]{1,0:T(8,128)(2,1)S(1)}, bf16[2048,256]{1,0:T(8,128)(2,1)S(1)}, u32[]{:S(2)}, u32[]{:S(2)}) collective-permute-start(bf16[2048,256]{1,0:T(8,128)(2,1)S(1)} %get-tuple-element.405), channel_id=1, source_target_pairs={{0,2},{2,0},{1,3},{3,1},{4,6},{6,4},{5,7},{7,5},{8,10},{10,8},{9,1... | collective-permute-start | bytes 3145736 | tf_op jit(solution)/shard_map/ppermute | solution.py:930
  183.3 34.5 %collective-permute-start.33 = (bf16[512,1024]{1,0:T(8,128)(2,1)S(1)}, bf16[512,1024]{1,0:T(8,128)(2,1)S(1)}, u32[]{:S(2)}, u32[]{:S(2)}) collective-permute-start(bf16[512,1024]{1,0:T(8,128)(2,1)S(1)} %side_sum.5), channel_id=1, source_target_pairs={{0,4},{4,0},{1,5},{5,1},{2,6},{6,2},{3,7},{7,3},{8,12},{12,8},{9,1... | collective-permute-start | bytes 3145736 | tf_op jit(solution)/shard_map/ppermute | solution.py:930
  184.9 23.1 %collective-permute-start.27 = (bf16[256,1024]{1,0:T(8,128)(2,1)S(1)}, bf16[256,1024]{1,0:T(8,128)(2,1)S(1)}, u32[]{:S(2)}, u32[]{:S(2)}) collective-permute-start(bf16[256,1024]{1,0:T(8,128)(2,1)S(1)} %add_low.8.a_ref), channel_id=1, source_target_pairs={{0,16},{8,24},{16,0},{24,8},{1,17},{9,25},{17,1},{25,9},{2,18},{10... | collective-permute-start | bytes 1572872 | tf_op jit(solution)/shard_map/ppermute | solution.py:974
  208.1 14.1 %collective-permute-start.32 = (bf16[256,1024]{1,0:T(8,128)(2,1)S(1)}, bf16[256,1024]{1,0:T(8,128)(2,1)S(1)}, u32[]{:S(2)}, u32[]{:S(2)}) collective-permute-start(bf16[256,1024]{1,0:T(8,128)(2,1)S(1)} %add_low.9.mine_ref), channel_id=1, source_target_pairs={{0,8},{8,0},{16,24},{24,16},{1,9},{9,1},{17,25},{25,17},{2,10},{10... | collective-permute-start | bytes 1572872 | tf_op jit(solution)/shard_map/ppermute | solution.py:974
  234.7 28.5 %collective-permute-start.39 = (bf16[2176,256]{1,0:T(8,128)(2,1)S(1)}, bf16[2176,256]{1,0:T(8,128)(2,1)S(1)}, u32[]{:S(2)}, u32[]{:S(2)}) collective-permute-start(bf16[2176,256]{1,0:T(8,128)(2,1)S(1)} %ride.2), channel_id=1, source_target_pairs={{0,2},{2,0},{1,3},{3,1},{4,6},{6,4},{5,7},{7,5},{8,10},{10,8},{9,1... | collective-permute-start | bytes 3342344 | tf_op jit(solution)/shard_map/ppermute | solution.py:930
  236.3 20.6 %collective-permute-start.42 = (bf16[256,1024]{1,0:T(8,128)(2,1)S(1)}, bf16[256,1024]{1,0:T(8,128)(2,1)S(1)}, u32[]{:S(2)}, u32[]{:S(2)}) collective-permute-start(bf16[256,1024]{1,0:T(8,128)(2,1)S(1)} %add_low.9.mine_ref), channel_id=1, source_target_pairs={{0,4},{4,0},{1,5},{5,1},{2,6},{6,2},{3,7},{7,3},{8,12},{12,8},{9,1... | collective-permute-start | bytes 1572872 | tf_op jit(solution)/shard_map/ppermute | solution.py:930
  237.8 22.2 %collective-permute-start.41 = (bf16[256,1024]{1,0:T(8,128)(2,1)S(1)}, bf16[256,1024]{1,0:T(8,128)(2,1)S(1)}, u32[]{:S(2)}, u32[]{:S(2)}) collective-permute-start(bf16[256,1024]{1,0:T(8,128)(2,1)S(1)} %collective-permute-done.32.mine_ref), channel_id=1, source_target_pairs={{0,4},{4,0},{1,5},{5,1},{2,6},{6,2},{3,7},{7,3},{8,12},{12,8},{9,1... | collective-permute-start | bytes 1572872 | tf_op jit(solution)/shard_map/ppermute | solution.py:930
  238.3 24.8 %collective-permute-start.40 = (bf16[256,1024]{1,0:T(8,128)(2,1)S(1)}, bf16[256,1024]{1,0:T(8,128)(2,1)S(1)}, u32[]{:S(2)}, u32[]{:S(2)}) collective-permute-start(bf16[256,1024]{1,0:T(8,128)(2,1)S(1)} %add_low.10.a_ref), channel_id=1, source_target_pairs={{0,16},{8,24},{16,0},{24,8},{1,17},{9,25},{17,1},{25,9},{2,18},{10... | collective-permute-start | bytes 1572872 | tf_op jit(solution)/shard_map/ppermute | solution.py:974
  241.7 15.1 %collective-permute-start.35 = (bf16[512,256]{1,0:T(8,128)(2,1)S(1)}, bf16[512,256]{1,0:T(8,128)(2,1)S(1)}, u32[]{:S(2)}, u32[]{:S(2)}) collective-permute-start(bf16[512,256]{1,0:T(8,128)(2,1)S(1)} %get-tuple-element.477), channel_id=1, source_target_pairs={{0,8},{8,0},{16,24},{24,16},{1,9},{9,1},{17,25},{25,17},{2,10},{10... | collective-permute-start | bytes 786440 | tf_op jit(solution)/shard_map/ppermute | solution.py:974
  263.5 18.6 %collective-permute-start.46 = (bf16[1088,256]{1,0:T(8,128)(2,1)S(1)}, bf16[1088,256]{1,0:T(8,128)(2,1)S(1)}, u32[]{:S(2)}, u32[]{:S(2)}) collective-permute-start(bf16[1088,256]{1,0:T(8,128)(2,1)S(1)} %side_sum.7), channel_id=1, source_target_pairs={{0,4},{4,0},{1,5},{5,1},{2,6},{6,2},{3,7},{7,3},{8,12},{12,8},{9,1... | collective-permute-start | bytes 1671176 | tf_op jit(solution)/shard_map/ppermute | solution.py:930
  265.1 20.9 %collective-permute-start.45 = (bf16[256,1024]{1,0:T(8,128)(2,1)S(1)}, bf16[256,1024]{1,0:T(8,128)(2,1)S(1)}, u32[]{:S(2)}, u32[]{:S(2)}) collective-permute-start(bf16[256,1024]{1,0:T(8,128)(2,1)S(1)} %add_low.12.mine_ref), channel_id=1, source_target_pairs={{0,8},{8,0},{16,24},{24,16},{1,9},{9,1},{17,25},{25,17},{2,10},{10... | collective-permute-start | bytes 1572872 | tf_op jit(solution)/shard_map/ppermute | solution.py:974
  266.3 15.8 %collective-permute-start.38 = (bf16[512,256]{1,0:T(8,128)(2,1)S(1)}, bf16[512,256]{1,0:T(8,128)(2,1)S(1)}, u32[]{:S(2)}, u32[]{:S(2)}) collective-permute-start(bf16[512,256]{1,0:T(8,128)(2,1)S(1)} %add_low.11.a_ref), channel_id=1, source_target_pairs={{0,16},{8,24},{16,0},{24,8},{1,17},{9,25},{17,1},{25,9},{2,18},{10... | collective-permute-start | bytes 786440 | tf_op jit(solution)/shard_map/ppermute | solution.py:974
  268.4 22.0 %collective-permute-start.44 = (bf16[256,1024]{1,0:T(8,128)(2,1)S(1)}, bf16[256,1024]{1,0:T(8,128)(2,1)S(1)}, u32[]{:S(2)}, u32[]{:S(2)}) collective-permute-start(bf16[256,1024]{1,0:T(8,128)(2,1)S(1)} %add_low.12.mine_ref), channel_id=1, source_target_pairs={{0,4},{4,0},{1,5},{5,1},{2,6},{6,2},{3,7},{7,3},{8,12},{12,8},{9,1... | collective-permute-start | bytes 1572872 | tf_op jit(solution)/shard_map/ppermute | solution.py:930
  286.0 25.1 %collective-permute-start.50 = (bf16[256,1024]{1,0:T(8,128)(2,1)S(1)}, bf16[256,1024]{1,0:T(8,128)(2,1)S(1)}, u32[]{:S(2)}, u32[]{:S(2)}) collective-permute-start(bf16[256,1024]{1,0:T(8,128)(2,1)S(1)} %collective-permute-done.45.mine_ref), channel_id=1, source_target_pairs={{0,4},{4,0},{1,5},{5,1},{2,6},{6,2},{3,7},{7,3},{8,12},{12,8},{9,1... | collective-permute-start | bytes 1572872 | tf_op jit(solution)/shard_map/ppermute | solution.py:930
  295.9 19.7 %collective-permute-start.51 = (bf16[544,256]{1,0:T(8,128)(2,1)S(1)}, bf16[544,256]{1,0:T(8,128)(2,1)S(1)}, u32[]{:S(2)}, u32[]{:S(2)}) collective-permute-start(bf16[544,256]{1,0:T(8,128)(2,1)S(1)} %add_low.14.a_ref), channel_id=1, source_target_pairs={{0,16},{8,24},{16,0},{24,8},{1,17},{9,25},{17,1},{25,9},{2,18},{10... | collective-permute-start | bytes 835592 | tf_op jit(solution)/shard_map/ppermute | solution.py:974
  (79 other events, 599.2 us)

commit v2 on v1

--- a/solution.py
+++ b/solution.py
@@ -672,38 +672,52 @@
     )(sums_h, sum_dz, sums_x)
 
 
-def ride_body(trio_ref, up_ref, mine_ref, came_ref, whole_ref, out_ref, lines):
+def lines_body(trio_ref, up_ref, mine_ref, came_ref, out_ref):
     cols = out_ref.shape[1]
-    lines[...] = jnp.zeros_like(lines)
-    lines[0:1] = trio_ref[0]
-    lines[1:2] = trio_ref[2]
+    out_ref[...] = jnp.zeros_like(out_ref)
+    out_ref[0:1] = trio_ref[0]
+    out_ref[1:2] = trio_ref[2]
     at = 2
     for part in range(up_ref.shape[1] // cols):
-        lines[at : at + 1] = up_ref[:, part * cols : (part + 1) * cols]
+        out_ref[at : at + 1] = up_ref[:, part * cols : (part + 1) * cols]
         at += 1
     both = mine_ref[...] + came_ref[...]
     for row in range(6):
         for part in range(both.shape[1] // cols):
-            lines[at : at + 1] = both[row : row + 1, part * cols : (part + 1) * cols]
+            out_ref[at : at + 1] = both[row : row + 1, part * cols : (part + 1) * cols]
             at += 1
+
+
+def lines_of(trio, up, mine, came):
+    return pl.pallas_call(
+        lines_body,
+        out_shape=jax.ShapeDtypeStruct((EXTRA // 4, trio.shape[2]), f32),
+        cost_estimate=BRIEF,
+        compiler_params=pltpu.CompilerParams(vmem_limit_bytes=GRANT),
+        name="lines_of",
+    )(trio, up, mine, came)
+
+
+def ride_body(mine_ref, came_ref, whole_ref, out_ref, lines):
+    lines[...] = jnp.zeros_like(lines)
+    lines[: mine_ref.shape[0]] = mine_ref[...] + came_ref[...]
     out_ref[...] = lines[...].astype(bf16)
 
 
-def ride(whole, trio, up, mine, came):
+def ride(whole, mine, came):
     rows, cols = whole.shape
     return pl.pallas_call(
         ride_body,
         out_shape=jax.ShapeDtypeStruct((rows, cols), bf16),
         grid=(1,),
-        in_specs=[const_spec(value.shape) for value in (trio, up, mine, came)]
-        + [pl.BlockSpec(memory_space=pl.ANY)],
+        in_specs=[const_spec(mine.shape), const_spec(came.shape), pl.BlockSpec(memory_space=pl.ANY)],
         out_specs=pl.BlockSpec((EXTRA, cols), lambda i: (rows // EXTRA - 1, 0)),
         scratch_shapes=[pltpu.VMEM((EXTRA, cols), f32)],
-        input_output_aliases={4: 0},
+        input_output_aliases={2: 0},
         cost_estimate=BRIEF,
         compiler_params=pltpu.CompilerParams(vmem_limit_bytes=GRANT),
         name="ride",
-    )(trio, up, mine, came, whole)
+    )(mine, came, whole)
 
 
 def norm_rows(values, gain, shift):
@@ -1110,6 +1124,7 @@
 
     trio_other, attn_other, sum_trio_other = back(other, out_other)
     first_got = cross(attn_other[0])
+    second_got = cross(attn_other[1])
     down_sum = near_z(down_own, down_got, down_near)
     y_here, y_there = line(partial(sum_dots, nn), [act_own, act_other], [w_down, down_other])
     y_came = core(y_there)
@@ -1134,15 +1149,15 @@
 
     first_sum = near_z(first_own, first_got, first_near)
     up_sum = far_z(*up_sum)
-    second_other = line(ride, attn_other[1], sum_trio_other, sum_up_other, common, common_came)
-    second_got = cross(second_other)
-    second_own = line(ride, attn_own[1], sum_trio_own, sum_up_own, common, common_came)
+    lines_came = cross(line(lines_of, sum_trio_other, sum_up_other, common, common_came))
+    lines_own = line(lines_of, sum_trio_own, sum_up_own, common, common_came)
+    second_own = line(ride, attn_own[1], lines_own, lines_came)
+    second_own, second_got = by_side(second_own), by_side(second_got)
+    second_near = spread_y(second_own, second_got)
     first_sum = far_z(*first_sum)
     grad_down = put(down_sum[0])
     grad_down = put(down_sum[1], grad_down)
     up_sum = back_z(*up_sum)
-    second_own, second_got = by_side(second_own), by_side(second_got)
-    second_near = spread_y(second_own, second_got)
     first_sum = back_z(*first_sum)
     second_sum = near_z(second_own, second_got, second_near)
     up_sum = wait_near(up_sum)

time: 337 us -> 332 us (0.985)
  Pallas kernels: 155 us -> 149 us
    ppermute x12, starting transfers between devices: 20.5 us -> 14.2 us  [swap_z(): return lax.ppermute(value, 'z', [(i, i ^ bits) for i in range(4)])]
    ppermute x37 -> x38, starting transfers between devices: 32.2 us -> 36.6 us  [swap(): return lax.ppermute(value, axis, [(0, 1), (1, 0)])]
    ppermute x37 -> x38, waiting for transfers between devices: 33.9 us -> 33.9 us  [swap(): return lax.ppermute(value, axis, [(0, 1), (1, 0)])]
  transfers between devices with their start and end apart: 55 -> 56, of which waited for: 22 -> 21; matrix products, arithmetic and copies ran while one was open for 4% -> 4% of each run, Pallas kernels for 45% -> 45%
where the time goes in v2:
time: 332 us; the launch traced here: 331 us
  Pallas kernels  149 us (45%)
  waiting for transfers between devices  86.5 us (26%)
  starting transfers between devices  56.3 us (17%)
  local copies, waits for them, and re-layouts  35.6 us (11%)
    ppermute x12, waiting for transfers between devices, swap_z(): return lax.ppermute(value, 'z', [(i, i ^ bits) for i in range(4)])  47.2 us
    ppermute x38, starting transfers between devices, swap(): return lax.ppermute(value, axis, [(0, 1), (1, 0)])  36.6 us
    ppermute x38, waiting for transfers between devices, swap(): return lax.ppermute(value, axis, [(0, 1), (1, 0)])  33.9 us
    pallas_call x2, Pallas kernels, attn_bwd(): pl.pallas_call(body, out_shape=jax.ShapeDtypeStruct((3,) + query.shape, b...  23.6 us
    pallas_call x2, Pallas kernels, attn_fwd(): pl.pallas_call(attn_fwd_body, out_shape=(jax.ShapeDtypeStruct(query.shape...  21 us
    pallas_call x4, Pallas kernels, sum_dots(): pl.pallas_call(body, out_shape=(jax.ShapeDtypeStruct((m // 2, n), f32), j...  17.3 us
    unnamed x124, local copies, waits for them, and re-layouts  16.4 us
    pallas_call x8, Pallas kernels, settle(): pl.pallas_call(settle_body, out_shape=jax.ShapeDtypeStruct((4 + extra //...  15.4 us
  transfers between devices with their start and end apart: 56, of which 21 were waited for; matrix products, arithmetic and copies ran while one was open for 4% of the time, Pallas kernels for 45%

profile of v2, /device:TPU:0, one launch (start us, length us, event | category | flops | bytes accessed | tf_op | source)
XLA Modules:
  0.0 330.7 jit_solution(9390872216362722671)
XLA Ops:
  27.4 10.5 %attn_fwd.2 = (bf16[1024,256]{1,0:T(8,128)(2,1)S(1)}, f32[4,1024]{1,0:T(4,128)S(1)}) custom-call(s32[5]{0:T(128)S(1)} %pad_add_fusion.info.refs_0_, bf16[1024,256]{1,0:T(8,128)(2,1)S(1)} %get-tuple-element.427.q_ref.refs_1_, bf16[1024,256]{1,0:T(8,128)(2,1)S(1)} %get-tuple-element.428.k_ref.refs_2_, bf16[1024,256]{1,0:T(8,128)(2,1)S(1)} %copy-done.36, ...), custom_call_target="tpu_custom_call" | custom-call | flops 1 | bytes 1 | tf_op jit(solution)/shard_map/attn_fwd/pallas_call | solution.py:156
  37.9 3.1 collective-permute-done.5
  52.9 10.5 %attn_fwd.3 = (bf16[1024,256]{1,0:T(8,128)(2,1)S(1)}, f32[4,1024]{1,0:T(4,128)S(1)}) custom-call(s32[5]{0:T(128)S(1)} %pad_add_fusion.info.refs_0_, bf16[1024,256]{1,0:T(8,128)(2,1)S(1)} %get-tuple-element.395.q_ref.refs_1_, bf16[1024,256]{1,0:T(8,128)(2,1)S(1)} %get-tuple-element.396.k_ref.refs_2_, bf16[1024,256]{1,0:T(8,128)(2,1)S(1)} %get-tuple-element.397.v_ref.refs_3_, ...), custom_call_target="tpu_custom_call" | custom-call | flops 1 | bytes 1 | tf_op jit(solution)/shard_map/attn_fwd/pallas_call | solution.py:156
  76.6 6.2 %up_gelu.2 = (bf16[1024,1024]{1,0:T(8,128)(2,1)S(1)}, bf16[1024,1024]{1,0:T(8,128)(2,1)S(1)}) custom-call(bf16[1024,1024]{1,0:T(8,128)(2,1)S(1)} %constant_dynamic-update-slice_fusion.5.a_ref, bf16[1024,1024]{1,0:T(8,128)(2,1)S(1)} %bitcast.102, bf16[1,1024]{1,0:T(2,128)(2,1)S(1)} %reshape.197.b_ref), custom_call_target="tpu_custom_call" | custom-call | flops 1 | bytes 1 | tf_op jit(solution)/shard_map/up_gelu/pallas_call | solution.py:228
  82.8 4.1 %across_frames.4 = bf16[1024,1024]{1,0:T(8,128)(2,1)} custom-call(bf16[1024,1024]{1,0:T(8,128)(2,1)S(1)} %get-tuple-element.413.a_ref.refs_1_, bf16[1024,1024]{1,0:T(8,128)(2,1)S(1)} %constant_dynamic-update-slice_fusion.3.g_ref.z_ref), custom_call_target="tpu_custom_call" | custom-call | flops 1 | bytes 1 | tf_op jit(solution)/shard_map/across_frames/pallas_call | solution.py:489
  88.5 6.2 %up_gelu.3 = (bf16[1024,1024]{1,0:T(8,128)(2,1)S(1)}, bf16[1024,1024]{1,0:T(8,128)(2,1)S(1)}) custom-call(bf16[1024,1024]{1,0:T(8,128)(2,1)S(1)} %constant_dynamic-update-slice_fusion.5.a_ref, bf16[1024,1024]{1,0:T(8,128)(2,1)S(1)} %copy-done.10, bf16[1,1024]{1,0:T(2,128)(2,1)S(1)} %reshape.198.b_ref), custom_call_target="tpu_custom_call" | custom-call | flops 1 | bytes 1 | tf_op jit(solution)/shard_map/up_gelu/pallas_call | solution.py:228
  94.7 3.3 %across_frames.5 = bf16[1024,1024]{1,0:T(8,128)(2,1)S(1)} custom-call(bf16[1024,1024]{1,0:T(8,128)(2,1)S(1)} %get-tuple-element.412.a_ref.refs_0_, bf16[1024,1024]{1,0:T(8,128)(2,1)S(1)} %constant_dynamic-update-slice_fusion.3.g_ref.z_ref), custom_call_target="tpu_custom_call" | custom-call | flops 1 | bytes 1 | tf_op jit(solution)/shard_map/across_frames/pallas_call | solution.py:489
  99.4 3.3 %back_act.2 = (bf16[1024,1024]{1,0:T(8,128)(2,1)S(1)}, f32[1,1024]{1,0:T(1,128)S(1)}) custom-call(bf16[1024,1024]{1,0:T(8,128)(2,1)S(1)} %constant_dynamic-update-slice_fusion.3.g_ref.z_ref, bf16[1024,1024]{1,0:T(8,128)(2,1)S(1)} %copy-done.8, bf16[1024,1024]{1,0:T(8,128)(2,1)S(1)} %get-tuple-element.357.s_ref), custom_call_target="tpu_custom_call" | custom-call | flops 1 | bytes 1 | tf_op jit(solution)/shard_map/back_act/pallas_call | solution.py:431
  103.2 3.3 %back_act.3 = (bf16[1024,1024]{1,0:T(8,128)(2,1)S(1)}, f32[1,1024]{1,0:T(1,128)S(1)}) custom-call(bf16[1024,1024]{1,0:T(8,128)(2,1)S(1)} %constant_dynamic-update-slice_fusion.3.g_ref.z_ref, bf16[1024,1024]{1,0:T(8,128)(2,1)S(1)} %bitcast.100, bf16[1024,1024]{1,0:T(8,128)(2,1)S(1)} %get-tuple-element.366.s_ref), custom_call_target="tpu_custom_call" | custom-call | flops 1 | bytes 1 | tf_op jit(solution)/shard_map/back_act/pallas_call | solution.py:431
  106.6 5.4 %sum_dots.5 = (f32[512,1024]{1,0:T(8,128)S(1)}, bf16[512,1024]{1,0:T(8,128)(2,1)S(1)}) custom-call(bf16[1024,1024]{1,0:T(8,128)(2,1)S(1)} %get-tuple-element.384.refs_0_.g_ref, bf16[1024,1024]{1,0:T(8,128)(2,1)S(1)} %get-tuple-element.375.refs_1_.g_ref, bf16[1024,1024]{1,0:T(8,128)(2,1)S(1)} %copy-done.10, bf16[1024,1024]{1,0:T(8,128)(2,1)S(1)} %bitcast.103), custom_call_target="tpu_custom_call" | custom-call | flops 1 | bytes 1 | tf_op jit(solution)/shard_map/sum_dots/pallas_call | solution.py:303
  113.7 4.1 %across_frames.6 = bf16[1024,1024]{1,0:T(8,128)(2,1)} custom-call(bf16[1024,1024]{1,0:T(8,128)(2,1)S(1)} %constant_dynamic-update-slice_fusion.5.a_ref, bf16[1024,1024]{1,0:T(8,128)(2,1)S(1)} %get-tuple-element.375.refs_1_.g_ref), custom_call_target="tpu_custom_call" | custom-call | flops 1 | bytes 1 | tf_op jit(solution)/shard_map/across_frames/pallas_call | solution.py:489
  122.9 4.0 %norm_back.2 = (f32[512,1024]{1,0:T(8,128)S(1)}, bf16[512,1024]{1,0:T(8,128)(2,1)S(1)}, f32[8,1024]{1,0:T(8,128)S(1)}) custom-call(f32[512,1024]{1,0:T(8,128)S(1)} %copy-done.23, f32[512,1024]{1,0:T(8,128)S(1)} %copy-done.45, bf16[256,1024]{1,0:T(8,128)(2,1)} %collective-permute-done.20.low_came_ref, ...), custom_call_target="tpu_custom_call" | custom-call | flops 1 | bytes 1 | tf_op jit(solution)/shard_map/norm_back/pallas_call | solution.py:400
  126.9 3.3 across_frames.7
  130.2 5.6 %collective-permute-done.19 = bf16[1024,1024]{1,0:T(8,128)(2,1)} collective-permute-done((bf16[1024,1024]{1,0:T(8,128)(2,1)}, bf16[1024,1024]{1,0:T(8,128)(2,1)}, u32[]{:S(2)}, u32[]{:S(2)}) %collective-permute-start.19) | collective-permute-done | bytes 2097184 | tf_op jit(solution)/shard_map/ppermute | solution.py:944
  144.0 11.7 %attn_bwd.2.d_ref.refs_1_ = bf16[3,1024,256]{2,1,0:T(8,128)(2,1)S(1)} custom-call(s32[5]{0:T(128)S(1)} %pad_add_fusion.info.refs_0_, bf16[1024,256]{1,0:T(8,128)(2,1)S(1)} %copy-done.39, bf16[1024,256]{1,0:T(8,128)(2,1)S(1)} %copy-done.41, bf16[1024,256]{1,0:T(8,128)(2,1)S(1)} %copy-done.43, s32[1,1024]{1,0:T(1,128)S(1)} %bitcast.123, ...), custom_call_target="tpu_custom_call" | custom-call | flops 1 | bytes 1 | tf_op jit(solution)/shard_map/attn_bwd/pallas_call | solution.py:184
  160.5 3.3 %quarter_sums.4 = (bf16[256,1024]{1,0:T(8,128)(2,1)S(1)}, bf16[256,1024]{1,0:T(8,128)(2,1)S(1)}) custom-call(s32[2]{0:T(128)S(1)} %pad_add_fusion.1.info, bf16[2,2,256,1024]{3,2,1,0:T(8,128)(2,1)S(1)} %bitcast.99, bf16[2,2,256,1024]{3,2,1,0:T(8,128)(2,1)} %bitcast.29.got_ref, bf16[2,256,1024]{2,1,0:T(8,128)(2,1)S(1)} %bitcast.118), custom_call_target="tpu_custom_call" | custom-call | flops 1 | bytes 1 | tf_op jit(solution)/shard_map/quarter_sums/pallas_call | solution.py:588
  165.5 5.3 %sum_dots.6 = (f32[512,1024]{1,0:T(8,128)S(1)}, bf16[512,1024]{1,0:T(8,128)(2,1)S(1)}) custom-call(bf16[1024,1024]{1,0:T(8,128)(2,1)S(1)} %copy-done.19, bf16[1024,1024]{1,0:T(8,128)(2,1)S(1)} %copy-done.17, bf16[1024,1024]{1,0:T(8,128)(2,1)S(1)} %copy-done.9, bf16[1024,1024]{1,0:T(8,128)(2,1)S(1)} %bitcast.101), custom_call_target="tpu_custom_call" | custom-call | flops 1 | bytes 1 | tf_op jit(solution)/shard_map/sum_dots/pallas_call | solution.py:303
  173.8 3.1 collective-permute-done.26.b_ref
  177.0 3.7 %collective-permute-done.28 = bf16[1024,1024]{1,0:T(8,128)(2,1)} collective-permute-done((bf16[1024,1024]{1,0:T(8,128)(2,1)}, bf16[1024,1024]{1,0:T(8,128)(2,1)}, u32[]{:S(2)}, u32[]{:S(2)}) %collective-permute-start.28) | collective-permute-done | bytes 2097184 | tf_op jit(solution)/shard_map/ppermute | solution.py:944
  187.2 12.0 %attn_bwd.3.d_ref.refs_0_ = bf16[3,1024,256]{2,1,0:T(8,128)(2,1)S(1)} custom-call(s32[5]{0:T(128)S(1)} %pad_add_fusion.info.refs_0_, bf16[1024,256]{1,0:T(8,128)(2,1)S(1)} %copy-done.32, bf16[1024,256]{1,0:T(8,128)(2,1)S(1)} %copy-done.34, bf16[1024,256]{1,0:T(8,128)(2,1)S(1)} %copy-done.37, s32[1,1024]{1,0:T(1,128)S(1)} %bitcast.124, ...), custom_call_target="tpu_custom_call" | custom-call | flops 1 | bytes 1 | tf_op jit(solution)/shard_map/attn_bwd/pallas_call | solution.py:184
  201.8 6.0 %collective-permute-done.27.b_ref = bf16[256,1024]{1,0:T(8,128)(2,1)S(1)} collective-permute-done((bf16[256,1024]{1,0:T(8,128)(2,1)S(1)}, bf16[256,1024]{1,0:T(8,128)(2,1)S(1)}, u32[]{:S(2)}, u32[]{:S(2)}) %collective-permute-start.27) | collective-permute-done | bytes 524320 | tf_op jit(solution)/shard_map/ppermute | solution.py:988
  213.4 4.6 %sum_dots.7 = (f32[512,1024]{1,0:T(8,128)S(1)}, bf16[512,1024]{1,0:T(8,128)(2,1)S(1)}) custom-call(bf16[3,1024,256]{2,1,0:T(8,128)(2,1)S(1)} %attn_bwd.3.d_ref.refs_0_, bf16[3,1024,256]{2,1,0:T(8,128)(2,1)S(1)} %attn_bwd.2.d_ref.refs_1_, bf16[3,1024,256]{2,1,0:T(8,128)(2,1)S(1)} %copy-done.26, bf16[3,1024,256]{2,1,0:T(8,128)(2,1)S(1)} %bitcast.105), custom_call_target="tpu_custom_call" | custom-call | flops 1 | bytes 1 | tf_op jit(solution)/shard_map/sum_dots/pallas_call | solution.py:303
  225.1 3.3 norm_back.3
  228.4 5.0 %collective-permute-done.34 = bf16[1024,256]{1,0:T(8,128)(2,1)S(1)} collective-permute-done((bf16[1024,256]{1,0:T(8,128)(2,1)S(1)}, bf16[1024,256]{1,0:T(8,128)(2,1)S(1)}, u32[]{:S(2)}, u32[]{:S(2)}) %collective-permute-start.34) | collective-permute-done | bytes 524320 | tf_op jit(solution)/shard_map/ppermute | solution.py:944
  236.0 3.4 %collective-permute-start.41 = (bf16[256,1024]{1,0:T(8,128)(2,1)S(1)}, bf16[256,1024]{1,0:T(8,128)(2,1)S(1)}, u32[]{:S(2)}, u32[]{:S(2)}) collective-permute-start(bf16[256,1024]{1,0:T(8,128)(2,1)S(1)} %add_low.10.a_ref), channel_id=1, source_target_pairs={{0,16},{8,24},{16,0},{24,8},{1,17},{9,25},{17,1},{25,9},{2,18},{10... | collective-permute-start | bytes 1572872 | tf_op jit(solution)/shard_map/ppermute | solution.py:988
  241.3 3.4 %collective-permute-done.38.came_ref = f32[32,256]{1,0:T(8,128)S(1)} collective-permute-done((f32[32,256]{1,0:T(8,128)S(1)}, f32[32,256]{1,0:T(8,128)S(1)}, u32[]{:S(2)}, u32[]{:S(2)}) %collective-permute-start.38) | collective-permute-done | bytes 32800 | tf_op jit(solution)/shard_map/ppermute | solution.py:944
  246.9 16.5 %collective-permute-done.35.b_ref = bf16[512,256]{1,0:T(8,128)(2,1)S(1)} collective-permute-done((bf16[512,256]{1,0:T(8,128)(2,1)S(1)}, bf16[512,256]{1,0:T(8,128)(2,1)S(1)}, u32[]{:S(2)}, u32[]{:S(2)}) %collective-permute-start.35) | collective-permute-done | bytes 262176 | tf_op jit(solution)/shard_map/ppermute | solution.py:988
  270.2 11.3 %collective-permute-done.40.b_ref = bf16[512,256]{1,0:T(8,128)(2,1)S(1)} collective-permute-done((bf16[512,256]{1,0:T(8,128)(2,1)S(1)}, bf16[512,256]{1,0:T(8,128)(2,1)S(1)}, u32[]{:S(2)}, u32[]{:S(2)}) %collective-permute-start.40) | collective-permute-done | bytes 262176 | tf_op jit(solution)/shard_map/ppermute | solution.py:988
  288.6 6.2 %collective-permute-done.44.mine_ref = bf16[512,256]{1,0:T(8,128)(2,1)S(1)} collective-permute-done((bf16[512,256]{1,0:T(8,128)(2,1)S(1)}, bf16[512,256]{1,0:T(8,128)(2,1)S(1)}, u32[]{:S(2)}, u32[]{:S(2)}) %collective-permute-start.44) | collective-permute-done | bytes 262176 | tf_op jit(solution)/shard_map/ppermute | solution.py:988
  297.1 6.4 %collective-permute-done.49.other_ref = bf16[512,256]{1,0:T(8,128)(2,1)S(1)} collective-permute-done((bf16[512,256]{1,0:T(8,128)(2,1)S(1)}, bf16[512,256]{1,0:T(8,128)(2,1)S(1)}, u32[]{:S(2)}, u32[]{:S(2)}) %collective-permute-start.49) | collective-permute-done | bytes 262176 | tf_op jit(solution)/shard_map/ppermute | solution.py:944
  313.7 3.1 collective-permute-done.53.mine_ref
  319.8 3.6 %collective-permute-done.54.other_ref = bf16[544,256]{1,0:T(8,128)(2,1)S(1)} collective-permute-done((bf16[544,256]{1,0:T(8,128)(2,1)S(1)}, bf16[544,256]{1,0:T(8,128)(2,1)S(1)}, u32[]{:S(2)}, u32[]{:S(2)}) %collective-permute-start.54) | collective-permute-done | bytes 278560 | tf_op jit(solution)/shard_map/ppermute | solution.py:944
  (309 shorter events, 144.1 us)
Async XLA Ops:
  10.3 15.6 %collective-permute-start.6 = (bf16[1536]{0:T(1024)(128)(2,1)S(1)}, bf16[1536]{0:T(1024)(128)(2,1)S(1)}, u32[]{:S(2)}, u32[]{:S(2)}) collective-permute-start(bf16[1536]{0:T(1024)(128)(2,1)S(1)} %pad_maximum_fusion), channel_id=1, source_target_pairs={{0,2},{2,0},{1,3},{3,1},{4,6},{6,4},{5,7},{7,5},{8,10},{10,8},{9,1... | collective-permute-start | bytes 9224 | tf_op jit(solution)/shard_map/ppermute | solution.py:944
  20.2 17.7 %collective-permute-start.3 = (bf16[768,256]{1,0:T(8,128)(2,1)}, bf16[768,256]{1,0:T(8,128)(2,1)}, u32[]{:S(2)}, u32[]{:S(2)}) collective-permute-start(bf16[768,256]{1,0:T(8,128)(2,1)} %collective-permute-done.2), channel_id=1, source_target_pairs={{0,4},{4,0},{1,5},{5,1},{2,6},{6,2},{3,7},{7,3},{8,12},{12,8},{9,1... | collective-permute-start | bytes 1179656 | tf_op jit(solution)/shard_map/ppermute | solution.py:944
  22.0 15.9 %collective-permute-start.4 = (bf16[768,256]{1,0:T(8,128)(2,1)}, bf16[768,256]{1,0:T(8,128)(2,1)}, u32[]{:S(2)}, u32[]{:S(2)}) collective-permute-start(bf16[768,256]{1,0:T(8,128)(2,1)} %collective-permute-done.2), channel_id=1, source_target_pairs={{0,8},{4,12},{8,0},{12,4},{16,24},{20,28},{24,16},{28,20},{1,9},{5... | collective-permute-start | bytes 1179656 | tf_op jit(solution)/shard_map/ppermute | solution.py:975
  23.6 17.5 %collective-permute-start.5 = (bf16[768,256]{1,0:T(8,128)(2,1)}, bf16[768,256]{1,0:T(8,128)(2,1)}, u32[]{:S(2)}, u32[]{:S(2)}) collective-permute-start(bf16[768,256]{1,0:T(8,128)(2,1)} %collective-permute-done.2), channel_id=1, source_target_pairs={{0,12},{4,8},{8,4},{12,0},{16,28},{20,24},{24,20},{28,16},{1,13},{... | collective-permute-start | bytes 1179656 | tf_op jit(solution)/shard_map/ppermute | solution.py:975
  24.1 19.2 %collective-permute-start.9 = (bf16[256,1024]{1,0:T(8,128)(2,1)}, bf16[256,1024]{1,0:T(8,128)(2,1)}, u32[]{:S(2)}, u32[]{:S(2)}) collective-permute-start(bf16[256,1024]{1,0:T(8,128)(2,1)} %dynamic-slice_bitcast_fusion.1), channel_id=1, source_target_pairs={{0,2},{2,0},{1,3},{3,1},{4,6},{6,4},{5,7},{7,5},{8,10},{10,8},{9,1... | collective-permute-start | bytes 1572872 | tf_op jit(solution)/shard_map/ppermute | solution.py:944
  26.0 37.5 %collective-permute-start.7 = (bf16[256,1024]{1,0:T(8,128)(2,1)}, bf16[256,1024]{1,0:T(8,128)(2,1)S(1)}, u32[]{:S(2)}, u32[]{:S(2)}) collective-permute-start(bf16[256,1024]{1,0:T(8,128)(2,1)} %w_ref.3), channel_id=1, source_target_pairs={{0,2},{2,0},{1,3},{3,1},{4,6},{6,4},{5,7},{7,5},{8,10},{10,8},{9,1... | collective-permute-start | bytes 1572872 | tf_op jit(solution)/shard_map/ppermute | solution.py:944
  43.2 23.0 %collective-permute-start.10 = (bf16[256,1024]{1,0:T(8,128)(2,1)}, bf16[256,1024]{1,0:T(8,128)(2,1)S(1)}, u32[]{:S(2)}, u32[]{:S(2)}) collective-permute-start(bf16[256,1024]{1,0:T(8,128)(2,1)} %collective-permute-done.9), channel_id=1, source_target_pairs={{0,4},{4,0},{1,5},{5,1},{2,6},{6,2},{3,7},{7,3},{8,12},{12,8},{9,1... | collective-permute-start | bytes 1572872 | tf_op jit(solution)/shard_map/ppermute | solution.py:944
  45.0 21.3 %collective-permute-start.11 = (bf16[256,1024]{1,0:T(8,128)(2,1)}, bf16[256,1024]{1,0:T(8,128)(2,1)S(1)}, u32[]{:S(2)}, u32[]{:S(2)}) collective-permute-start(bf16[256,1024]{1,0:T(8,128)(2,1)} %collective-permute-done.9), channel_id=1, source_target_pairs={{0,8},{4,12},{8,0},{12,4},{16,24},{20,28},{24,16},{28,20},{1,9},{5... | collective-permute-start | bytes 1572872 | tf_op jit(solution)/shard_map/ppermute | solution.py:975
  46.5 22.0 %collective-permute-start.12 = (bf16[256,1024]{1,0:T(8,128)(2,1)}, bf16[256,1024]{1,0:T(8,128)(2,1)S(1)}, u32[]{:S(2)}, u32[]{:S(2)}) collective-permute-start(bf16[256,1024]{1,0:T(8,128)(2,1)} %collective-permute-done.9), channel_id=1, source_target_pairs={{0,12},{4,8},{8,4},{12,0},{16,28},{20,24},{24,20},{28,16},{1,13},{... | collective-permute-start | bytes 1572872 | tf_op jit(solution)/shard_map/ppermute | solution.py:975
  46.8 18.9 %collective-permute-start.14 = (bf16[256,1024]{1,0:T(8,128)(2,1)S(1)}, bf16[256,1024]{1,0:T(8,128)(2,1)S(1)}, u32[]{:S(2)}, u32[]{:S(2)}) collective-permute-start(bf16[256,1024]{1,0:T(8,128)(2,1)S(1)} %copy-done.51), channel_id=1, source_target_pairs={{0,2},{2,0},{1,3},{3,1},{4,6},{6,4},{5,7},{7,5},{8,10},{10,8},{9,1... | collective-permute-start | bytes 1572872 | tf_op jit(solution)/shard_map/ppermute | solution.py:944
  72.7 30.0 %collective-permute-start.16 = (bf16[256,1024]{1,0:T(8,128)(2,1)S(1)}, bf16[256,1024]{1,0:T(8,128)(2,1)S(1)}, u32[]{:S(2)}, u32[]{:S(2)}) collective-permute-start(bf16[256,1024]{1,0:T(8,128)(2,1)S(1)} %collective-permute-done.14), channel_id=1, source_target_pairs={{0,4},{4,0},{1,5},{5,1},{2,6},{6,2},{3,7},{7,3},{8,12},{12,8},{9,1... | collective-permute-start | bytes 1572872 | tf_op jit(solution)/shard_map/ppermute | solution.py:944
  74.3 28.4 %collective-permute-start.17 = (bf16[256,1024]{1,0:T(8,128)(2,1)S(1)}, bf16[256,1024]{1,0:T(8,128)(2,1)S(1)}, u32[]{:S(2)}, u32[]{:S(2)}) collective-permute-start(bf16[256,1024]{1,0:T(8,128)(2,1)S(1)} %collective-permute-done.14), channel_id=1, source_target_pairs={{0,8},{4,12},{8,0},{12,4},{16,24},{20,28},{24,16},{28,20},{1,9},{5... | collective-permute-start | bytes 1572872 | tf_op jit(solution)/shard_map/ppermute | solution.py:975
  75.9 26.8 %collective-permute-start.18 = (bf16[256,1024]{1,0:T(8,128)(2,1)S(1)}, bf16[256,1024]{1,0:T(8,128)(2,1)S(1)}, u32[]{:S(2)}, u32[]{:S(2)}) collective-permute-start(bf16[256,1024]{1,0:T(8,128)(2,1)S(1)} %collective-permute-done.14), channel_id=1, source_target_pairs={{0,12},{4,8},{8,4},{12,0},{16,28},{20,24},{24,20},{28,16},{1,13},{... | collective-permute-start | bytes 1572872 | tf_op jit(solution)/shard_map/ppermute | solution.py:975
  87.0 48.8 %collective-permute-start.19 = (bf16[1024,1024]{1,0:T(8,128)(2,1)}, bf16[1024,1024]{1,0:T(8,128)(2,1)}, u32[]{:S(2)}, u32[]{:S(2)}) collective-permute-start(bf16[1024,1024]{1,0:T(8,128)(2,1)} %across_frames.4), channel_id=1, source_target_pairs={{0,2},{2,0},{1,3},{3,1},{4,6},{6,4},{5,7},{7,5},{8,10},{10,8},{9,1... | collective-permute-start | bytes 6291464 | tf_op jit(solution)/shard_map/ppermute | solution.py:944
  117.8 62.9 %collective-permute-start.28 = (bf16[1024,1024]{1,0:T(8,128)(2,1)}, bf16[1024,1024]{1,0:T(8,128)(2,1)}, u32[]{:S(2)}, u32[]{:S(2)}) collective-permute-start(bf16[1024,1024]{1,0:T(8,128)(2,1)} %across_frames.6), channel_id=1, source_target_pairs={{0,2},{2,0},{1,3},{3,1},{4,6},{6,4},{5,7},{7,5},{8,10},{10,8},{9,1... | collective-permute-start | bytes 6291464 | tf_op jit(solution)/shard_map/ppermute | solution.py:944
  137.9 22.5 %collective-permute-start.22 = (bf16[512,1024]{1,0:T(8,128)(2,1)S(1)}, bf16[512,1024]{1,0:T(8,128)(2,1)S(1)}, u32[]{:S(2)}, u32[]{:S(2)}) collective-permute-start(bf16[512,1024]{1,0:T(8,128)(2,1)S(1)} %side_sum.4), channel_id=1, source_target_pairs={{0,4},{4,0},{1,5},{5,1},{2,6},{6,2},{3,7},{7,3},{8,12},{12,8},{9,1... | collective-permute-start | bytes 3145736 | tf_op jit(solution)/shard_map/ppermute | solution.py:944
  170.8 39.4 %collective-permute-start.25 = (bf16[512,1024]{1,0:T(8,128)(2,1)S(1)}, bf16[512,1024]{1,0:T(8,128)(2,1)S(1)}, u32[]{:S(2)}, u32[]{:S(2)}) collective-permute-start(bf16[512,1024]{1,0:T(8,128)(2,1)S(1)} %get-tuple-element.417), channel_id=1, source_target_pairs={{0,1},{1,0},{2,3},{3,2},{4,5},{5,4},{6,7},{7,6},{8,9},{9,8},{10,11... | collective-permute-start | bytes 3145736 | tf_op jit(solution)/shard_map/ppermute | solution.py:944
  170.8 41.2 %collective-permute-start.29 = (bf16[2048,256]{1,0:T(8,128)(2,1)S(1)}, bf16[2048,256]{1,0:T(8,128)(2,1)S(1)}, u32[]{:S(2)}, u32[]{:S(2)}) collective-permute-start(bf16[2048,256]{1,0:T(8,128)(2,1)S(1)} %get-tuple-element.406), channel_id=1, source_target_pairs={{0,2},{2,0},{1,3},{3,1},{4,6},{6,4},{5,7},{7,5},{8,10},{10,8},{9,1... | collective-permute-start | bytes 3145736 | tf_op jit(solution)/shard_map/ppermute | solution.py:944
  183.0 35.6 %collective-permute-start.33 = (bf16[512,1024]{1,0:T(8,128)(2,1)S(1)}, bf16[512,1024]{1,0:T(8,128)(2,1)S(1)}, u32[]{:S(2)}, u32[]{:S(2)}) collective-permute-start(bf16[512,1024]{1,0:T(8,128)(2,1)S(1)} %side_sum.5), channel_id=1, source_target_pairs={{0,4},{4,0},{1,5},{5,1},{2,6},{6,2},{3,7},{7,3},{8,12},{12,8},{9,1... | collective-permute-start | bytes 3145736 | tf_op jit(solution)/shard_map/ppermute | solution.py:944
  184.6 23.1 %collective-permute-start.27 = (bf16[256,1024]{1,0:T(8,128)(2,1)S(1)}, bf16[256,1024]{1,0:T(8,128)(2,1)S(1)}, u32[]{:S(2)}, u32[]{:S(2)}) collective-permute-start(bf16[256,1024]{1,0:T(8,128)(2,1)S(1)} %add_low.8.a_ref), channel_id=1, source_target_pairs={{0,16},{8,24},{16,0},{24,8},{1,17},{9,25},{17,1},{25,9},{2,18},{10... | collective-permute-start | bytes 1572872 | tf_op jit(solution)/shard_map/ppermute | solution.py:988
  207.9 14.3 %collective-permute-start.32 = (bf16[256,1024]{1,0:T(8,128)(2,1)S(1)}, bf16[256,1024]{1,0:T(8,128)(2,1)S(1)}, u32[]{:S(2)}, u32[]{:S(2)}) collective-permute-start(bf16[256,1024]{1,0:T(8,128)(2,1)S(1)} %add_low.9.mine_ref), channel_id=1, source_target_pairs={{0,8},{8,0},{16,24},{24,16},{1,9},{9,1},{17,25},{25,17},{2,10},{10... | collective-permute-start | bytes 1572872 | tf_op jit(solution)/shard_map/ppermute | solution.py:988
  208.6 36.4 %collective-permute-start.39 = (bf16[2176,256]{1,0:T(8,128)(2,1)S(1)}, bf16[2176,256]{1,0:T(8,128)(2,1)S(1)}, u32[]{:S(2)}, u32[]{:S(2)}) collective-permute-start(bf16[2176,256]{1,0:T(8,128)(2,1)S(1)} %get-tuple-element.498), channel_id=1, source_target_pairs={{0,2},{2,0},{1,3},{3,1},{4,6},{6,4},{5,7},{7,5},{8,10},{10,8},{9,1... | collective-permute-start | bytes 3342344 | tf_op jit(solution)/shard_map/ppermute | solution.py:944
  218.6 14.8 %collective-permute-start.34 = (bf16[1024,256]{1,0:T(8,128)(2,1)S(1)}, bf16[1024,256]{1,0:T(8,128)(2,1)S(1)}, u32[]{:S(2)}, u32[]{:S(2)}) collective-permute-start(bf16[1024,256]{1,0:T(8,128)(2,1)S(1)} %side_sum.6), channel_id=1, source_target_pairs={{0,4},{4,0},{1,5},{5,1},{2,6},{6,2},{3,7},{7,3},{8,12},{12,8},{9,1... | collective-permute-start | bytes 1572872 | tf_op jit(solution)/shard_map/ppermute | solution.py:944
  223.6 39.8 %collective-permute-start.43 = (bf16[256,1024]{1,0:T(8,128)(2,1)S(1)}, bf16[256,1024]{1,0:T(8,128)(2,1)S(1)}, u32[]{:S(2)}, u32[]{:S(2)}) collective-permute-start(bf16[256,1024]{1,0:T(8,128)(2,1)S(1)} %add_low.9.mine_ref), channel_id=1, source_target_pairs={{0,4},{4,0},{1,5},{5,1},{2,6},{6,2},{3,7},{7,3},{8,12},{12,8},{9,1... | collective-permute-start | bytes 1572872 | tf_op jit(solution)/shard_map/ppermute | solution.py:944
  233.4 32.4 %collective-permute-start.42 = (bf16[256,1024]{1,0:T(8,128)(2,1)S(1)}, bf16[256,1024]{1,0:T(8,128)(2,1)S(1)}, u32[]{:S(2)}, u32[]{:S(2)}) collective-permute-start(bf16[256,1024]{1,0:T(8,128)(2,1)S(1)} %collective-permute-done.32.mine_ref), channel_id=1, source_target_pairs={{0,4},{4,0},{1,5},{5,1},{2,6},{6,2},{3,7},{7,3},{8,12},{12,8},{9,1... | collective-permute-start | bytes 1572872 | tf_op jit(solution)/shard_map/ppermute | solution.py:944
  236.0 32.2 %collective-permute-start.41 = (bf16[256,1024]{1,0:T(8,128)(2,1)S(1)}, bf16[256,1024]{1,0:T(8,128)(2,1)S(1)}, u32[]{:S(2)}, u32[]{:S(2)}) collective-permute-start(bf16[256,1024]{1,0:T(8,128)(2,1)S(1)} %add_low.10.a_ref), channel_id=1, source_target_pairs={{0,16},{8,24},{16,0},{24,8},{1,17},{9,25},{17,1},{25,9},{2,18},{10... | collective-permute-start | bytes 1572872 | tf_op jit(solution)/shard_map/ppermute | solution.py:988
  244.7 18.6 %collective-permute-start.35 = (bf16[512,256]{1,0:T(8,128)(2,1)S(1)}, bf16[512,256]{1,0:T(8,128)(2,1)S(1)}, u32[]{:S(2)}, u32[]{:S(2)}) collective-permute-start(bf16[512,256]{1,0:T(8,128)(2,1)S(1)} %get-tuple-element.478), channel_id=1, source_target_pairs={{0,8},{8,0},{16,24},{24,16},{1,9},{9,1},{17,25},{25,17},{2,10},{10... | collective-permute-start | bytes 786440 | tf_op jit(solution)/shard_map/ppermute | solution.py:988
  245.2 36.3 %collective-permute-start.47 = (bf16[1088,256]{1,0:T(8,128)(2,1)S(1)}, bf16[1088,256]{1,0:T(8,128)(2,1)S(1)}, u32[]{:S(2)}, u32[]{:S(2)}) collective-permute-start(bf16[1088,256]{1,0:T(8,128)(2,1)S(1)} %side_sum.7), channel_id=1, source_target_pairs={{0,4},{4,0},{1,5},{5,1},{2,6},{6,2},{3,7},{7,3},{8,12},{12,8},{9,1... | collective-permute-start | bytes 1671176 | tf_op jit(solution)/shard_map/ppermute | solution.py:944
  268.4 16.2 %collective-permute-start.46 = (bf16[256,1024]{1,0:T(8,128)(2,1)S(1)}, bf16[256,1024]{1,0:T(8,128)(2,1)S(1)}, u32[]{:S(2)}, u32[]{:S(2)}) collective-permute-start(bf16[256,1024]{1,0:T(8,128)(2,1)S(1)} %add_low.12.mine_ref), channel_id=1, source_target_pairs={{0,8},{8,0},{16,24},{24,16},{1,9},{9,1},{17,25},{25,17},{2,10},{10... | collective-permute-start | bytes 1572872 | tf_op jit(solution)/shard_map/ppermute | solution.py:988
  268.6 17.6 %collective-permute-start.45 = (bf16[256,1024]{1,0:T(8,128)(2,1)S(1)}, bf16[256,1024]{1,0:T(8,128)(2,1)S(1)}, u32[]{:S(2)}, u32[]{:S(2)}) collective-permute-start(bf16[256,1024]{1,0:T(8,128)(2,1)S(1)} %add_low.12.mine_ref), channel_id=1, source_target_pairs={{0,4},{4,0},{1,5},{5,1},{2,6},{6,2},{3,7},{7,3},{8,12},{12,8},{9,1... | collective-permute-start | bytes 1572872 | tf_op jit(solution)/shard_map/ppermute | solution.py:944
  284.6 21.0 %collective-permute-start.51 = (bf16[256,1024]{1,0:T(8,128)(2,1)S(1)}, bf16[256,1024]{1,0:T(8,128)(2,1)S(1)}, u32[]{:S(2)}, u32[]{:S(2)}) collective-permute-start(bf16[256,1024]{1,0:T(8,128)(2,1)S(1)} %collective-permute-done.46.mine_ref), channel_id=1, source_target_pairs={{0,4},{4,0},{1,5},{5,1},{2,6},{6,2},{3,7},{7,3},{8,12},{12,8},{9,1... | collective-permute-start | bytes 1572872 | tf_op jit(solution)/shard_map/ppermute | solution.py:944
  294.9 15.2 %collective-permute-start.52 = (bf16[544,256]{1,0:T(8,128)(2,1)S(1)}, bf16[544,256]{1,0:T(8,128)(2,1)S(1)}, u32[]{:S(2)}, u32[]{:S(2)}) collective-permute-start(bf16[544,256]{1,0:T(8,128)(2,1)S(1)} %add_low.14.a_ref), channel_id=1, source_target_pairs={{0,16},{8,24},{16,0},{24,8},{1,17},{9,25},{17,1},{25,9},{2,18},{10... | collective-permute-start | bytes 835592 | tf_op jit(solution)/shard_map/ppermute | solution.py:988
  (80 other events, 596.7 us)

commit v3 on v2

--- a/solution.py
+++ b/solution.py
@@ -1158,8 +1158,8 @@
     grad_down = put(down_sum[0])
     grad_down = put(down_sum[1], grad_down)
     up_sum = back_z(*up_sum)
+    second_sum = near_z(second_own, second_got, second_near)
     first_sum = back_z(*first_sum)
-    second_sum = near_z(second_own, second_got, second_near)
     up_sum = wait_near(up_sum)
     grad_up = put(up_sum[0])
     first_sum = wait_near(first_sum)

time: 332 us -> 332 us (level)
  transfers between devices with their start and end apart: 56 -> 56, of which waited for: 21 -> 22; matrix products, arithmetic and copies ran while one was open for 4% -> 4% of each run, Pallas kernels for 45% -> 44%
where the time goes in v3:
time: 332 us; the launch traced here: 331 us
  Pallas kernels  149 us (45%)
  waiting for transfers between devices  88.1 us (27%)
  starting transfers between devices  55 us (17%)
  local copies, waits for them, and re-layouts  35.6 us (11%)
    ppermute x12, waiting for transfers between devices, swap_z(): return lax.ppermute(value, 'z', [(i, i ^ bits) for i in range(4)])  46.9 us
    ppermute x38, starting transfers between devices, swap(): return lax.ppermute(value, axis, [(0, 1), (1, 0)])  36.5 us
    ppermute x38, waiting for transfers between devices, swap(): return lax.ppermute(value, axis, [(0, 1), (1, 0)])  35.8 us
    pallas_call x2, Pallas kernels, attn_bwd(): pl.pallas_call(body, out_shape=jax.ShapeDtypeStruct((3,) + query.shape, b...  23.6 us
    pallas_call x2, Pallas kernels, attn_fwd(): pl.pallas_call(attn_fwd_body, out_shape=(jax.ShapeDtypeStruct(query.shape...  21 us
    pallas_call x4, Pallas kernels, sum_dots(): pl.pallas_call(body, out_shape=(jax.ShapeDtypeStruct((m // 2, n), f32), j...  17.3 us
    unnamed x124, local copies, waits for them, and re-layouts  16.4 us
    pallas_call x8, Pallas kernels, settle(): pl.pallas_call(settle_body, out_shape=jax.ShapeDtypeStruct((4 + extra //...  15.4 us
  transfers between devices with their start and end apart: 56, of which 22 were waited for; matrix products, arithmetic and copies ran while one was open for 4% of the time, Pallas kernels for 44%

profile of v3, /device:TPU:0, one launch (start us, length us, event | category | flops | bytes accessed | tf_op | source)
XLA Modules:
  0.0 330.9 jit_solution(2548664737209825599)
XLA Ops:
  27.4 10.5 %attn_fwd.2 = (bf16[1024,256]{1,0:T(8,128)(2,1)S(1)}, f32[4,1024]{1,0:T(4,128)S(1)}) custom-call(s32[5]{0:T(128)S(1)} %pad_add_fusion.info.refs_0_, bf16[1024,256]{1,0:T(8,128)(2,1)S(1)} %get-tuple-element.427.q_ref.refs_1_, bf16[1024,256]{1,0:T(8,128)(2,1)S(1)} %get-tuple-element.428.k_ref.refs_2_, bf16[1024,256]{1,0:T(8,128)(2,1)S(1)} %copy-done.36, ...), custom_call_target="tpu_custom_call" | custom-call | flops 1 | bytes 1 | tf_op jit(solution)/shard_map/attn_fwd/pallas_call | solution.py:156
  37.9 3.1 collective-permute-done.5
  52.9 10.5 %attn_fwd.3 = (bf16[1024,256]{1,0:T(8,128)(2,1)S(1)}, f32[4,1024]{1,0:T(4,128)S(1)}) custom-call(s32[5]{0:T(128)S(1)} %pad_add_fusion.info.refs_0_, bf16[1024,256]{1,0:T(8,128)(2,1)S(1)} %get-tuple-element.395.q_ref.refs_1_, bf16[1024,256]{1,0:T(8,128)(2,1)S(1)} %get-tuple-element.396.k_ref.refs_2_, bf16[1024,256]{1,0:T(8,128)(2,1)S(1)} %get-tuple-element.397.v_ref.refs_3_, ...), custom_call_target="tpu_custom_call" | custom-call | flops 1 | bytes 1 | tf_op jit(solution)/shard_map/attn_fwd/pallas_call | solution.py:156
  76.6 6.2 %up_gelu.2 = (bf16[1024,1024]{1,0:T(8,128)(2,1)S(1)}, bf16[1024,1024]{1,0:T(8,128)(2,1)S(1)}) custom-call(bf16[1024,1024]{1,0:T(8,128)(2,1)S(1)} %constant_dynamic-update-slice_fusion.5.a_ref, bf16[1024,1024]{1,0:T(8,128)(2,1)S(1)} %bitcast.102, bf16[1,1024]{1,0:T(2,128)(2,1)S(1)} %reshape.197.b_ref), custom_call_target="tpu_custom_call" | custom-call | flops 1 | bytes 1 | tf_op jit(solution)/shard_map/up_gelu/pallas_call | solution.py:228
  82.8 4.1 %across_frames.4 = bf16[1024,1024]{1,0:T(8,128)(2,1)} custom-call(bf16[1024,1024]{1,0:T(8,128)(2,1)S(1)} %get-tuple-element.413.a_ref.refs_1_, bf16[1024,1024]{1,0:T(8,128)(2,1)S(1)} %constant_dynamic-update-slice_fusion.3.g_ref.z_ref), custom_call_target="tpu_custom_call" | custom-call | flops 1 | bytes 1 | tf_op jit(solution)/shard_map/across_frames/pallas_call | solution.py:489
  88.5 6.2 %up_gelu.3 = (bf16[1024,1024]{1,0:T(8,128)(2,1)S(1)}, bf16[1024,1024]{1,0:T(8,128)(2,1)S(1)}) custom-call(bf16[1024,1024]{1,0:T(8,128)(2,1)S(1)} %constant_dynamic-update-slice_fusion.5.a_ref, bf16[1024,1024]{1,0:T(8,128)(2,1)S(1)} %copy-done.10, bf16[1,1024]{1,0:T(2,128)(2,1)S(1)} %reshape.198.b_ref), custom_call_target="tpu_custom_call" | custom-call | flops 1 | bytes 1 | tf_op jit(solution)/shard_map/up_gelu/pallas_call | solution.py:228
  94.7 3.3 %across_frames.5 = bf16[1024,1024]{1,0:T(8,128)(2,1)S(1)} custom-call(bf16[1024,1024]{1,0:T(8,128)(2,1)S(1)} %get-tuple-element.412.a_ref.refs_0_, bf16[1024,1024]{1,0:T(8,128)(2,1)S(1)} %constant_dynamic-update-slice_fusion.3.g_ref.z_ref), custom_call_target="tpu_custom_call" | custom-call | flops 1 | bytes 1 | tf_op jit(solution)/shard_map/across_frames/pallas_call | solution.py:489
  99.4 3.3 %back_act.2 = (bf16[1024,1024]{1,0:T(8,128)(2,1)S(1)}, f32[1,1024]{1,0:T(1,128)S(1)}) custom-call(bf16[1024,1024]{1,0:T(8,128)(2,1)S(1)} %constant_dynamic-update-slice_fusion.3.g_ref.z_ref, bf16[1024,1024]{1,0:T(8,128)(2,1)S(1)} %copy-done.8, bf16[1024,1024]{1,0:T(8,128)(2,1)S(1)} %get-tuple-element.357.s_ref), custom_call_target="tpu_custom_call" | custom-call | flops 1 | bytes 1 | tf_op jit(solution)/shard_map/back_act/pallas_call | solution.py:431
  103.2 3.3 %back_act.3 = (bf16[1024,1024]{1,0:T(8,128)(2,1)S(1)}, f32[1,1024]{1,0:T(1,128)S(1)}) custom-call(bf16[1024,1024]{1,0:T(8,128)(2,1)S(1)} %constant_dynamic-update-slice_fusion.3.g_ref.z_ref, bf16[1024,1024]{1,0:T(8,128)(2,1)S(1)} %bitcast.100, bf16[1024,1024]{1,0:T(8,128)(2,1)S(1)} %get-tuple-element.366.s_ref), custom_call_target="tpu_custom_call" | custom-call | flops 1 | bytes 1 | tf_op jit(solution)/shard_map/back_act/pallas_call | solution.py:431
  106.6 5.4 %sum_dots.5 = (f32[512,1024]{1,0:T(8,128)S(1)}, bf16[512,1024]{1,0:T(8,128)(2,1)S(1)}) custom-call(bf16[1024,1024]{1,0:T(8,128)(2,1)S(1)} %get-tuple-element.384.refs_0_.g_ref, bf16[1024,1024]{1,0:T(8,128)(2,1)S(1)} %get-tuple-element.375.refs_1_.g_ref, bf16[1024,1024]{1,0:T(8,128)(2,1)S(1)} %copy-done.10, bf16[1024,1024]{1,0:T(8,128)(2,1)S(1)} %bitcast.103), custom_call_target="tpu_custom_call" | custom-call | flops 1 | bytes 1 | tf_op jit(solution)/shard_map/sum_dots/pallas_call | solution.py:303
  113.7 4.1 %across_frames.6 = bf16[1024,1024]{1,0:T(8,128)(2,1)} custom-call(bf16[1024,1024]{1,0:T(8,128)(2,1)S(1)} %constant_dynamic-update-slice_fusion.5.a_ref, bf16[1024,1024]{1,0:T(8,128)(2,1)S(1)} %get-tuple-element.375.refs_1_.g_ref), custom_call_target="tpu_custom_call" | custom-call | flops 1 | bytes 1 | tf_op jit(solution)/shard_map/across_frames/pallas_call | solution.py:489
  122.9 4.0 %norm_back.2 = (f32[512,1024]{1,0:T(8,128)S(1)}, bf16[512,1024]{1,0:T(8,128)(2,1)S(1)}, f32[8,1024]{1,0:T(8,128)S(1)}) custom-call(f32[512,1024]{1,0:T(8,128)S(1)} %copy-done.23, f32[512,1024]{1,0:T(8,128)S(1)} %copy-done.45, bf16[256,1024]{1,0:T(8,128)(2,1)} %collective-permute-done.20.low_came_ref, ...), custom_call_target="tpu_custom_call" | custom-call | flops 1 | bytes 1 | tf_op jit(solution)/shard_map/norm_back/pallas_call | solution.py:400
  126.9 3.3 across_frames.7
  130.2 5.6 %collective-permute-done.19 = bf16[1024,1024]{1,0:T(8,128)(2,1)} collective-permute-done((bf16[1024,1024]{1,0:T(8,128)(2,1)}, bf16[1024,1024]{1,0:T(8,128)(2,1)}, u32[]{:S(2)}, u32[]{:S(2)}) %collective-permute-start.19) | collective-permute-done | bytes 2097184 | tf_op jit(solution)/shard_map/ppermute | solution.py:944
  144.0 11.7 %attn_bwd.2.d_ref.refs_1_ = bf16[3,1024,256]{2,1,0:T(8,128)(2,1)S(1)} custom-call(s32[5]{0:T(128)S(1)} %pad_add_fusion.info.refs_0_, bf16[1024,256]{1,0:T(8,128)(2,1)S(1)} %copy-done.39, bf16[1024,256]{1,0:T(8,128)(2,1)S(1)} %copy-done.41, bf16[1024,256]{1,0:T(8,128)(2,1)S(1)} %copy-done.43, s32[1,1024]{1,0:T(1,128)S(1)} %bitcast.123, ...), custom_call_target="tpu_custom_call" | custom-call | flops 1 | bytes 1 | tf_op jit(solution)/shard_map/attn_bwd/pallas_call | solution.py:184
  160.5 3.3 %quarter_sums.4 = (bf16[256,1024]{1,0:T(8,128)(2,1)S(1)}, bf16[256,1024]{1,0:T(8,128)(2,1)S(1)}) custom-call(s32[2]{0:T(128)S(1)} %pad_add_fusion.1.info, bf16[2,2,256,1024]{3,2,1,0:T(8,128)(2,1)S(1)} %bitcast.99, bf16[2,2,256,1024]{3,2,1,0:T(8,128)(2,1)} %bitcast.29.got_ref, bf16[2,256,1024]{2,1,0:T(8,128)(2,1)S(1)} %bitcast.118), custom_call_target="tpu_custom_call" | custom-call | flops 1 | bytes 1 | tf_op jit(solution)/shard_map/quarter_sums/pallas_call | solution.py:588
  165.5 5.3 %sum_dots.6 = (f32[512,1024]{1,0:T(8,128)S(1)}, bf16[512,1024]{1,0:T(8,128)(2,1)S(1)}) custom-call(bf16[1024,1024]{1,0:T(8,128)(2,1)S(1)} %copy-done.19, bf16[1024,1024]{1,0:T(8,128)(2,1)S(1)} %copy-done.17, bf16[1024,1024]{1,0:T(8,128)(2,1)S(1)} %copy-done.9, bf16[1024,1024]{1,0:T(8,128)(2,1)S(1)} %bitcast.101), custom_call_target="tpu_custom_call" | custom-call | flops 1 | bytes 1 | tf_op jit(solution)/shard_map/sum_dots/pallas_call | solution.py:303
  175.8 4.9 %collective-permute-done.28 = bf16[1024,1024]{1,0:T(8,128)(2,1)} collective-permute-done((bf16[1024,1024]{1,0:T(8,128)(2,1)}, bf16[1024,1024]{1,0:T(8,128)(2,1)}, u32[]{:S(2)}, u32[]{:S(2)}) %collective-permute-start.28) | collective-permute-done | bytes 2097184 | tf_op jit(solution)/shard_map/ppermute | solution.py:944
  187.2 12.0 %attn_bwd.3.d_ref.refs_0_ = bf16[3,1024,256]{2,1,0:T(8,128)(2,1)S(1)} custom-call(s32[5]{0:T(128)S(1)} %pad_add_fusion.info.refs_0_, bf16[1024,256]{1,0:T(8,128)(2,1)S(1)} %copy-done.32, bf16[1024,256]{1,0:T(8,128)(2,1)S(1)} %copy-done.34, bf16[1024,256]{1,0:T(8,128)(2,1)S(1)} %copy-done.37, s32[1,1024]{1,0:T(1,128)S(1)} %bitcast.124, ...), custom_call_target="tpu_custom_call" | custom-call | flops 1 | bytes 1 | tf_op jit(solution)/shard_map/attn_bwd/pallas_call | solution.py:184
  201.8 6.0 %collective-permute-done.27.b_ref = bf16[256,1024]{1,0:T(8,128)(2,1)S(1)} collective-permute-done((bf16[256,1024]{1,0:T(8,128)(2,1)S(1)}, bf16[256,1024]{1,0:T(8,128)(2,1)S(1)}, u32[]{:S(2)}, u32[]{:S(2)}) %collective-permute-start.27) | collective-permute-done | bytes 524320 | tf_op jit(solution)/shard_map/ppermute | solution.py:988
  213.4 4.6 %sum_dots.7 = (f32[512,1024]{1,0:T(8,128)S(1)}, bf16[512,1024]{1,0:T(8,128)(2,1)S(1)}) custom-call(bf16[3,1024,256]{2,1,0:T(8,128)(2,1)S(1)} %attn_bwd.3.d_ref.refs_0_, bf16[3,1024,256]{2,1,0:T(8,128)(2,1)S(1)} %attn_bwd.2.d_ref.refs_1_, bf16[3,1024,256]{2,1,0:T(8,128)(2,1)S(1)} %copy-done.26, bf16[3,1024,256]{2,1,0:T(8,128)(2,1)S(1)} %bitcast.105), custom_call_target="tpu_custom_call" | custom-call | flops 1 | bytes 1 | tf_op jit(solution)/shard_map/sum_dots/pallas_call | solution.py:303
  219.1 3.0 quarter_sums.5
  225.1 3.3 norm_back.3
  228.4 5.0 %collective-permute-done.34 = bf16[1024,256]{1,0:T(8,128)(2,1)S(1)} collective-permute-done((bf16[1024,256]{1,0:T(8,128)(2,1)S(1)}, bf16[1024,256]{1,0:T(8,128)(2,1)S(1)}, u32[]{:S(2)}, u32[]{:S(2)}) %collective-permute-start.34) | collective-permute-done | bytes 524320 | tf_op jit(solution)/shard_map/ppermute | solution.py:944
  236.0 3.4 %collective-permute-start.42 = (bf16[256,1024]{1,0:T(8,128)(2,1)S(1)}, bf16[256,1024]{1,0:T(8,128)(2,1)S(1)}, u32[]{:S(2)}, u32[]{:S(2)}) collective-permute-start(bf16[256,1024]{1,0:T(8,128)(2,1)S(1)} %add_low.10.a_ref), channel_id=1, source_target_pairs={{0,16},{8,24},{16,0},{24,8},{1,17},{9,25},{17,1},{25,9},{2,18},{10... | collective-permute-start | bytes 1572872 | tf_op jit(solution)/shard_map/ppermute | solution.py:988
  241.3 3.4 %collective-permute-done.38.came_ref = f32[32,256]{1,0:T(8,128)S(1)} collective-permute-done((f32[32,256]{1,0:T(8,128)S(1)}, f32[32,256]{1,0:T(8,128)S(1)}, u32[]{:S(2)}, u32[]{:S(2)}) %collective-permute-start.38) | collective-permute-done | bytes 32800 | tf_op jit(solution)/shard_map/ppermute | solution.py:944
  246.9 16.5 %collective-permute-done.35.b_ref = bf16[512,256]{1,0:T(8,128)(2,1)S(1)} collective-permute-done((bf16[512,256]{1,0:T(8,128)(2,1)S(1)}, bf16[512,256]{1,0:T(8,128)(2,1)S(1)}, u32[]{:S(2)}, u32[]{:S(2)}) %collective-permute-start.35) | collective-permute-done | bytes 262176 | tf_op jit(solution)/shard_map/ppermute | solution.py:988
  273.0 11.3 %collective-permute-done.40.b_ref = bf16[512,256]{1,0:T(8,128)(2,1)S(1)} collective-permute-done((bf16[512,256]{1,0:T(8,128)(2,1)S(1)}, bf16[512,256]{1,0:T(8,128)(2,1)S(1)}, u32[]{:S(2)}, u32[]{:S(2)}) %collective-permute-start.40) | collective-permute-done | bytes 262176 | tf_op jit(solution)/shard_map/ppermute | solution.py:988
  290.0 4.6 %collective-permute-done.45.mine_ref = bf16[512,256]{1,0:T(8,128)(2,1)S(1)} collective-permute-done((bf16[512,256]{1,0:T(8,128)(2,1)S(1)}, bf16[512,256]{1,0:T(8,128)(2,1)S(1)}, u32[]{:S(2)}, u32[]{:S(2)}) %collective-permute-start.45) | collective-permute-done | bytes 262176 | tf_op jit(solution)/shard_map/ppermute | solution.py:988
  296.9 6.8 %collective-permute-done.49.other_ref = bf16[512,256]{1,0:T(8,128)(2,1)S(1)} collective-permute-done((bf16[512,256]{1,0:T(8,128)(2,1)S(1)}, bf16[512,256]{1,0:T(8,128)(2,1)S(1)}, u32[]{:S(2)}, u32[]{:S(2)}) %collective-permute-start.49) | collective-permute-done | bytes 262176 | tf_op jit(solution)/shard_map/ppermute | solution.py:944
  313.0 4.1 %collective-permute-done.53.mine_ref = bf16[544,256]{1,0:T(8,128)(2,1)S(1)} collective-permute-done((bf16[544,256]{1,0:T(8,128)(2,1)S(1)}, bf16[544,256]{1,0:T(8,128)(2,1)S(1)}, u32[]{:S(2)}, u32[]{:S(2)}) %collective-permute-start.53) | collective-permute-done | bytes 278560 | tf_op jit(solution)/shard_map/ppermute | solution.py:988
  321.0 2.6 collective-permute-done.54.other_ref
  (309 shorter events, 144.4 us)
Async XLA Ops:
  10.3 15.6 %collective-permute-start.6 = (bf16[1536]{0:T(1024)(128)(2,1)S(1)}, bf16[1536]{0:T(1024)(128)(2,1)S(1)}, u32[]{:S(2)}, u32[]{:S(2)}) collective-permute-start(bf16[1536]{0:T(1024)(128)(2,1)S(1)} %pad_maximum_fusion), channel_id=1, source_target_pairs={{0,2},{2,0},{1,3},{3,1},{4,6},{6,4},{5,7},{7,5},{8,10},{10,8},{9,1... | collective-permute-start | bytes 9224 | tf_op jit(solution)/shard_map/ppermute | solution.py:944
  20.2 17.7 %collective-permute-start.3 = (bf16[768,256]{1,0:T(8,128)(2,1)}, bf16[768,256]{1,0:T(8,128)(2,1)}, u32[]{:S(2)}, u32[]{:S(2)}) collective-permute-start(bf16[768,256]{1,0:T(8,128)(2,1)} %collective-permute-done.2), channel_id=1, source_target_pairs={{0,4},{4,0},{1,5},{5,1},{2,6},{6,2},{3,7},{7,3},{8,12},{12,8},{9,1... | collective-permute-start | bytes 1179656 | tf_op jit(solution)/shard_map/ppermute | solution.py:944
  22.0 15.9 %collective-permute-start.4 = (bf16[768,256]{1,0:T(8,128)(2,1)}, bf16[768,256]{1,0:T(8,128)(2,1)}, u32[]{:S(2)}, u32[]{:S(2)}) collective-permute-start(bf16[768,256]{1,0:T(8,128)(2,1)} %collective-permute-done.2), channel_id=1, source_target_pairs={{0,8},{4,12},{8,0},{12,4},{16,24},{20,28},{24,16},{28,20},{1,9},{5... | collective-permute-start | bytes 1179656 | tf_op jit(solution)/shard_map/ppermute | solution.py:975
  23.6 17.5 %collective-permute-start.5 = (bf16[768,256]{1,0:T(8,128)(2,1)}, bf16[768,256]{1,0:T(8,128)(2,1)}, u32[]{:S(2)}, u32[]{:S(2)}) collective-permute-start(bf16[768,256]{1,0:T(8,128)(2,1)} %collective-permute-done.2), channel_id=1, source_target_pairs={{0,12},{4,8},{8,4},{12,0},{16,28},{20,24},{24,20},{28,16},{1,13},{... | collective-permute-start | bytes 1179656 | tf_op jit(solution)/shard_map/ppermute | solution.py:975
  24.1 19.2 %collective-permute-start.9 = (bf16[256,1024]{1,0:T(8,128)(2,1)}, bf16[256,1024]{1,0:T(8,128)(2,1)}, u32[]{:S(2)}, u32[]{:S(2)}) collective-permute-start(bf16[256,1024]{1,0:T(8,128)(2,1)} %dynamic-slice_bitcast_fusion.1), channel_id=1, source_target_pairs={{0,2},{2,0},{1,3},{3,1},{4,6},{6,4},{5,7},{7,5},{8,10},{10,8},{9,1... | collective-permute-start | bytes 1572872 | tf_op jit(solution)/shard_map/ppermute | solution.py:944
  26.0 37.5 %collective-permute-start.7 = (bf16[256,1024]{1,0:T(8,128)(2,1)}, bf16[256,1024]{1,0:T(8,128)(2,1)S(1)}, u32[]{:S(2)}, u32[]{:S(2)}) collective-permute-start(bf16[256,1024]{1,0:T(8,128)(2,1)} %w_ref.3), channel_id=1, source_target_pairs={{0,2},{2,0},{1,3},{3,1},{4,6},{6,4},{5,7},{7,5},{8,10},{10,8},{9,1... | collective-permute-start | bytes 1572872 | tf_op jit(solution)/shard_map/ppermute | solution.py:944
  43.2 23.0 %collective-permute-start.10 = (bf16[256,1024]{1,0:T(8,128)(2,1)}, bf16[256,1024]{1,0:T(8,128)(2,1)S(1)}, u32[]{:S(2)}, u32[]{:S(2)}) collective-permute-start(bf16[256,1024]{1,0:T(8,128)(2,1)} %collective-permute-done.9), channel_id=1, source_target_pairs={{0,4},{4,0},{1,5},{5,1},{2,6},{6,2},{3,7},{7,3},{8,12},{12,8},{9,1... | collective-permute-start | bytes 1572872 | tf_op jit(solution)/shard_map/ppermute | solution.py:944
  45.0 21.3 %collective-permute-start.11 = (bf16[256,1024]{1,0:T(8,128)(2,1)}, bf16[256,1024]{1,0:T(8,128)(2,1)S(1)}, u32[]{:S(2)}, u32[]{:S(2)}) collective-permute-start(bf16[256,1024]{1,0:T(8,128)(2,1)} %collective-permute-done.9), channel_id=1, source_target_pairs={{0,8},{4,12},{8,0},{12,4},{16,24},{20,28},{24,16},{28,20},{1,9},{5... | collective-permute-start | bytes 1572872 | tf_op jit(solution)/shard_map/ppermute | solution.py:975
  46.5 22.0 %collective-permute-start.12 = (bf16[256,1024]{1,0:T(8,128)(2,1)}, bf16[256,1024]{1,0:T(8,128)(2,1)S(1)}, u32[]{:S(2)}, u32[]{:S(2)}) collective-permute-start(bf16[256,1024]{1,0:T(8,128)(2,1)} %collective-permute-done.9), channel_id=1, source_target_pairs={{0,12},{4,8},{8,4},{12,0},{16,28},{20,24},{24,20},{28,16},{1,13},{... | collective-permute-start | bytes 1572872 | tf_op jit(solution)/shard_map/ppermute | solution.py:975
  46.8 18.9 %collective-permute-start.14 = (bf16[256,1024]{1,0:T(8,128)(2,1)S(1)}, bf16[256,1024]{1,0:T(8,128)(2,1)S(1)}, u32[]{:S(2)}, u32[]{:S(2)}) collective-permute-start(bf16[256,1024]{1,0:T(8,128)(2,1)S(1)} %copy-done.51), channel_id=1, source_target_pairs={{0,2},{2,0},{1,3},{3,1},{4,6},{6,4},{5,7},{7,5},{8,10},{10,8},{9,1... | collective-permute-start | bytes 1572872 | tf_op jit(solution)/shard_map/ppermute | solution.py:944
  72.7 30.0 %collective-permute-start.16 = (bf16[256,1024]{1,0:T(8,128)(2,1)S(1)}, bf16[256,1024]{1,0:T(8,128)(2,1)S(1)}, u32[]{:S(2)}, u32[]{:S(2)}) collective-permute-start(bf16[256,1024]{1,0:T(8,128)(2,1)S(1)} %collective-permute-done.14), channel_id=1, source_target_pairs={{0,4},{4,0},{1,5},{5,1},{2,6},{6,2},{3,7},{7,3},{8,12},{12,8},{9,1... | collective-permute-start | bytes 1572872 | tf_op jit(solution)/shard_map/ppermute | solution.py:944
  74.3 28.4 %collective-permute-start.17 = (bf16[256,1024]{1,0:T(8,128)(2,1)S(1)}, bf16[256,1024]{1,0:T(8,128)(2,1)S(1)}, u32[]{:S(2)}, u32[]{:S(2)}) collective-permute-start(bf16[256,1024]{1,0:T(8,128)(2,1)S(1)} %collective-permute-done.14), channel_id=1, source_target_pairs={{0,8},{4,12},{8,0},{12,4},{16,24},{20,28},{24,16},{28,20},{1,9},{5... | collective-permute-start | bytes 1572872 | tf_op jit(solution)/shard_map/ppermute | solution.py:975
  75.9 26.8 %collective-permute-start.18 = (bf16[256,1024]{1,0:T(8,128)(2,1)S(1)}, bf16[256,1024]{1,0:T(8,128)(2,1)S(1)}, u32[]{:S(2)}, u32[]{:S(2)}) collective-permute-start(bf16[256,1024]{1,0:T(8,128)(2,1)S(1)} %collective-permute-done.14), channel_id=1, source_target_pairs={{0,12},{4,8},{8,4},{12,0},{16,28},{20,24},{24,20},{28,16},{1,13},{... | collective-permute-start | bytes 1572872 | tf_op jit(solution)/shard_map/ppermute | solution.py:975
  87.0 48.8 %collective-permute-start.19 = (bf16[1024,1024]{1,0:T(8,128)(2,1)}, bf16[1024,1024]{1,0:T(8,128)(2,1)}, u32[]{:S(2)}, u32[]{:S(2)}) collective-permute-start(bf16[1024,1024]{1,0:T(8,128)(2,1)} %across_frames.4), channel_id=1, source_target_pairs={{0,2},{2,0},{1,3},{3,1},{4,6},{6,4},{5,7},{7,5},{8,10},{10,8},{9,1... | collective-permute-start | bytes 6291464 | tf_op jit(solution)/shard_map/ppermute | solution.py:944
  117.8 62.9 %collective-permute-start.28 = (bf16[1024,1024]{1,0:T(8,128)(2,1)}, bf16[1024,1024]{1,0:T(8,128)(2,1)}, u32[]{:S(2)}, u32[]{:S(2)}) collective-permute-start(bf16[1024,1024]{1,0:T(8,128)(2,1)} %across_frames.6), channel_id=1, source_target_pairs={{0,2},{2,0},{1,3},{3,1},{4,6},{6,4},{5,7},{7,5},{8,10},{10,8},{9,1... | collective-permute-start | bytes 6291464 | tf_op jit(solution)/shard_map/ppermute | solution.py:944
  137.9 22.5 %collective-permute-start.22 = (bf16[512,1024]{1,0:T(8,128)(2,1)S(1)}, bf16[512,1024]{1,0:T(8,128)(2,1)S(1)}, u32[]{:S(2)}, u32[]{:S(2)}) collective-permute-start(bf16[512,1024]{1,0:T(8,128)(2,1)S(1)} %side_sum.4), channel_id=1, source_target_pairs={{0,4},{4,0},{1,5},{5,1},{2,6},{6,2},{3,7},{7,3},{8,12},{12,8},{9,1... | collective-permute-start | bytes 3145736 | tf_op jit(solution)/shard_map/ppermute | solution.py:944
  170.8 39.4 %collective-permute-start.25 = (bf16[512,1024]{1,0:T(8,128)(2,1)S(1)}, bf16[512,1024]{1,0:T(8,128)(2,1)S(1)}, u32[]{:S(2)}, u32[]{:S(2)}) collective-permute-start(bf16[512,1024]{1,0:T(8,128)(2,1)S(1)} %get-tuple-element.417), channel_id=1, source_target_pairs={{0,1},{1,0},{2,3},{3,2},{4,5},{5,4},{6,7},{7,6},{8,9},{9,8},{10,11... | collective-permute-start | bytes 3145736 | tf_op jit(solution)/shard_map/ppermute | solution.py:944
  170.8 41.2 %collective-permute-start.29 = (bf16[2048,256]{1,0:T(8,128)(2,1)S(1)}, bf16[2048,256]{1,0:T(8,128)(2,1)S(1)}, u32[]{:S(2)}, u32[]{:S(2)}) collective-permute-start(bf16[2048,256]{1,0:T(8,128)(2,1)S(1)} %get-tuple-element.406), channel_id=1, source_target_pairs={{0,2},{2,0},{1,3},{3,1},{4,6},{6,4},{5,7},{7,5},{8,10},{10,8},{9,1... | collective-permute-start | bytes 3145736 | tf_op jit(solution)/shard_map/ppermute | solution.py:944
  183.0 35.6 %collective-permute-start.33 = (bf16[512,1024]{1,0:T(8,128)(2,1)S(1)}, bf16[512,1024]{1,0:T(8,128)(2,1)S(1)}, u32[]{:S(2)}, u32[]{:S(2)}) collective-permute-start(bf16[512,1024]{1,0:T(8,128)(2,1)S(1)} %side_sum.5), channel_id=1, source_target_pairs={{0,4},{4,0},{1,5},{5,1},{2,6},{6,2},{3,7},{7,3},{8,12},{12,8},{9,1... | collective-permute-start | bytes 3145736 | tf_op jit(solution)/shard_map/ppermute | solution.py:944
  184.6 23.1 %collective-permute-start.27 = (bf16[256,1024]{1,0:T(8,128)(2,1)S(1)}, bf16[256,1024]{1,0:T(8,128)(2,1)S(1)}, u32[]{:S(2)}, u32[]{:S(2)}) collective-permute-start(bf16[256,1024]{1,0:T(8,128)(2,1)S(1)} %add_low.8.a_ref), channel_id=1, source_target_pairs={{0,16},{8,24},{16,0},{24,8},{1,17},{9,25},{17,1},{25,9},{2,18},{10... | collective-permute-start | bytes 1572872 | tf_op jit(solution)/shard_map/ppermute | solution.py:988
  208.6 36.4 %collective-permute-start.39 = (bf16[2176,256]{1,0:T(8,128)(2,1)S(1)}, bf16[2176,256]{1,0:T(8,128)(2,1)S(1)}, u32[]{:S(2)}, u32[]{:S(2)}) collective-permute-start(bf16[2176,256]{1,0:T(8,128)(2,1)S(1)} %get-tuple-element.498), channel_id=1, source_target_pairs={{0,2},{2,0},{1,3},{3,1},{4,6},{6,4},{5,7},{7,5},{8,10},{10,8},{9,1... | collective-permute-start | bytes 3342344 | tf_op jit(solution)/shard_map/ppermute | solution.py:944
  218.6 14.8 %collective-permute-start.34 = (bf16[1024,256]{1,0:T(8,128)(2,1)S(1)}, bf16[1024,256]{1,0:T(8,128)(2,1)S(1)}, u32[]{:S(2)}, u32[]{:S(2)}) collective-permute-start(bf16[1024,256]{1,0:T(8,128)(2,1)S(1)} %side_sum.6), channel_id=1, source_target_pairs={{0,4},{4,0},{1,5},{5,1},{2,6},{6,2},{3,7},{7,3},{8,12},{12,8},{9,1... | collective-permute-start | bytes 1572872 | tf_op jit(solution)/shard_map/ppermute | solution.py:944
  223.6 39.8 %collective-permute-start.44 = (bf16[256,1024]{1,0:T(8,128)(2,1)S(1)}, bf16[256,1024]{1,0:T(8,128)(2,1)S(1)}, u32[]{:S(2)}, u32[]{:S(2)}) collective-permute-start(bf16[256,1024]{1,0:T(8,128)(2,1)S(1)} %add_low.9.mine_ref), channel_id=1, source_target_pairs={{0,4},{4,0},{1,5},{5,1},{2,6},{6,2},{3,7},{7,3},{8,12},{12,8},{9,1... | collective-permute-start | bytes 1572872 | tf_op jit(solution)/shard_map/ppermute | solution.py:944
  233.4 32.4 %collective-permute-start.43 = (bf16[256,1024]{1,0:T(8,128)(2,1)S(1)}, bf16[256,1024]{1,0:T(8,128)(2,1)S(1)}, u32[]{:S(2)}, u32[]{:S(2)}) collective-permute-start(bf16[256,1024]{1,0:T(8,128)(2,1)S(1)} %collective-permute-done.32.mine_ref), channel_id=1, source_target_pairs={{0,4},{4,0},{1,5},{5,1},{2,6},{6,2},{3,7},{7,3},{8,12},{12,8},{9,1... | collective-permute-start | bytes 1572872 | tf_op jit(solution)/shard_map/ppermute | solution.py:944
  236.0 32.2 %collective-permute-start.42 = (bf16[256,1024]{1,0:T(8,128)(2,1)S(1)}, bf16[256,1024]{1,0:T(8,128)(2,1)S(1)}, u32[]{:S(2)}, u32[]{:S(2)}) collective-permute-start(bf16[256,1024]{1,0:T(8,128)(2,1)S(1)} %add_low.10.a_ref), channel_id=1, source_target_pairs={{0,16},{8,24},{16,0},{24,8},{1,17},{9,25},{17,1},{25,9},{2,18},{10... | collective-permute-start | bytes 1572872 | tf_op jit(solution)/shard_map/ppermute | solution.py:988
  244.7 18.6 %collective-permute-start.35 = (bf16[512,256]{1,0:T(8,128)(2,1)S(1)}, bf16[512,256]{1,0:T(8,128)(2,1)S(1)}, u32[]{:S(2)}, u32[]{:S(2)}) collective-permute-start(bf16[512,256]{1,0:T(8,128)(2,1)S(1)} %get-tuple-element.478), channel_id=1, source_target_pairs={{0,8},{8,0},{16,24},{24,16},{1,9},{9,1},{17,25},{25,17},{2,10},{10... | collective-permute-start | bytes 786440 | tf_op jit(solution)/shard_map/ppermute | solution.py:988
  245.2 24.8 %collective-permute-start.41 = (bf16[1088,256]{1,0:T(8,128)(2,1)S(1)}, bf16[1088,256]{1,0:T(8,128)(2,1)S(1)}, u32[]{:S(2)}, u32[]{:S(2)}) collective-permute-start(bf16[1088,256]{1,0:T(8,128)(2,1)S(1)} %side_sum.7), channel_id=1, source_target_pairs={{0,4},{4,0},{1,5},{5,1},{2,6},{6,2},{3,7},{7,3},{8,12},{12,8},{9,1... | collective-permute-start | bytes 1671176 | tf_op jit(solution)/shard_map/ppermute | solution.py:944
  268.4 17.7 %collective-permute-start.47 = (bf16[256,1024]{1,0:T(8,128)(2,1)S(1)}, bf16[256,1024]{1,0:T(8,128)(2,1)S(1)}, u32[]{:S(2)}, u32[]{:S(2)}) collective-permute-start(bf16[256,1024]{1,0:T(8,128)(2,1)S(1)} %add_low.12.mine_ref), channel_id=1, source_target_pairs={{0,8},{8,0},{16,24},{24,16},{1,9},{9,1},{17,25},{25,17},{2,10},{10... | collective-permute-start | bytes 1572872 | tf_op jit(solution)/shard_map/ppermute | solution.py:988
  268.5 19.1 %collective-permute-start.46 = (bf16[256,1024]{1,0:T(8,128)(2,1)S(1)}, bf16[256,1024]{1,0:T(8,128)(2,1)S(1)}, u32[]{:S(2)}, u32[]{:S(2)}) collective-permute-start(bf16[256,1024]{1,0:T(8,128)(2,1)S(1)} %add_low.12.mine_ref), channel_id=1, source_target_pairs={{0,4},{4,0},{1,5},{5,1},{2,6},{6,2},{3,7},{7,3},{8,12},{12,8},{9,1... | collective-permute-start | bytes 1572872 | tf_op jit(solution)/shard_map/ppermute | solution.py:944
  271.0 23.6 %collective-permute-start.50 = (bf16[544,256]{1,0:T(8,128)(2,1)S(1)}, bf16[544,256]{1,0:T(8,128)(2,1)S(1)}, u32[]{:S(2)}, u32[]{:S(2)}) collective-permute-start(bf16[544,256]{1,0:T(8,128)(2,1)S(1)} %get-tuple-element.515), channel_id=1, source_target_pairs={{0,8},{8,0},{16,24},{24,16},{1,9},{9,1},{17,25},{25,17},{2,10},{10... | collective-permute-start | bytes 835592 | tf_op jit(solution)/shard_map/ppermute | solution.py:988
  286.1 19.7 %collective-permute-start.51 = (bf16[256,1024]{1,0:T(8,128)(2,1)S(1)}, bf16[256,1024]{1,0:T(8,128)(2,1)S(1)}, u32[]{:S(2)}, u32[]{:S(2)}) collective-permute-start(bf16[256,1024]{1,0:T(8,128)(2,1)S(1)} %collective-permute-done.47.mine_ref), channel_id=1, source_target_pairs={{0,4},{4,0},{1,5},{5,1},{2,6},{6,2},{3,7},{7,3},{8,12},{12,8},{9,1... | collective-permute-start | bytes 1572872 | tf_op jit(solution)/shard_map/ppermute | solution.py:944
  294.7 15.7 %collective-permute-start.52 = (bf16[544,256]{1,0:T(8,128)(2,1)S(1)}, bf16[544,256]{1,0:T(8,128)(2,1)S(1)}, u32[]{:S(2)}, u32[]{:S(2)}) collective-permute-start(bf16[544,256]{1,0:T(8,128)(2,1)S(1)} %add_low.14.a_ref), channel_id=1, source_target_pairs={{0,16},{8,24},{16,0},{24,8},{1,17},{9,25},{17,1},{25,9},{2,18},{10... | collective-permute-start | bytes 835592 | tf_op jit(solution)/shard_map/ppermute | solution.py:988
  (80 other events, 599.9 us)
